TPU v7x, 32 devices: a whole 2x2x4 slice. The times are simulated.
32 devices in a mesh: stream: 2 (over x), mp: 4 (over z), dp: 4 (over y, core).
Axes of the slice: x: 2, y: 2, z: 4, core: 2. Of those that a mesh axis runs over, the one named last changes fastest.
Arguments:
- hidden: bfloat16 [2, 4096, 1024], P('stream', 'dp'), may hold values from -6 to 6
- cotangent: bfloat16 [2, 4096, 1024], P('stream', 'dp'), may hold values from -6 to 6
- segments: int32 [2, 32, 128], P(None, 'dp'), may hold values from 0 to 3, never falling along the last dimension, each value on 1 to 36 neighbouring positions
- cross_in: bfloat16 [2, 1024, 3, 1024], P('stream', None, None, 'mp'), may hold values from -0.1875 to 0.1875
- cross_bias: bfloat16 [2, 2, 1024], P('stream', None, 'mp'), may hold values from -3 to 3
- cross_out: bfloat16 [2, 1024, 1024], P('stream', 'mp'), may hold values from -1 to 1
- up_weight: bfloat16 [2, 1024, 3072], P('stream', None, 'mp'), may hold values from -0.1875 to 0.1875
- up_bias: bfloat16 [2, 3072], P('stream', 'mp'), may hold values from -3 to 3
- down_weight: bfloat16 [2, 3072, 1024], P('stream', 'mp'), may hold values from -0.1875 to 0.1875
- attend_in: bfloat16 [2, 1024, 3, 1024], P('stream', None, None, 'mp'), may hold values from -0.1875 to 0.1875
- attend_bias: bfloat16 [2, 2, 1024], P('stream', None, 'mp'), may hold values from -3 to 3
- attend_out: bfloat16 [2, 1024, 1024], P('stream', 'mp'), may hold values from -1 to 1
- out_bias: bfloat16 [2, 3, 1024], P('stream'), may hold values from -3 to 3
- norm_gains: bfloat16 [2, 3, 1024], P('stream'), may hold values from 0.5 to 1.5
- norm_shifts: bfloat16 [2, 3, 1024], P('stream'), may hold values from -3 to 3
Outputs:
- layer_out: bfloat16 [2, 4096, 1024], P('stream', 'dp')
- hidden_grad: bfloat16 [2, 4096, 1024], P('stream', 'dp')
- cross_in_grad: float32 [2, 1024, 3, 1024], P('stream', 'dp', None, 'mp')
- cross_bias_grad: float32 [2, 2, 1024], P('stream', None, ('mp', 'dp'))
- cross_out_grad: float32 [2, 1024, 1024], P('stream', 'mp', 'dp')
- up_weight_grad: float32 [2, 1024, 3072], P('stream', 'dp', 'mp')
- up_bias_grad: float32 [2, 3072], P('stream', ('mp', 'dp'))
- down_weight_grad: float32 [2, 3072, 1024], P('stream', 'mp', 'dp')
- attend_in_grad: float32 [2, 1024, 3, 1024], P('stream', 'dp', None, 'mp')
- attend_bias_grad: float32 [2, 2, 1024], P('stream', None, ('mp', 'dp'))
- attend_out_grad: float32 [2, 1024, 1024], P('stream', 'mp', 'dp')
- out_bias_grad: float32 [2, 3, 1024], P('stream', None, 'dp')
- norm_gains_grad: float32 [2, 3, 1024], P('stream', None, 'dp')
- norm_shifts_grad: float32 [2, 3, 1024], P('stream', None, 'dp')
Inputs may be any that keep to these rules, and one draw needn't show every extreme that they name: `segments`: along each row of 128 positions the numbers never fall; each of the 4 numbers covers 1 to 36 positions, one of them exactly 36; caption k of a text row belongs with image k of the same image row.
All inputs are finite; a program needn't handle non-finite values.
Results may differ from a plain program's by a relative error of at most 0.02.
Values may be sent and summed in bfloat16 or wider, within the bound.
A program may use at most 192 MiB of HBM per device.

v0:
```python
from functools import partial
import math

import jax
import jax.numpy as jnp
from jax import lax
from jax.sharding import PartitionSpec as P

TEXT_WIDTH = 768
TEXT_HEADS = 12
TEXT_FF = 3072
IMAGE_WIDTH = 1024
IMAGE_HEADS = 8
IMAGE_FF = 1024
CO_HEADS = 8


norm_eps = 1e-12
masked_score = -1000000000.0


def partner(block, axis, distance):
    count = lax.axis_size(axis)
    route = []
    for low in range(count):
        high = low | 1 << distance
        if high != low and high < count:
            route += [(low, high), (high, low)]
    return lax.ppermute(block, axis, route)


def widen(value_in, full_shape):
    return jnp.pad(
        value_in,
        [(0, want_size - have_size) for have_size, want_size in zip(value_in.shape, full_shape)],
    )


def normalize(value_in, gain_row, shift_row):
    row_mean = jnp.mean(value_in, axis=-1, keepdims=True)
    centred = value_in - row_mean
    spread = jnp.mean(centred * centred, axis=-1, keepdims=True)
    return centred * lax.rsqrt(spread + norm_eps) * gain_row + shift_row


def norm_backward(summed, gain_row, shift_row, incoming):
    normal_out, pullback = jax.vjp(normalize, summed, gain_row, shift_row)
    return pullback(incoming)


def head_split(matrix, row_count, head_count):
    return matrix.reshape(
        row_count, matrix.shape[0] // row_count, head_count, matrix.shape[1] // head_count
    )


def attend_forward(queries, key_rows, value_rows, allowed, head_count):
    row_count = allowed.shape[0]
    head_dim = queries.shape[1] // head_count
    query_heads = head_split(queries, row_count, head_count)
    key_heads = head_split(key_rows, row_count, head_count)
    value_heads = head_split(value_rows, row_count, head_count)
    scores = jnp.einsum(
        "rqhd,rkhd->rhqk", query_heads, key_heads, preferred_element_type=jnp.float32
    ) * (1.0 / math.sqrt(head_dim))
    scores = jnp.where(allowed[:, None], scores, masked_score)
    highest = jnp.max(scores, axis=-1, keepdims=True)
    exponent = jnp.exp(scores - highest)
    totals = jnp.sum(exponent, axis=-1, keepdims=True)
    weights = (exponent / totals).astype(jnp.bfloat16)
    context = jnp.einsum(
        "rhqk,rkhd->rqhd", weights, value_heads, preferred_element_type=jnp.float32
    )
    log_total = (highest + jnp.log(totals))[..., 0]
    return (context.reshape(queries.shape).astype(jnp.bfloat16), log_total)


def attend_backward(queries, key_rows, value_rows, allowed, head_count, log_total, grad_context):
    row_count = allowed.shape[0]
    head_dim = queries.shape[1] // head_count
    scale_factor = 1.0 / math.sqrt(head_dim)
    query_heads = head_split(queries, row_count, head_count)
    key_heads = head_split(key_rows, row_count, head_count)
    value_heads = head_split(value_rows, row_count, head_count)
    grad_heads = head_split(grad_context, row_count, head_count)
    scores = (
        jnp.einsum("rqhd,rkhd->rhqk", query_heads, key_heads, preferred_element_type=jnp.float32)
        * scale_factor
    )
    scores = jnp.where(allowed[:, None], scores, masked_score)
    weights = jnp.exp(scores - log_total[..., None])
    grad_weights = jnp.einsum(
        "rqhd,rkhd->rhqk", grad_heads, value_heads, preferred_element_type=jnp.float32
    )
    grad_value = jnp.einsum(
        "rhqk,rqhd->rkhd",
        weights.astype(jnp.bfloat16),
        grad_heads,
        preferred_element_type=jnp.float32,
    )
    grad_scores = (
        weights * (grad_weights - jnp.sum(grad_weights * weights, axis=-1, keepdims=True))
    ).astype(jnp.bfloat16)
    grad_query = (
        jnp.einsum("rhqk,rkhd->rqhd", grad_scores, key_heads, preferred_element_type=jnp.float32)
        * scale_factor
    )
    grad_key = (
        jnp.einsum("rhqk,rqhd->rkhd", grad_scores, query_heads, preferred_element_type=jnp.float32)
        * scale_factor
    )
    return (
        grad_query.reshape(queries.shape).astype(jnp.bfloat16),
        grad_key.reshape(queries.shape).astype(jnp.bfloat16),
        grad_value.reshape(queries.shape).astype(jnp.bfloat16),
    )


def cross_project(setting, hidden_in, cross_in, cross_bias):
    width_real = setting[0]
    inner_dev = cross_in.shape[3]
    weight = cross_in[0, :width_real].reshape(width_real, 3 * inner_dev)
    mixed_rows = jnp.dot(hidden_in[:, :width_real], weight, preferred_element_type=jnp.float32)
    queries = (mixed_rows[:, :inner_dev] + cross_bias[0, 0]).astype(jnp.bfloat16)
    key_rows = mixed_rows[:, inner_dev : 2 * inner_dev].astype(jnp.bfloat16)
    value_rows = (mixed_rows[:, 2 * inner_dev :] + cross_bias[0, 1]).astype(jnp.bfloat16)
    return (queries, key_rows, value_rows)


def cross_output(setting, context, cross_out):
    width_real = setting[0]
    partial_out = jnp.dot(context, cross_out[0, :, :width_real], preferred_element_type=jnp.float32)
    return widen(partial_out, (context.shape[0], cross_out.shape[2]))


def feed_inner(setting, first_low, up_weight, up_bias, down_weight):
    width_real, hidden_dev = (setting[0], setting[3])
    token_count, padded = first_low.shape
    inner_rows = (
        jnp.dot(
            first_low[:, :width_real],
            up_weight[0, :width_real, :hidden_dev],
            preferred_element_type=jnp.float32,
        )
        + up_bias[0, :hidden_dev]
    )
    activated = jax.nn.gelu(inner_rows, approximate=False).astype(jnp.bfloat16)
    partial_out = jnp.dot(
        activated, down_weight[0, :hidden_dev, :width_real], preferred_element_type=jnp.float32
    )
    return (
        widen(inner_rows, (token_count, up_weight.shape[2])),
        widen(partial_out, (token_count, padded)),
    )


def feed_forward(
    setting,
    hidden_in,
    cross_sum,
    out_bias,
    norm_gains,
    norm_shifts,
    up_weight,
    up_bias,
    down_weight,
):
    width_real = setting[0]
    token_count, padded = hidden_in.shape
    summed = (
        hidden_in[:, :width_real].astype(jnp.float32)
        + cross_sum[:, :width_real]
        + out_bias[0, 0, :width_real]
    )
    first_norm = normalize(summed, norm_gains[0, 0, :width_real], norm_shifts[0, 0, :width_real])
    first_pad = widen(first_norm, (token_count, padded))
    inner_pad, partial_out = feed_inner(
        setting, first_pad.astype(jnp.bfloat16), up_weight, up_bias, down_weight
    )
    return (first_pad, inner_pad, partial_out)


def self_attend(setting, head_max, second_low, attend_in, attend_bias, attend_out, allowed):
    width_real, head_count, head_dim = (setting[0], setting[1], setting[2])
    inner_real = head_count * head_dim
    inner_dev = attend_in.shape[3]
    token_count, padded = second_low.shape
    weight = attend_in[0, :width_real, :, :inner_real].reshape(width_real, 3 * inner_real)
    mixed_rows = jnp.dot(second_low[:, :width_real], weight, preferred_element_type=jnp.float32)
    queries = (mixed_rows[:, :inner_real] + attend_bias[0, 0, :inner_real]).astype(jnp.bfloat16)
    key_rows = mixed_rows[:, inner_real : 2 * inner_real].astype(jnp.bfloat16)
    value_rows = (mixed_rows[:, 2 * inner_real :] + attend_bias[0, 1, :inner_real]).astype(
        jnp.bfloat16
    )
    context, log_total = attend_forward(queries, key_rows, value_rows, allowed, head_count)
    partial_out = jnp.dot(
        context, attend_out[0, :inner_real, :width_real], preferred_element_type=jnp.float32
    )
    lane_shape = (token_count, inner_dev)
    return (
        widen(queries, lane_shape),
        widen(key_rows, lane_shape),
        widen(value_rows, lane_shape),
        widen(context, lane_shape),
        widen(log_total, (log_total.shape[0], head_max, log_total.shape[2])),
        widen(partial_out, (token_count, padded)),
    )


def self_forward(
    setting,
    head_max,
    first_pad,
    feed_sum,
    out_bias,
    norm_gains,
    norm_shifts,
    attend_in,
    attend_bias,
    attend_out,
    allowed,
):
    width_real = setting[0]
    token_count, padded = first_pad.shape
    summed = first_pad[:, :width_real] + feed_sum[:, :width_real] + out_bias[0, 1, :width_real]
    second_norm = normalize(summed, norm_gains[0, 1, :width_real], norm_shifts[0, 1, :width_real])
    second_pad = widen(second_norm, (token_count, padded))
    return (second_pad,) + self_attend(
        setting,
        head_max,
        second_pad.astype(jnp.bfloat16),
        attend_in,
        attend_bias,
        attend_out,
        allowed,
    )


def final_norm(setting, second_pad, attend_sum, out_bias, norm_gains, norm_shifts):
    width_real = setting[0]
    summed = second_pad[:, :width_real] + attend_sum[:, :width_real] + out_bias[0, 2, :width_real]
    final_rows = normalize(summed, norm_gains[0, 2, :width_real], norm_shifts[0, 2, :width_real])
    return widen(final_rows, second_pad.shape).astype(jnp.bfloat16)


def self_grad_matmul(
    setting,
    grad_branch,
    second_low,
    self_queries,
    self_keys,
    self_values,
    self_context,
    self_log,
    attend_in,
    attend_out,
    allowed,
):
    width_real, head_count, head_dim = (setting[0], setting[1], setting[2])
    inner_real = head_count * head_dim
    token_count, padded = grad_branch.shape
    grad_rows = grad_branch[:, :width_real]
    context = self_context[:, :inner_real]
    out_rows = attend_out[0, :inner_real, :width_real]
    grad_out_weight = jnp.dot(context.T, grad_rows, preferred_element_type=jnp.float32)
    grad_out_bias = jnp.sum(grad_rows.astype(jnp.float32), axis=0)
    grad_context = jnp.dot(grad_rows, out_rows.T, preferred_element_type=jnp.float32).astype(
        jnp.bfloat16
    )
    grad_query, grad_key, grad_value = attend_backward(
        self_queries[:, :inner_real],
        self_keys[:, :inner_real],
        self_values[:, :inner_real],
        allowed,
        head_count,
        self_log[:, :head_count],
        grad_context,
    )
    grad_mixed = jnp.concatenate([grad_query, grad_key, grad_value], axis=1)
    weight = attend_in[0, :width_real, :, :inner_real].reshape(width_real, 3 * inner_real)
    grad_in_weight = jnp.dot(
        second_low[:, :width_real].T, grad_mixed, preferred_element_type=jnp.float32
    ).reshape(width_real, 3, inner_real)
    grad_bias = jnp.stack(
        [
            jnp.sum(grad_query.astype(jnp.float32), axis=0),
            jnp.sum(grad_value.astype(jnp.float32), axis=0),
        ]
    )
    partial_in = jnp.dot(grad_mixed, weight.T, preferred_element_type=jnp.float32)
    return (
        widen(partial_in, (token_count, padded)),
        widen(grad_in_weight, attend_in.shape[1:]),
        widen(grad_bias, (2, attend_in.shape[3])),
        widen(grad_out_weight, attend_out.shape[1:]),
        widen(grad_out_bias[None], (1, padded)),
    )


def self_backward(
    setting,
    second_pad,
    attend_sum,
    out_bias,
    norm_gains,
    norm_shifts,
    grad_out,
    self_queries,
    self_keys,
    self_values,
    self_context,
    self_log,
    attend_in,
    attend_out,
    allowed,
):
    width_real = setting[0]
    token_count, padded = second_pad.shape
    summed = second_pad[:, :width_real] + attend_sum[:, :width_real] + out_bias[0, 2, :width_real]
    grad_sum, grad_gain, grad_shift = norm_backward(
        summed,
        norm_gains[0, 2, :width_real],
        norm_shifts[0, 2, :width_real],
        grad_out[:, :width_real],
    )
    grad_branch = widen(grad_sum.astype(jnp.bfloat16), (token_count, padded))
    parts = self_grad_matmul(
        setting,
        grad_branch,
        second_pad.astype(jnp.bfloat16),
        self_queries,
        self_keys,
        self_values,
        self_context,
        self_log,
        attend_in,
        attend_out,
        allowed,
    )
    row_shape = (1, padded)
    return (
        (widen(grad_sum, (token_count, padded)),)
        + parts
        + (widen(grad_gain[None], row_shape), widen(grad_shift[None], row_shape))
    )


def feed_grad_matmul(setting, grad_branch, first_low, inner_pad, up_weight, down_weight):
    width_real, hidden_dev = (setting[0], setting[3])
    token_count, padded = grad_branch.shape
    grad_rows = grad_branch[:, :width_real]
    activated, gelu_pull = jax.vjp(
        partial(jax.nn.gelu, approximate=False), inner_pad[:, :hidden_dev]
    )
    grad_down = jnp.dot(
        activated.astype(jnp.bfloat16).T, grad_rows, preferred_element_type=jnp.float32
    )
    grad_down_bias = jnp.sum(grad_rows.astype(jnp.float32), axis=0)
    grad_activated = jnp.dot(
        grad_rows, down_weight[0, :hidden_dev, :width_real].T, preferred_element_type=jnp.float32
    )
    grad_inner = gelu_pull(grad_activated)[0].astype(jnp.bfloat16)
    grad_up = jnp.dot(first_low[:, :width_real].T, grad_inner, preferred_element_type=jnp.float32)
    grad_up_bias = jnp.sum(grad_inner.astype(jnp.float32), axis=0)
    partial_in = jnp.dot(
        grad_inner, up_weight[0, :width_real, :hidden_dev].T, preferred_element_type=jnp.float32
    )
    return (
        widen(partial_in, (token_count, padded)),
        widen(grad_up, up_weight.shape[1:]),
        widen(grad_up_bias[None], (1, up_weight.shape[2])),
        widen(grad_down, down_weight.shape[1:]),
        widen(grad_down_bias[None], (1, padded)),
    )


def feed_backward(
    setting,
    first_pad,
    feed_sum,
    out_bias,
    norm_gains,
    norm_shifts,
    grad_second,
    inner_pad,
    up_weight,
    down_weight,
):
    width_real = setting[0]
    token_count, padded = first_pad.shape
    summed = first_pad[:, :width_real] + feed_sum[:, :width_real] + out_bias[0, 1, :width_real]
    grad_sum, grad_gain, grad_shift = norm_backward(
        summed,
        norm_gains[0, 1, :width_real],
        norm_shifts[0, 1, :width_real],
        grad_second[:, :width_real],
    )
    grad_branch = widen(grad_sum.astype(jnp.bfloat16), (token_count, padded))
    parts = feed_grad_matmul(
        setting, grad_branch, first_pad.astype(jnp.bfloat16), inner_pad, up_weight, down_weight
    )
    row_shape = (1, padded)
    return (
        (widen(grad_sum, (token_count, padded)),)
        + parts
        + (widen(grad_gain[None], row_shape), widen(grad_shift[None], row_shape))
    )


def cross_grad_matmul(setting, grad_branch, context, cross_out):
    width_real = setting[0]
    padded = grad_branch.shape[1]
    grad_rows = grad_branch[:, :width_real]
    grad_out_weight = jnp.dot(context.T, grad_rows, preferred_element_type=jnp.float32)
    grad_out_bias = jnp.sum(grad_rows.astype(jnp.float32), axis=0)
    grad_context = jnp.dot(
        grad_rows, cross_out[0, :, :width_real].T, preferred_element_type=jnp.float32
    ).astype(jnp.bfloat16)
    return (
        grad_context,
        widen(grad_out_weight, cross_out.shape[1:]),
        widen(grad_out_bias[None], (1, padded)),
    )


def cross_backward(
    setting, hidden_in, cross_sum, out_bias, norm_gains, norm_shifts, grad_first, context, cross_out
):
    width_real = setting[0]
    token_count, padded = hidden_in.shape
    summed = (
        hidden_in[:, :width_real].astype(jnp.float32)
        + cross_sum[:, :width_real]
        + out_bias[0, 0, :width_real]
    )
    grad_sum, grad_gain, grad_shift = norm_backward(
        summed,
        norm_gains[0, 0, :width_real],
        norm_shifts[0, 0, :width_real],
        grad_first[:, :width_real],
    )
    grad_branch = widen(grad_sum.astype(jnp.bfloat16), (token_count, padded))
    parts = cross_grad_matmul(setting, grad_branch, context, cross_out)
    row_shape = (1, padded)
    return (
        (widen(grad_sum, (token_count, padded)),)
        + parts
        + (widen(grad_gain[None], row_shape), widen(grad_shift[None], row_shape))
    )


def cross_input_backward(setting, hidden_in, grad_mixed, cross_in):
    width_real = setting[0]
    token_count, padded = hidden_in.shape
    weight = cross_in[0, :width_real].reshape(width_real, grad_mixed.shape[1])
    grad_weight = jnp.dot(
        hidden_in[:, :width_real].T, grad_mixed, preferred_element_type=jnp.float32
    ).reshape(width_real, 3, cross_in.shape[3])
    partial_in = jnp.dot(grad_mixed, weight.T, preferred_element_type=jnp.float32)
    return (widen(partial_in, (token_count, padded)), widen(grad_weight, cross_in.shape[1:]))


def shards(
    hidden,
    cotangent,
    segments,
    cross_in,
    cross_bias,
    cross_out,
    up_weight,
    up_bias,
    down_weight,
    attend_in,
    attend_bias,
    attend_out,
    out_bias,
    norm_gains,
    norm_shifts,
):
    groups = lax.axis_size("mp")
    stream_side = lax.axis_index("stream")
    is_image = stream_side == 1
    text_setting = (TEXT_WIDTH, TEXT_HEADS // groups, TEXT_WIDTH // TEXT_HEADS, TEXT_FF // groups)
    image_setting = (
        IMAGE_WIDTH,
        IMAGE_HEADS // groups,
        IMAGE_WIDTH // IMAGE_HEADS,
        IMAGE_FF // groups,
    )
    head_max = max(text_setting[1], image_setting[1])
    cross_heads = CO_HEADS // groups

    def by_stream(stream_piece, *operands):
        return lax.cond(
            is_image,
            partial(stream_piece, image_setting),
            partial(stream_piece, text_setting),
            *operands
        )

    def self_piece(setting, *remaining):
        return self_forward(setting, head_max, *remaining)

    def across_heads(partial_out):
        return lax.psum(partial_out, "mp")

    def across_inputs(partial_in):
        return lax.psum(partial_in.astype(jnp.bfloat16), "mp").astype(jnp.float32)

    cross_bias = cross_bias.astype(jnp.float32)
    up_bias = up_bias.astype(jnp.float32)
    attend_bias = attend_bias.astype(jnp.float32)
    out_bias = out_bias.astype(jnp.float32)
    norm_gains = norm_gains.astype(jnp.float32)
    norm_shifts = norm_shifts.astype(jnp.float32)
    hidden_in = hidden[0]
    grad_out = cotangent[0].astype(jnp.float32)
    own_rows = lax.dynamic_index_in_dim(segments, stream_side, 0, keepdims=False)
    other_rows = lax.dynamic_index_in_dim(segments, 1 - stream_side, 0, keepdims=False)
    cross_mask = own_rows[:, :, None] == other_rows[:, None, :]
    self_mask = own_rows[:, :, None] == own_rows[:, None, :]
    queries, key_rows, value_rows = by_stream(cross_project, hidden_in, cross_in, cross_bias)
    pair_keys, pair_values = partner((key_rows, value_rows), "stream", 0)
    context, log_total = attend_forward(queries, pair_keys, pair_values, cross_mask, cross_heads)
    cross_part = by_stream(cross_output, context, cross_out)
    cross_sum = across_heads(cross_part)
    first_pad, inner_pad, feed_part = by_stream(
        feed_forward,
        hidden_in,
        cross_sum,
        out_bias,
        norm_gains,
        norm_shifts,
        up_weight,
        up_bias,
        down_weight,
    )
    feed_sum = across_heads(feed_part)
    second_pad, self_queries, self_keys, self_values, self_context, self_log, attend_part = (
        by_stream(
            self_piece,
            first_pad,
            feed_sum,
            out_bias,
            norm_gains,
            norm_shifts,
            attend_in,
            attend_bias,
            attend_out,
            self_mask,
        )
    )
    attend_sum = across_heads(attend_part)
    layer_out = by_stream(final_norm, second_pad, attend_sum, out_bias, norm_gains, norm_shifts)
    (
        grad_third,
        self_part,
        attend_in_term,
        attend_bias_term,
        attend_out_term,
        third_bias_term,
        third_gain_term,
        third_shift_term,
    ) = by_stream(
        self_backward,
        second_pad,
        attend_sum,
        out_bias,
        norm_gains,
        norm_shifts,
        grad_out,
        self_queries,
        self_keys,
        self_values,
        self_context,
        self_log,
        attend_in,
        attend_out,
        self_mask,
    )
    grad_second = grad_third + across_inputs(self_part)
    (
        grad_middle,
        feed_input,
        up_term,
        up_bias_term,
        down_term,
        second_bias_term,
        second_gain_term,
        second_shift_term,
    ) = by_stream(
        feed_backward,
        first_pad,
        feed_sum,
        out_bias,
        norm_gains,
        norm_shifts,
        grad_second,
        inner_pad,
        up_weight,
        down_weight,
    )
    grad_first = grad_middle + across_inputs(feed_input)
    grad_entry, grad_context, cross_out_term, first_bias_term, first_gain_term, first_shift_term = (
        by_stream(
            cross_backward,
            hidden_in,
            cross_sum,
            out_bias,
            norm_gains,
            norm_shifts,
            grad_first,
            context,
            cross_out,
        )
    )
    grad_query, grad_pair_key, grad_pair_value = attend_backward(
        queries, pair_keys, pair_values, cross_mask, cross_heads, log_total, grad_context
    )
    grad_key, grad_value = partner((grad_pair_key, grad_pair_value), "stream", 0)
    grad_mixed = jnp.concatenate([grad_query, grad_key, grad_value], axis=1)
    input_part, cross_in_part = by_stream(cross_input_backward, hidden_in, grad_mixed, cross_in)
    bias_part = jnp.stack(
        [
            jnp.sum(grad_query.astype(jnp.float32), axis=0),
            jnp.sum(grad_value.astype(jnp.float32), axis=0),
        ]
    )
    input_part, cross_in_term, cross_bias_term = (input_part, cross_in_part, bias_part)
    hidden_grad = (grad_entry + across_inputs(input_part)).astype(jnp.bfloat16)
    every_total = (
        lax.psum_scatter(
            attend_in_term.astype(jnp.bfloat16), "dp", scatter_dimension=0, tiled=True
        ).astype(jnp.float32),
        lax.psum_scatter(
            attend_bias_term.astype(jnp.bfloat16), "dp", scatter_dimension=1, tiled=True
        ).astype(jnp.float32),
        lax.psum_scatter(
            attend_out_term.astype(jnp.bfloat16), "dp", scatter_dimension=1, tiled=True
        ).astype(jnp.float32),
        lax.psum_scatter(
            third_bias_term.astype(jnp.bfloat16), "dp", scatter_dimension=1, tiled=True
        ).astype(jnp.float32),
        lax.psum_scatter(
            third_gain_term.astype(jnp.bfloat16), "dp", scatter_dimension=1, tiled=True
        ).astype(jnp.float32),
        lax.psum_scatter(
            third_shift_term.astype(jnp.bfloat16), "dp", scatter_dimension=1, tiled=True
        ).astype(jnp.float32),
        lax.psum_scatter(
            up_term.astype(jnp.bfloat16), "dp", scatter_dimension=0, tiled=True
        ).astype(jnp.float32),
        lax.psum_scatter(
            up_bias_term.astype(jnp.bfloat16), "dp", scatter_dimension=1, tiled=True
        ).astype(jnp.float32),
        lax.psum_scatter(
            down_term.astype(jnp.bfloat16), "dp", scatter_dimension=1, tiled=True
        ).astype(jnp.float32),
        lax.psum_scatter(
            second_bias_term.astype(jnp.bfloat16), "dp", scatter_dimension=1, tiled=True
        ).astype(jnp.float32),
        lax.psum_scatter(
            second_gain_term.astype(jnp.bfloat16), "dp", scatter_dimension=1, tiled=True
        ).astype(jnp.float32),
        lax.psum_scatter(
            second_shift_term.astype(jnp.bfloat16), "dp", scatter_dimension=1, tiled=True
        ).astype(jnp.float32),
        lax.psum_scatter(
            cross_in_term.astype(jnp.bfloat16), "dp", scatter_dimension=0, tiled=True
        ).astype(jnp.float32),
        lax.psum_scatter(
            cross_bias_term.astype(jnp.bfloat16), "dp", scatter_dimension=1, tiled=True
        ).astype(jnp.float32),
        lax.psum_scatter(
            cross_out_term.astype(jnp.bfloat16), "dp", scatter_dimension=1, tiled=True
        ).astype(jnp.float32),
        lax.psum_scatter(
            first_bias_term.astype(jnp.bfloat16), "dp", scatter_dimension=1, tiled=True
        ).astype(jnp.float32),
        lax.psum_scatter(
            first_gain_term.astype(jnp.bfloat16), "dp", scatter_dimension=1, tiled=True
        ).astype(jnp.float32),
        lax.psum_scatter(
            first_shift_term.astype(jnp.bfloat16), "dp", scatter_dimension=1, tiled=True
        ).astype(jnp.float32),
    )
    self_total = every_total[0:6]
    feed_total = every_total[6:12]
    cross_total = every_total[12:18]
    out_bias_grad = jnp.concatenate([cross_total[3], feed_total[3], self_total[3]], axis=0)[None]
    norm_gains_grad = jnp.concatenate([cross_total[4], feed_total[4], self_total[4]], axis=0)[None]
    norm_shifts_grad = jnp.concatenate([cross_total[5], feed_total[5], self_total[5]], axis=0)[None]
    return (
        layer_out[None],
        hidden_grad[None],
        cross_total[0][None],
        cross_total[1][None],
        cross_total[2][None],
        feed_total[0][None],
        feed_total[1],
        feed_total[2][None],
        self_total[0][None],
        self_total[1][None],
        self_total[2][None],
        out_bias_grad,
        norm_gains_grad,
        norm_shifts_grad,
    )


def solution(mesh):
    placed = (
        P("stream", "dp", None),
        P("stream", "dp", None),
        P(None, "dp", None),
        P("stream", None, None, "mp"),
        P("stream", None, "mp"),
        P("stream", "mp", None),
        P("stream", None, "mp"),
        P("stream", "mp"),
        P("stream", "mp", None),
        P("stream", None, None, "mp"),
        P("stream", None, "mp"),
        P("stream", "mp", None),
        P("stream", None, None),
        P("stream", None, None),
        P("stream", None, None),
    )
    return jax.shard_map(
        shards,
        mesh=mesh,
        in_specs=placed,
        out_specs=(
            P("stream", "dp", None),
            P("stream", "dp", None),
            P("stream", "dp", None, "mp"),
            P("stream", None, ("mp", "dp")),
            P("stream", "mp", "dp"),
            P("stream", "dp", "mp"),
            P("stream", ("mp", "dp")),
            P("stream", "mp", "dp"),
            P("stream", "dp", None, "mp"),
            P("stream", None, ("mp", "dp")),
            P("stream", "mp", "dp"),
            P("stream", None, "dp"),
            P("stream", None, "dp"),
            P("stream", None, "dp"),
        ),
        check_vma=False,
    )
```

profile of v0, /device:TPU:0, one launch (start us, length us, event | category | flops | bytes accessed | tf_op | source)
XLA Modules:
  0.0 1368.4 jit_solution(18078337223005170312)
XLA Ops:
  7.9 8.5 conditional.16
  7.9 2.7 copy.198
  12.0 3.1 fusion
  17.7 3.4 collective-permute-start.1
  24.2 9.7 collective-permute-done.1
  34.8 9.5 collective-permute-done
  46.2 4.2 conditional.17
  47.8 2.5 pad.93
  51.1 155.5 %all-reduce.44.cloned.1.call-done = f32[1024,1024]{1,0:T(8,128)} async-done(((f32[1024,1024]{1,0:T(8,128)}), f32[1024,1024]{1,0:T(8,128)}) %all-reduce.44.cloned.1.call-update) | async-done | bytes 4194320 | tf_op jit(solution)/shard_map/psum | solution.py:505
  206.6 25.1 %conditional.18 = (f32[1024,1024]{1,0:T(8,128)}, f32[1024,768]{1,0:T(8,128)}, f32[1024,1024]{1,0:T(8,128)}) conditional(s32[]{:T(128)} %convert_element_type.506, (bf16[1024,1024]{1,0:T(8,128)(2,1)S(1)}, f32[1024,1024]{1,0:T(8,128)}, f32[1,3,1024]{2,1,0:T(4,128)S(1)}, f32[1,3,1024]{2,1,0:T(4,128)S(1)}, f32[1,3,1024]{2,1,0:T(4,128)S(1)}, ...), branch_computations={%region_7.10_spmd, %region_10.13_spmd} | conditional | flops 2481193984 | bytes 76364920 | solution.py:494
  211.1 2.8 multiply_add_fusion.5
  213.9 3.1 convolution_add_fusion
  217.0 2.5 pad.94
  219.5 9.5 fusion.166
  229.0 2.5 pad.95
  232.4 154.3 %all-reduce.46.cloned.1.call-done = f32[1024,1024]{1,0:T(8,128)} async-done(((f32[1024,1024]{1,0:T(8,128)}), f32[1024,1024]{1,0:T(8,128)}) %all-reduce.46.cloned.1.call-update) | async-done | bytes 4194320 | tf_op jit(solution)/shard_map/psum | solution.py:505
  386.7 24.0 %conditional.19 = (f32[1024,1024]{1,0:T(8,128)}, bf16[1024,256]{0,1:T(8,128)(2,1)}, bf16[1024,256]{0,1:T(8,128)(2,1)}, bf16[1024,256]{0,1:T(8,128)(2,1)}, bf16[1...) conditional(s32[]{:T(128)} %convert_element_type.506, (f32[1024,1024]{1,0:T(8,128)}, ...), branch_computations={%region_14.19_spmd, %region_19.24_spmd} | conditional | flops 2296642560 | bytes 79400536 | solution.py:494
  386.8 3.3 fusion.291
  395.8 3.0 fusion.204
  404.7 2.5 pad.97
  410.8 4.0 bitcast_convert_fusion
  414.8 159.6 %all-reduce.48.cloned.1.call-done = f32[1024,1024]{1,0:T(8,128)} async-done(((f32[1024,1024]{1,0:T(8,128)}), f32[1024,1024]{1,0:T(8,128)}) %all-reduce.48.cloned.1.call-update) | async-done | bytes 4194320 | tf_op jit(solution)/shard_map/psum | solution.py:505
  574.5 39.7 %conditional.21 = (f32[1024,1024]{1,0:T(8,128)}, bf16[1024,1024]{1,0:T(8,128)(2,1)}, bf16[1024,3,256]{0,2,1:T(8,128)(2,1)S(1)}, bf16[2,256]{1,0:T(2,128)(2,1)S(1...) conditional(s32[]{:T(128)} %convert_element_type.506, ...), branch_computations={%region_31.42_spmd, %region_42.53_spmd} | conditional | flops 4664856064 | bytes 128750808 | solution.py:494
  576.0 3.4 fusion.294
  602.9 3.4 fusion.216
  609.4 2.7 fusion.310
  614.2 93.6 %all-reduce.50.cloned.1.call-done = bf16[1024,1024]{1,0:T(8,128)(2,1)} async-done(((bf16[1024,1024]{1,0:T(8,128)(2,1)}), bf16[1024,1024]{1,0:T(8,128)(2,1)}) %all-reduce.50.cloned.1.call-update) | async-done | bytes 2097168 | tf_op jit(solution)/shard_map/psum | solution.py:508
  707.9 3.7 convert_add_fusion.1
  712.9 32.2 %conditional.22 = (f32[1024,1024]{1,0:T(8,128)}, bf16[1024,1024]{1,0:T(8,128)(2,1)S(1)}, bf16[1024,768]{0,1:T(8,128)(2,1)}, bf16[1,768]{1,0:T(2,128)(2,1)S(1)}, ...) conditional(s32[]{:T(128)} %convert_element_type.506, ...), branch_computations={%region_54.63_spmd, %region_63.72_spmd} | conditional | flops 4916776960 | bytes 89024080 | solution.py:494
  719.3 7.6 fusion.236
  726.9 3.4 fusion.242
  730.4 4.2 convert_reduce_fusion.10
  734.6 3.4 convolution_bitcast_fusion.3
  740.7 2.5 pad.113
  754.8 2.6 copy.236
  757.5 73.7 %all-reduce.52.cloned.1.call-done = bf16[1024,1024]{1,0:T(8,128)(2,1)} async-done(((bf16[1024,1024]{1,0:T(8,128)(2,1)}), bf16[1024,1024]{1,0:T(8,128)(2,1)}) %all-reduce.52.cloned.1.call-update) | async-done | bytes 2097168 | tf_op jit(solution)/shard_map/psum | solution.py:508
  831.2 17.2 %conditional.23 = (f32[1024,1024]{1,0:T(8,128)}, bf16[256,1024]{0,1:T(8,128)(2,1)}, f32[1,1024]{1,0:T(1,128)S(1)}, f32[1,1024]{1,0:T(1,128)S(1)}, f32[1,1024]{1,0:T(1,128)S(1)}, /*index=5*/bf16[1024,256]{1,0:T(8,128)(2,1)}) conditional(s32[]{:T(128)} %convert_element_type.506, (bf16[1024,1024]{1,0:T(8,128)(2,1)}, f32[1024,1024]{1,0:T(8,128)}, ...), branch_computations={%region_73.81_spmd, %region_81.89_spmd} | conditional | flops 1107562496 | bytes 67231824 | solution.py:494
  835.4 3.1 multiply_reduce_fusion.23
  838.5 3.0 fusion.297
  853.4 2.5 multiply_reduce_fusion.26
  860.3 6.6 collective-permute-start.3
  872.8 6.4 collective-permute-done.3
  884.1 2.6 copy.235
  892.7 10.1 collective-permute-done.2
  904.1 10.4 conditional.24
  910.0 2.9 fusion.308
  916.2 5.6 conditional.20
  916.2 3.3 fusion.292
  926.0 18.4 %reduce-scatter.53.cloned.1.call-done = bf16[256,256]{1,0:T(8,128)(2,1)} async-done(((bf16[256,1024]{1,0:T(8,128)(2,1)}), bf16[256,256]{1,0:T(8,128)(2,1)}) %reduce-scatter.53.cloned.1.call-update) | async-done | bytes 131088 | tf_op jit(solution)/shard_map/reduce_scatter | solution.py:638
  946.0 20.6 %reduce-scatter.57.cloned.1.call-done = bf16[192,1]{1,0:T(8,128)(2,1)} async-done(((bf16[768,1]{1,0:T(8,128)(2,1)}), bf16[192,1]{1,0:T(8,128)(2,1)}) %reduce-scatter.57.cloned.1.call-update) | async-done | bytes 400
  968.1 20.9 %reduce-scatter.75.cloned.1.call-done = bf16[256,1]{1,0:T(8,128)(2,1)} async-done(((bf16[1024,1]{1,0:T(8,128)(2,1)}), bf16[256,1]{1,0:T(8,128)(2,1)}) %reduce-scatter.75.cloned.1.call-update) | async-done | bytes 528
  989.9 21.7 %reduce-scatter.69.cloned.1.call-done = bf16[256,1]{1,0:T(8,128)(2,1)} async-done(((bf16[1024,1]{1,0:T(8,128)(2,1)}), bf16[256,1]{1,0:T(8,128)(2,1)}) %reduce-scatter.69.cloned.1.call-update) | async-done | bytes 528
  1012.6 22.0 %reduce-scatter.63.cloned.1.call-done = bf16[256,1]{1,0:T(8,128)(2,1)} async-done(((bf16[1024,1]{1,0:T(8,128)(2,1)}), bf16[256,1]{1,0:T(8,128)(2,1)}) %reduce-scatter.63.cloned.1.call-update) | async-done | bytes 528
  1035.5 29.9 %reduce-scatter.51.cloned.1.call-done = bf16[256,3,256]{2,0,1:T(8,128)(2,1)} async-done(((bf16[1024,3,256]{2,0,1:T(8,128)(2,1)}), bf16[256,3,256]{2,0,1:T(8,128)(2,1)}) %reduce-scatter.51.cloned.1.call-update) | async-done | bytes 393232 | tf_op jit(solution)/shard_map/reduce_scatter | solution.py:632
  1067.3 20.4 %reduce-scatter.61.cloned.1.call-done = bf16[256,1]{1,0:T(8,128)(2,1)} async-done(((bf16[1024,1]{1,0:T(8,128)(2,1)}), bf16[256,1]{1,0:T(8,128)(2,1)}) %reduce-scatter.61.cloned.1.call-update) | async-done | bytes 528
  1089.2 21.0 %reduce-scatter.67.cloned.1.call-done = bf16[256,1]{1,0:T(8,128)(2,1)} async-done(((bf16[1024,1]{1,0:T(8,128)(2,1)}), bf16[256,1]{1,0:T(8,128)(2,1)}) %reduce-scatter.67.cloned.1.call-update) | async-done | bytes 528
  1111.8 20.8 %reduce-scatter.73.cloned.1.call-done = bf16[256,1]{1,0:T(8,128)(2,1)} async-done(((bf16[1024,1]{1,0:T(8,128)(2,1)}), bf16[256,1]{1,0:T(8,128)(2,1)}) %reduce-scatter.73.cloned.1.call-update) | async-done | bytes 528
  1134.1 20.5 %reduce-scatter.55.cloned.1.call-done = bf16[64,2]{1,0:T(8,128)(2,1)} async-done(((bf16[256,2]{1,0:T(8,128)(2,1)}), bf16[64,2]{1,0:T(8,128)(2,1)}) %reduce-scatter.55.cloned.1.call-update) | async-done | bytes 272
  1156.0 22.7 %reduce-scatter.45.cloned.1.call-done = bf16[256,256]{1,0:T(8,128)(2,1)} async-done(((bf16[256,1024]{1,0:T(8,128)(2,1)}), bf16[256,256]{1,0:T(8,128)(2,1)}) %reduce-scatter.45.cloned.1.call-update) | async-done | bytes 131088 | tf_op jit(solution)/shard_map/reduce_scatter | solution.py:674
  1180.3 29.3 %reduce-scatter.49.cloned.1.call-done = bf16[768,256]{1,0:T(8,128)(2,1)} async-done(((bf16[768,1024]{1,0:T(8,128)(2,1)}), bf16[768,256]{1,0:T(8,128)(2,1)}) %reduce-scatter.49.cloned.1.call-update) | async-done | bytes 393232 | tf_op jit(solution)/shard_map/reduce_scatter | solution.py:656
  1211.5 28.8 %reduce-scatter.47.cloned.1.call-done = bf16[256,768]{1,0:T(8,128)(2,1)} async-done(((bf16[1024,768]{1,0:T(8,128)(2,1)}), bf16[256,768]{1,0:T(8,128)(2,1)}) %reduce-scatter.47.cloned.1.call-update) | async-done | bytes 393232 | tf_op jit(solution)/shard_map/reduce_scatter | solution.py:650
  1242.2 87.7 %all-reduce.54.cloned.1.call-done = bf16[1024,1024]{1,0:T(8,128)(2,1)} async-done(((bf16[1024,1024]{1,0:T(8,128)(2,1)}), bf16[1024,1024]{1,0:T(8,128)(2,1)}) %all-reduce.54.cloned.1.call-update) | async-done | bytes 2097168 | tf_op jit(solution)/shard_map/psum | solution.py:508
  1329.9 5.0 fusion.262
  1334.9 24.6 %reduce-scatter.43.cloned.1.call-done = bf16[256,3,256]{2,0,1:T(8,128)(2,1)} async-done(((bf16[1024,3,256]{2,0,1:T(8,128)(2,1)}), bf16[256,3,256]{2,0,1:T(8,128)(2,1)}) %reduce-scatter.43.cloned.1.call-update) | async-done | bytes 393232 | tf_op jit(solution)/shard_map/reduce_scatter | solution.py:668
  (390 shorter events, 157.7 us)
Async XLA Ops:
  7.2 199.4 %all-reduce.44.cloned.1.call-start = ((), (), s32[]{:S(2)}) async-start(), calls=%async_computation.18 | async-start | bytes 8388608 | tf_op jit(solution)/shard_map/psum | solution.py:505
  7.9 15.4 %copy-start.63 = (s32[2,8,128]{2,1,0:T(8,128)S(1)}, s32[2,8,128]{2,1,0:T(8,128)}, u32[]{:S(2)}) copy-start(s32[2,8,128]{2,1,0:T(8,128)} %param.35) | copy-start | bytes 24580
  7.9 4.1 copy-start.4
  17.7 16.2 %collective-permute-start.1 = (bf16[1024,256]{1,0:T(8,128)(2,1)S(1)}, bf16[1024,256]{1,0:T(8,128)(2,1)S(1)}, u32[]{:S(2)}, u32[]{:S(2)}) collective-permute-start(bf16[1024,256]{1,0:T(8,128)(2,1)S(1)} %slice.471), channel_id=1, source_target_pairs={{0,16},{16,0},{1,17},{17,1},{2,18},{18,2},{3,19},{19,3},{4,20},{20... | collective-permute-start | bytes 1572872 | tf_op jit(solution)/shard_map/ppermute | solution.py:29
  23.2 21.1 %collective-permute-start = (bf16[1024,256]{1,0:T(8,128)(2,1)}, bf16[1024,256]{1,0:T(8,128)(2,1)S(1)}, u32[]{:S(2)}, u32[]{:S(2)}) collective-permute-start(bf16[1024,256]{1,0:T(8,128)(2,1)} %add_convert_fusion.5), channel_id=1, source_target_pairs={{0,16},{16,0},{1,17},{17,1},{2,18},{18,2},{3,19},{19,3},{4,20},{20... | collective-permute-start | bytes 1572872 | tf_op jit(solution)/shard_map/ppermute | solution.py:29
  24.2 20.1 %copy-start.26 = (bf16[8,128,2,128]{1,3,2,0:T(8,128)(2,1)}, bf16[8,128,2,128]{1,3,2,0:T(8,128)(2,1)S(1)}, u32[]{:S(2)}) copy-start(bf16[8,128,2,128]{1,3,2,0:T(8,128)(2,1)S(1)} %copy.222) | copy-start | bytes 1572868
  34.4 10.5 copy-start.13
  34.4 10.5 copy-start.53
  34.8 10.4 copy-start.55
  50.4 156.2 %copy-start.2 = (bf16[1,1024,1024]{2,1,0:T(8,128)(2,1)S(1)}, bf16[1,1024,1024]{2,1,0:T(8,128)(2,1)}, u32[]{:S(2)}) copy-start(bf16[1,1024,1024]{2,1,0:T(8,128)(2,1)} %param.33) | copy-start | bytes 6291460
  50.4 336.3 %all-reduce.46.cloned.1.call-start = ((), (), s32[]{:S(2)}) async-start(), calls=%async_computation.19 | async-start | bytes 8388608 | tf_op jit(solution)/shard_map/psum | solution.py:505
  51.1 523.4 %copy-start.44 = (f32[1,3,1024]{2,1,0:T(4,128)}, f32[1,3,1024]{2,1,0:T(4,128)S(1)}, u32[]{:S(2)}) copy-start(f32[1,3,1024]{2,1,0:T(4,128)S(1)} %convert_element_type.514) | copy-start | bytes 36868
  51.1 335.6 %copy-start.50 = (f32[1,3,1024]{2,1,0:T(4,128)}, f32[1,3,1024]{2,1,0:T(4,128)S(1)}, u32[]{:S(2)}) copy-start(f32[1,3,1024]{2,1,0:T(4,128)S(1)} %convert_element_type.515) | copy-start | bytes 36868
  207.1 3.1 copy-start
  211.1 2.8 copy-start.41
  217.0 2.5 copy-start.68
  231.8 155.0 %copy-start.11 = (bf16[1,1024,3,256]{3,1,2,0:T(8,128)(2,1)S(1)}, bf16[1,1024,3,256]{3,1,2,0:T(8,128)(2,1)}, u32[]{:S(2)}) copy-start(bf16[1,1024,3,256]{3,1,2,0:T(8,128)(2,1)} %param.42) | copy-start | bytes 4718596
  231.8 155.0 %copy-start.21 = (bf16[1,256,1024]{2,1,0:T(8,128)(2,1)S(1)}, bf16[1,256,1024]{2,1,0:T(8,128)(2,1)}, u32[]{:S(2)}) copy-start(bf16[1,256,1024]{2,1,0:T(8,128)(2,1)} %param.44) | copy-start | bytes 1572868
  231.8 342.7 %all-reduce.48.cloned.1.call-start = ((), (), s32[]{:S(2)}) async-start(), calls=%async_computation.20 | async-start | bytes 8388608 | tf_op jit(solution)/shard_map/psum | solution.py:505
  410.8 297.1 %all-reduce.50.cloned.1.call-start = ((), (), s32[]{:S(2)}) async-start(), calls=%async_computation.21 | async-start | bytes 4194304 | tf_op jit(solution)/shard_map/psum | solution.py:508
  574.6 4.8 copy-start.48
  574.7 4.8 copy-start.51
  576.0 4.0 copy-start.6
  588.5 4.7 copy-start.36
  602.9 3.4 copy-start.47
  614.2 97.4 %copy-start.20 = (bf16[1024,3,256]{0,2,1:T(8,128)(2,1)}, bf16[1024,3,256]{0,2,1:T(8,128)(2,1)S(1)}, u32[]{:S(2)}) copy-start(bf16[1024,3,256]{0,2,1:T(8,128)(2,1)S(1)} %get-tuple-element.465) | copy-start | bytes 4718596
  614.2 217.0 %all-reduce.52.cloned.1.call-start = ((), (), s32[]{:S(2)}) async-start(), calls=%async_computation.22 | async-start | bytes 4194304 | tf_op jit(solution)/shard_map/psum | solution.py:508
  707.8 4.1 copy-start.8
  707.8 4.5 copy-start.40
  707.8 4.5 copy-start.45
  707.9 5.0 copy-start.67
  712.9 34.5 %copy-start.59 = (f32[1,1024]{1,0:T(1,128)S(1)}, f32[1,1024]{1,0:T(1,128)}, u32[]{:S(2)}) copy-start(f32[1,1024]{1,0:T(1,128)} %get-tuple-element.476) | copy-start | bytes 12292
  712.9 35.5 %copy-start.58 = (f32[1,1024]{1,0:T(1,128)S(1)}, f32[1,1024]{1,0:T(1,128)}, u32[]{:S(2)}) copy-start(f32[1,1024]{1,0:T(1,128)} %get-tuple-element.473) | copy-start | bytes 12292
  745.1 4.2 copy-start.57
  746.5 175.4 %reduce-scatter.59.cloned.1.call-start = ((), (), s32[]{:S(2)}) async-start(), calls=%async_computation.32 | async-start | bytes 81920
  747.3 176.0 %reduce-scatter.77.cloned.1.call-start = ((), (), s32[]{:S(2)}) async-start(), calls=%async_computation.41 | async-start | bytes 327680
  748.3 175.9 %reduce-scatter.71.cloned.1.call-start = ((), (), s32[]{:S(2)}) async-start(), calls=%async_computation.38 | async-start | bytes 327680
  749.3 175.8 %reduce-scatter.65.cloned.1.call-start = ((), (), s32[]{:S(2)}) async-start(), calls=%async_computation.35 | async-start | bytes 327680
  750.3 194.2 %reduce-scatter.53.cloned.1.call-start = ((), (), s32[]{:S(2)}) async-start(), calls=%async_computation.29 | async-start | bytes 655360 | tf_op jit(solution)/shard_map/reduce_scatter | solution.py:638
  750.8 215.8 %reduce-scatter.57.cloned.1.call-start = ((), (), s32[]{:S(2)}) async-start(), calls=%async_computation.31 | async-start | bytes 245760
  751.8 237.2 %reduce-scatter.75.cloned.1.call-start = ((), (), s32[]{:S(2)}) async-start(), calls=%async_computation.40 | async-start | bytes 327680
  751.8 5.6 copy-start.54
  751.8 5.6 copy-start.56
  751.8 79.3 %copy-start.3 = (bf16[1,1024,1024]{2,1,0:T(8,128)(2,1)S(1)}, bf16[1,1024,1024]{2,1,0:T(8,128)(2,1)}, u32[]{:S(2)}) copy-start(bf16[1,1024,1024]{2,1,0:T(8,128)(2,1)} %param.33) | copy-start | bytes 6291460
  751.9 79.3 %copy-start.18 = (bf16[1,256,1024]{2,1,0:T(8,128)(2,1)S(1)}, bf16[1,256,1024]{2,1,0:T(8,128)(2,1)}, u32[]{:S(2)}) copy-start(bf16[1,256,1024]{2,1,0:T(8,128)(2,1)} %param.38) | copy-start | bytes 1572868
  752.8 258.9 %reduce-scatter.69.cloned.1.call-start = ((), (), s32[]{:S(2)}) async-start(), calls=%async_computation.37 | async-start | bytes 327680
  753.7 280.8 %reduce-scatter.63.cloned.1.call-start = ((), (), s32[]{:S(2)}) async-start(), calls=%async_computation.34 | async-start | bytes 327680
  754.7 310.6 %reduce-scatter.51.cloned.1.call-start = ((), (), s32[]{:S(2)}) async-start(), calls=%async_computation.28 | async-start | bytes 1966080 | tf_op jit(solution)/shard_map/reduce_scatter | solution.py:632
  757.4 330.3 %reduce-scatter.61.cloned.1.call-start = ((), (), s32[]{:S(2)}) async-start(), calls=%async_computation.33 | async-start | bytes 327680
  848.4 5.0 copy-start.14
  853.3 256.9 %reduce-scatter.67.cloned.1.call-start = ((), (), s32[]{:S(2)}) async-start(), calls=%async_computation.36 | async-start | bytes 327680
  853.3 2.6 copy-start.22
  860.3 18.8 %collective-permute-start.3 = (bf16[1024,256]{0,1:T(8,128)(2,1)}, bf16[1024,256]{0,1:T(8,128)(2,1)}, u32[]{:S(2)}, u32[]{:S(2)}) collective-permute-start(bf16[1024,256]{0,1:T(8,128)(2,1)} %bitcast.391), channel_id=1, source_target_pairs={{0,16},{16,0},{1,17},{17,1},{2,18},{18,2},{3,19},{19,3},{4,20},{20... | collective-permute-start | bytes 1572872 | tf_op jit(solution)/shard_map/ppermute | solution.py:29
  866.9 265.6 %reduce-scatter.73.cloned.1.call-start = ((), (), s32[]{:S(2)}) async-start(), calls=%async_computation.39 | async-start | bytes 327680
  872.8 281.8 %reduce-scatter.55.cloned.1.call-start = ((), (), s32[]{:S(2)}) async-start(), calls=%async_computation.30 | async-start | bytes 81920
  881.1 297.5 %reduce-scatter.45.cloned.1.call-start = ((), (), s32[]{:S(2)}) async-start(), calls=%async_computation.25 | async-start | bytes 655360 | tf_op jit(solution)/shard_map/reduce_scatter | solution.py:674
  883.3 326.3 %reduce-scatter.49.cloned.1.call-start = ((), (), s32[]{:S(2)}) async-start(), calls=%async_computation.27 | async-start | bytes 1966080 | tf_op jit(solution)/shard_map/reduce_scatter | solution.py:656
  883.3 3.4 copy-start.24
  883.3 3.4 copy-start.27
  884.0 356.3 %reduce-scatter.47.cloned.1.call-start = ((), (), s32[]{:S(2)}) async-start(), calls=%async_computation.26 | async-start | bytes 1966080 | tf_op jit(solution)/shard_map/reduce_scatter | solution.py:650
  886.7 443.3 %all-reduce.54.cloned.1.call-start = ((), (), s32[]{:S(2)}) async-start(), calls=%async_computation.23 | async-start | bytes 4194304 | tf_op jit(solution)/shard_map/psum | solution.py:508
  889.5 13.3 collective-permute-start.2
  914.5 444.9 %reduce-scatter.43.cloned.1.call-start = ((), (), s32[]{:S(2)}) async-start(), calls=%async_computation.24 | async-start | bytes 1966080 | tf_op jit(solution)/shard_map/reduce_scatter | solution.py:668
  921.8 413.1 %copy-start.25 = (bf16[1,1024,1024]{2,1,0:T(8,128)(2,1)}, bf16[1,1024,1024]{2,1,0:T(8,128)(2,1)S(1)}, u32[]{:S(2)}) copy-start(bf16[1,1024,1024]{2,1,0:T(8,128)(2,1)S(1)} %get-tuple-element.942) | copy-start | bytes 6291460
  (21 other events, 30.2 us)
Sparse Core Ops, SparseCore 0:
  50.5 156.0 all-reduce.43
  231.9 154.7 all-reduce.45
  410.9 163.5 all-reduce.47
  614.3 93.4 all-reduce.49
  746.6 84.5 all-reduce.51
  833.6 18.3 reduce-scatter.58
  854.5 19.9 reduce-scatter.76
  877.1 19.9 reduce-scatter.70
  900.2 20.0 reduce-scatter.64
  922.8 21.6 reduce-scatter.52
  946.9 19.7 reduce-scatter.56
  968.9 20.0 reduce-scatter.74
  991.6 19.9 reduce-scatter.68
  1014.5 20.0 reduce-scatter.62
  1037.1 28.1 reduce-scatter.50
  1067.7 19.9 reduce-scatter.60
  1090.1 20.0 reduce-scatter.66
  1112.5 19.9 reduce-scatter.72
  1135.1 19.4 reduce-scatter.54
  1156.9 21.6 reduce-scatter.44
  1181.3 28.1 reduce-scatter.48
  1212.1 28.1 reduce-scatter.46
  1243.4 86.5 all-reduce.53
  1332.3 27.1 reduce-scatter.42
where the time goes:
time: 1380 us; the launch traced here: 1370 us
  waiting for transfers between devices  1080 us (78%)
  local copies, waits for them, and re-layouts  110 us (8%)
  other arithmetic  81.8 us (6%)
  matrix products  62.2 us (5%)
  between operations  15.2 us (1%)
    psum x3, waiting for transfers between devices, across_heads(): return lax.psum(partial_out, 'mp')  469 us
    psum x3, waiting for transfers between devices, across_inputs(): return lax.psum(partial_in.astype(jnp.bfloat16), 'mp').astype(jnp.float32)  255 us
    unnamed x36, waiting for transfers between devices  170 us
    ppermute x4, waiting for transfers between devices, partner(): return lax.ppermute(block, axis, route)  35.6 us
    pad x30, local copies, waits for them, and re-layouts, widen(): jnp.pad(value_in, [(0, want_size - have_size) for have_size, want_size in...  33.7 us
    reduce_scatter x1, waiting for transfers between devices, shards(): lax.psum_scatter(attend_in_term.astype(jnp.bfloat16), 'dp', scatter_dimen...  29.9 us
    unnamed x106, local copies, waits for them, and re-layouts  29.8 us
    reduce_scatter x1, waiting for transfers between devices, shards(): lax.psum_scatter(down_term.astype(jnp.bfloat16), 'dp', scatter_dimension=...  29.3 us
  transfers between devices with their start and end apart: 28, of which 24 were waited for; matrix products, arithmetic and copies ran while one was open for 8% of the time, Pallas kernels for 0%

commit v1 on v0

v1 whole, which is shorter than its diff:
```python
import math
from functools import partial

import jax
import jax.numpy as jnp
from jax import lax
from jax.experimental import pallas as pl
from jax.experimental.pallas import tpu as pltpu
from jax.sharding import PartitionSpec as P

TEXT_WIDTH = 768
TEXT_HEADS = 12
TEXT_FF = 3072
IMAGE_WIDTH = 1024
IMAGE_HEADS = 8
IMAGE_FF = 1024
CO_HEADS = 8

norm_eps = 1e-12
masked_score = -1000000000.0
low = jnp.bfloat16
wide = jnp.float32
ANY = pl.BlockSpec(memory_space=pl.ANY)
VMEM = pl.BlockSpec(memory_space=pltpu.VMEM)
MESH = pl.DeviceIdType.MESH
VMEM_LIMIT = 64000 * 1024
TILE = 256


def dot(left, right):
    return jnp.dot(left, right, preferred_element_type=wide)


def dot_nt(left, right):
    return lax.dot_general(left, right, (((1,), (1,)), ((), ())), preferred_element_type=wide)


def dot_tn(left, right):
    return lax.dot_general(left, right, (((0,), (0,)), ((), ())), preferred_element_type=wide)


class Setting:
    def __init__(self, width, count, units, groups):
        self.width = width
        self.head = width // count
        self.units = units // groups
        self.lanes = width // groups
        self.parts = width // TILE
        self.per_group = count // groups


class Layout:
    def __init__(self, s, inner):
        self.attend_out = 0
        self.attend_in = inner
        self.down = 4 * inner
        self.up = 4 * inner + s.units
        self.cross_out = 4 * inner + 2 * s.units
        self.total = 5 * inner + 2 * s.units


def lane(start, size=TILE):
    return pl.ds(pl.multiple_of(start, 128), size)


def ring_gather(groups, stride, pieces, z, copy, sems):
    send_z, recv_z, send_y, recv_y, send_c, recv_c = sems
    quarter = lax.rem(copy // stride, 4)
    to_y = (quarter ^ 2) * stride + lax.rem(copy, stride)
    to_c = (quarter ^ 1) * stride + lax.rem(copy, stride)
    count = len(pieces)

    def z_copy(p, way, hop):
        step = 1 - 2 * way
        origin = z - hop * step
        source, full, cut = pieces[p]
        src = cut(source, quarter) if hop == 0 else cut(full.at[origin], quarter)
        return pltpu.make_async_remote_copy(
            src, cut(full.at[origin], quarter), send_z.at[p, way, hop], recv_z.at[p, way, hop],
            device_id={"mp": z + step}, device_id_type=MESH)

    def z_arrival(p, way, hop):
        step = 1 - 2 * way
        origin = z - (hop + 1) * step
        source, full, cut = pieces[p]
        block = cut(full.at[origin], quarter)
        return pltpu.make_async_remote_copy(
            block, block, send_z.at[p, way, hop], recv_z.at[p, way, hop],
            device_id={"mp": z - step}, device_id_type=MESH)

    def y_copy(p, way, hop):
        origin = z - (hop + 1) * (1 - 2 * way)
        source, full, cut = pieces[p]
        block = cut(full.at[origin], quarter)
        return pltpu.make_async_remote_copy(
            block, block, send_y.at[p, way, hop], recv_y.at[p, way, hop],
            device_id={"dp": to_y}, device_id_type=MESH)

    def y_arrival(p, way, hop):
        origin = z - (hop + 1) * (1 - 2 * way)
        source, full, cut = pieces[p]
        block = cut(full.at[origin], quarter ^ 2)
        return pltpu.make_async_remote_copy(
            block, block, send_y.at[p, way, hop], recv_y.at[p, way, hop],
            device_id={"dp": to_y}, device_id_type=MESH)

    def c_copy(p, way, hop, which, mine=True):
        origin = z - (hop + 1) * (1 - 2 * way)
        source, full, cut = pieces[p]
        whose = (quarter if mine else quarter ^ 1) ^ (2 * which)
        block = cut(full.at[origin], whose)
        return pltpu.make_async_remote_copy(
            block, block, send_c.at[p, way, hop, which], recv_c.at[p, way, hop, which],
            device_id={"dp": to_c}, device_id_type=MESH)

    def sends(way, hop):
        if way == 0:
            return jnp.logical_and(z >= hop, z < groups - 1)
        return jnp.logical_and(z <= groups - 1 - hop, z > 0)

    def arrives(way, hop):
        return z >= hop + 1 if way == 0 else z <= groups - 2 - hop

    at_end = jnp.logical_or(z == 0, z == groups - 1)
    ahead = 2

    def own(p):
        for way in range(2):
            @pl.when(sends(way, 0))
            def _():
                z_copy(p, way, 0).start()

    def received(p):
        for hop in range(groups - 1):
            for way in range(2):
                @pl.when(arrives(way, hop))
                def _():
                    z_arrival(p, way, hop).wait_recv()
                    if hop + 1 < groups - 1:
                        @pl.when(sends(way, hop + 1))
                        def _():
                            z_copy(p, way, hop + 1).start()
                    y_copy(p, way, hop).start()
                    c_copy(p, way, hop, 0).start()

    def shared(p):
        for hop in range(groups - 1):
            for way in range(2):
                @pl.when(arrives(way, hop))
                def _():
                    y_arrival(p, way, hop).wait_recv()
                    c_copy(p, way, hop, 1).start()

    def settled(p):
        for hop in range(groups - 1):
            for way in range(2):
                @pl.when(arrives(way, hop))
                def _():
                    for which in range(2):
                        c_copy(p, way, hop, which, mine=False).wait_recv()

    def drained(p):
        for hop in range(groups - 1):
            for way in range(2):
                @pl.when(sends(way, hop))
                def _():
                    z_copy(p, way, hop).wait_send()

                @pl.when(arrives(way, hop))
                def _():
                    y_copy(p, way, hop).wait_send()
                    for which in range(2):
                        c_copy(p, way, hop, which).wait_send()

    for p in range(min(ahead, count)):
        own(p)
    for p in range(ahead, count):
        pl.when(at_end)(partial(own, p))
    for p in range(count):
        received(p)
        if p + ahead < count:
            pl.when(jnp.logical_not(at_end))(partial(own, p + ahead))
        if p:
            shared(p - 1)
    shared(count - 1)
    for p in range(count):
        settled(p)
    for p in range(count):
        drained(p)


def greet(groups, z, partners):
    barrier = pltpu.get_barrier_semaphore()
    for step in (-1, 1):
        @pl.when(jnp.logical_and(z + step >= 0, z + step < groups))
        def _():
            pl.semaphore_signal(barrier, inc=1, device_id={"mp": z + step}, device_id_type=MESH)
    for peer in partners:
        pl.semaphore_signal(barrier, inc=1, device_id=peer, device_id_type=MESH)
    at_end = jnp.logical_or(z == 0, z == groups - 1)

    @pl.when(at_end)
    def _():
        pl.semaphore_wait(barrier, 1 + len(partners))

    @pl.when(jnp.logical_not(at_end))
    def _():
        pl.semaphore_wait(barrier, 2 + len(partners))


def gather_kernel(settings, groups, stride, cross_in, cross_out, up, down, attend_in, attend_out,
                  f_cross_in, f_cross_out, f_up, f_down, f_attend_in, f_attend_out,
                  send_z, recv_z, send_y, recv_y, send_c, recv_c, local):
    z = lax.axis_index("mp")
    copy = lax.axis_index("dp")
    side = lax.axis_index("stream")
    quarter = lax.rem(copy // stride, 4)
    to_y = (quarter ^ 2) * stride + lax.rem(copy, stride)
    to_c = (quarter ^ 1) * stride + lax.rem(copy, stride)
    greet(groups, z, [{"dp": to_y}, {"dp": to_c}])
    inner = cross_out.shape[0]

    def run(s):
        w, u = s.width, s.units

        def projection(ref, part):
            return ref.at[:, pl.ds(part * (w // 4), w // 4), :]

        def leave(ref, part):
            return ref.at[pl.ds(part * (inner // 4), inner // 4), pl.ds(0, w)]

        def enter(ref, part):
            return ref.at[pl.ds(part * (w // 4), w // 4), pl.ds(0, u)]

        def fall(ref, part):
            return ref.at[pl.ds(part * (u // 4), u // 4), pl.ds(0, w)]

        pieces = [
            (cross_in, f_cross_in, projection),
            (cross_out, f_cross_out, leave),
            (up, f_up, enter),
            (down, f_down, fall),
            (attend_in, f_attend_in, projection),
            (attend_out, f_attend_out, leave),
        ]
        mine = []
        for p, (source, full, cut) in enumerate(pieces):
            if cut is projection:
                pair = [ref.at[:, pl.ds(0, w), :] for ref in (source, full.at[z])]
            elif cut is enter:
                pair = [ref.at[pl.ds(0, w), pl.ds(0, u)] for ref in (source, full.at[z])]
            else:
                rows = inner if cut is leave else u
                pair = [ref.at[pl.ds(0, rows), pl.ds(0, w)] for ref in (source, full.at[z])]
            mine.append(pltpu.make_async_copy(pair[0], pair[1], local.at[p]))
        for item in mine:
            item.start()
        ring_gather(groups, stride, pieces, z, copy,
                    (send_z, recv_z, send_y, recv_y, send_c, recv_c))
        for item in mine:
            item.wait()

    for which, s in enumerate(settings):
        pl.when(side == which)(partial(run, s))


def project_kernel(s, groups, x, bias, full, q, k, v, held, sems):
    w = s.width
    inner = held.shape[3]
    loads = [
        pltpu.make_async_copy(full.at[z, :, pl.ds(0, w), :], held.at[z, :, pl.ds(0, w), :],
                              sems.at[z]) for z in range(groups)]
    for load in loads:
        load.start()
    for z in range(groups):
        loads[z].wait()
        cols = slice(z * inner, (z + 1) * inner)
        own = x[:, :w]
        k[:, cols] = dot(own, held[z, 1, :w]).astype(low)
        v[:, cols] = (dot(own, held[z, 2, :w]) + bias[1:2, cols]).astype(low)
        q[:, cols] = (dot(own, held[z, 0, :w]) + bias[0:1, cols]).astype(low)


def softmax(scores, allowed):
    scores = jnp.where(allowed, scores, masked_score)
    exponent = jnp.exp(scores - jnp.max(scores, axis=-1, keepdims=True))
    return exponent / jnp.sum(exponent, axis=-1, keepdims=True)


def norm_into(summed_ref, normal_ref, inverse_ref, w):
    summed = summed_ref[...]
    mean = jnp.sum(summed, axis=-1, keepdims=True) * (1.0 / w)
    centred = summed - mean
    inverse = lax.rsqrt(jnp.sum(centred * centred, axis=-1, keepdims=True) * (1.0 / w) + norm_eps)
    normal_ref[...] = centred * inverse
    inverse_ref[...] = inverse


def norm_back(normal, inverse, gain, incoming, w):
    scaled = incoming * gain
    first = jnp.sum(scaled, axis=-1, keepdims=True) * (1.0 / w)
    second = jnp.sum(scaled * normal, axis=-1, keepdims=True) * (1.0 / w)
    return inverse * (scaled - first - normal * second)


def down_sum(value):
    return jnp.sum(value, axis=0, keepdims=True)


def cross_forward(length, rows, q, k, v, allowed, prob, context):
    scale = 1.0 / math.sqrt(128)

    @pl.loop(0, CO_HEADS)
    def _(h):
        cols = lane(h * 128, 128)
        for r in range(rows):
            at = slice(r * length, (r + 1) * length)
            p = softmax(dot_nt(q[at, cols], k[at, cols]) * scale, allowed[at, :] > 0)
            prob[h * rows + r] = p
            context[at, cols] = dot(p.astype(low), v[at, cols]).astype(low)


def score_grad(p, grad):
    return (p * (grad - jnp.sum(grad * p, axis=-1, keepdims=True))).astype(low)


def cross_backward(length, rows, q, k, v, prob, grad_context, dq, dk, dv):
    scale = 1.0 / math.sqrt(128)

    @pl.loop(0, CO_HEADS)
    def _(h):
        cols = lane(h * 128, 128)
        for r in range(rows):
            at = slice(r * length, (r + 1) * length)
            p = prob[h * rows + r]
            dc = grad_context[at, cols]
            ds = score_grad(p, dot_nt(dc, v[at, cols]))
            dv[at, cols] = dot_tn(p.astype(low), dc).astype(low)
            dq[at, cols] = (dot(ds, k[at, cols]) * scale).astype(low)
            dk[at, cols] = (dot_tn(ds, q[at, cols]) * scale).astype(low)


def head_slots(s, groups):
    if s.head == 128:
        return [(b, None) for b in range(s.per_group)]
    return [(h // 2, h % 2) for h in range(s.per_group)]


def half(value, which):
    if which is None:
        return value
    index = lax.broadcasted_iota(jnp.int32, value.shape, 1)
    keep = index < 64 if which == 0 else index >= 64
    return jnp.where(keep, value, jnp.zeros_like(value))


def self_forward(s, groups, length, rows, q, k, v, allowed, prob, context):
    scale = 1.0 / math.sqrt(s.head)
    inner = q.shape[1] // groups
    slots = head_slots(s, groups)

    @pl.loop(0, groups)
    def _(z):
        for b in range(inner // 128):
            cols = lane(z * inner + b * 128, 128)
            for r in range(rows):
                at = slice(r * length, (r + 1) * length)
                out = jnp.zeros((length, 128), wide)
                for i, (block, part) in enumerate(slots):
                    if block != b:
                        continue
                    qh = half(q[at, cols], part)
                    p = softmax(dot_nt(qh, k[at, cols]) * scale, allowed[at, :] > 0)
                    prob[(z * len(slots) + i) * rows + r] = p
                    out = out + half(dot(p.astype(low), v[at, cols]), part)
                context[at, cols] = out.astype(low)


def self_backward(s, groups, length, rows, q, k, v, prob, grad_context, dq, dk, dv):
    scale = 1.0 / math.sqrt(s.head)
    inner = q.shape[1] // groups
    slots = head_slots(s, groups)

    @pl.loop(0, groups)
    def _(z):
        for b in range(inner // 128):
            cols = lane(z * inner + b * 128, 128)
            for r in range(rows):
                at = slice(r * length, (r + 1) * length)
                sums = [jnp.zeros((length, 128), wide)] * 3
                for i, (block, part) in enumerate(slots):
                    if block != b:
                        continue
                    p = prob[(z * len(slots) + i) * rows + r]
                    dc = half(grad_context[at, cols], part)
                    ds = score_grad(p, dot_nt(dc, v[at, cols]))
                    sums = [
                        sums[0] + half(dot(ds, k[at, cols]) * scale, part),
                        sums[1] + half(dot_tn(ds, q[at, cols]) * scale, part),
                        sums[2] + dot_tn(p.astype(low), dc),
                    ]
                dq[at, cols] = sums[0].astype(low)
                dk[at, cols] = sums[1].astype(low)
                dv[at, cols] = sums[2].astype(low)


def middle_kernel(s, layout, groups, length,
                  x, grad_out, q, k, v, cross_allowed, self_allowed, up_bias, attend_bias,
                  out_bias, gains, shifts, f_cross_out, f_up, f_down, f_attend_in, f_attend_out,
                  layer_out, entry, dq, dk, dv, grads, vectors, up_sums, attend_sums,
                  w_cross_out, w_up, w_down, w_attend_in, w_attend_out, staged,
                  context, cross_prob, acc, n1, n2, n3, r1, r2, r3, h1, h2, slope, active,
                  q2, k2, v2, self_prob, context2, low_grad, grad_context, dq2, dk2, dv2, dz,
                  load_sem, store_sem):
    w, u = s.width, s.units
    inner = f_cross_out.shape[1]
    rows = x.shape[0] // length
    loads = {}
    number = 0

    def load(name, src, dst):
        nonlocal number
        item = pltpu.make_async_copy(src, dst, load_sem.at[number])
        number += 1
        item.start()
        loads.setdefault(name, []).append(item)

    for z in range(groups):
        load("co", f_cross_out.at[z, :, pl.ds(0, w)], w_cross_out.at[pl.ds(z * inner, inner)])
    for z in range(groups):
        load("up", f_up.at[z, pl.ds(0, w), pl.ds(0, u)], w_up.at[z])
    for z in range(groups):
        load("down", f_down.at[z, pl.ds(0, u), pl.ds(0, w)], w_down.at[pl.ds(z * u, u)])
    for z in range(groups):
        load("ai", f_attend_in.at[z, :, pl.ds(0, w)], w_attend_in.at[z])
    for z in range(groups):
        load("ao", f_attend_out.at[z, :, pl.ds(0, w)], w_attend_out.at[pl.ds(z * inner, inner)])

    def ready(name):
        for item in loads[name]:
            item.wait()

    cross_forward(length, rows, q, k, v, cross_allowed, cross_prob, context)
    ready("co")

    def leave(source, weight, residual, line):
        @pl.loop(0, s.parts)
        def _(j):
            cols = lane(j * TILE)
            acc[:, cols] = (dot(source[...], weight[:, cols]) + residual(cols)
                            + out_bias[line : line + 1, cols])

    def scaled(normal, line, cols):
        return normal[:, cols] * gains[line : line + 1, cols] + shifts[line : line + 1, cols]

    leave(context, w_cross_out, lambda cols: x[:, cols].astype(wide), 0)
    norm_into(acc, n1, r1, w)
    h1[...] = scaled(n1, 0, slice(0, w)).astype(low)
    ready("up")

    @pl.loop(0, groups)
    def _(z):
        for j in range(u // TILE):
            cols = lane(z * u + j * TILE)
            value = dot(h1[...], w_up[z, :, j * TILE : (j + 1) * TILE]) + up_bias[0:1, cols]
            bell = 0.5 * (1.0 + lax.erf(value * math.sqrt(0.5)))
            active[:, cols] = (value * bell).astype(low)
            slope[:, cols] = bell + value * (
                jnp.exp(-0.5 * value * value) * (1.0 / math.sqrt(2.0 * math.pi)))

    ready("down")
    leave(active, w_down, lambda cols: scaled(n1, 0, cols), 1)
    norm_into(acc, n2, r2, w)
    h2[...] = scaled(n2, 1, slice(0, w)).astype(low)
    ready("ai")

    @pl.loop(0, groups)
    def _(z):
        cols = lane(z * inner, inner)
        q2[:, cols] = (dot(h2[...], w_attend_in[z, 0]) + attend_bias[0:1, cols]).astype(low)
        k2[:, cols] = dot(h2[...], w_attend_in[z, 1]).astype(low)
        v2[:, cols] = (dot(h2[...], w_attend_in[z, 2]) + attend_bias[1:2, cols]).astype(low)

    self_forward(s, groups, length, rows, q2, k2, v2, self_allowed, self_prob, context2)
    ready("ao")
    leave(context2, w_attend_out, lambda cols: scaled(n2, 1, cols), 2)
    norm_into(acc, n3, r3, w)
    layer_out[:, :w] = scaled(n3, 2, slice(0, w)).astype(low)
    if w < layer_out.shape[1]:
        layer_out[:, w:] = jnp.zeros((layer_out.shape[0], layer_out.shape[1] - w), low)
        entry[:, w:] = jnp.zeros((entry.shape[0], entry.shape[1] - w), wide)
    vectors[...] = jnp.zeros_like(vectors)
    up_sums[...] = jnp.zeros_like(up_sums)

    stores = []

    def weight_grads(left, right, row, size):
        for z in range(groups):
            for j in range(size // TILE):
                slot = len(stores)
                start = z * size + j * TILE
                staged[slot] = dot_tn(left[:, start : start + TILE], right[...]).astype(low)
                item = pltpu.make_async_copy(
                    staged.at[slot], grads.at[z, pl.ds(row + j * TILE, TILE), pl.ds(0, w)],
                    store_sem.at[slot])
                item.start()
                stores.append(item)

    def back_norm(incoming, normal, inverse, line):
        vectors[3 + line : 4 + line, :w] = down_sum(incoming * normal[...])
        vectors[6 + line : 7 + line, :w] = down_sum(incoming)
        out = norm_back(normal[...], inverse[...], gains[line : line + 1, :w], incoming, w)
        acc[...] = out
        low_grad[...] = out.astype(low)
        vectors[line : line + 1, :w] = down_sum(low_grad[...].astype(wide))

    back_norm(grad_out[:, :w].astype(wide), n3, r3, 2)

    @pl.loop(0, groups)
    def _(z):
        at = pl.ds(pl.multiple_of(z * inner, inner), inner)
        grad_context[:, lane(z * inner, inner)] = dot_nt(
            low_grad[...], w_attend_out[at, :]).astype(low)

    weight_grads(context2, low_grad, layout.attend_out, inner)
    self_backward(s, groups, length, rows, q2, k2, v2, self_prob, grad_context, dq2, dk2, dv2)
    for which, d in enumerate((dq2, dk2, dv2)):
        weight_grads(d, h2, layout.attend_in + which * inner, inner)
    attend_sums[0:1, :] = down_sum(dq2[...].astype(wide))
    attend_sums[1:2, :] = down_sum(dv2[...].astype(wide))

    @pl.loop(0, groups)
    def _(z):
        cols = lane(z * inner, inner)
        for which, d in enumerate((dq2, dk2, dv2)):
            acc[...] += dot_nt(d[:, cols], w_attend_in[z, which])

    back_norm(acc[...], n2, r2, 1)

    @pl.loop(0, groups)
    def _(z):
        for j in range(u // TILE):
            cols = lane(z * u + j * TILE)
            at = pl.ds(pl.multiple_of(z * u + j * TILE, TILE), TILE)
            value = (dot_nt(low_grad[...], w_down[at, :]) * slope[:, cols]).astype(low)
            dz[:, cols] = value
            up_sums[0:1, cols] = down_sum(value.astype(wide))

    weight_grads(active, low_grad, layout.down, u)
    weight_grads(dz, h1, layout.up, u)

    @pl.loop(0, groups)
    def _(z):
        acc[...] += dot_nt(dz[:, lane(z * u, u)], w_up[z])

    back_norm(acc[...], n1, r1, 0)
    entry[:, :w] = acc[...]

    @pl.loop(0, groups)
    def _(z):
        at = pl.ds(pl.multiple_of(z * inner, inner), inner)
        grad_context[:, lane(z * inner, inner)] = dot_nt(
            low_grad[...], w_cross_out[at, :]).astype(low)

    cross_backward(length, rows, q, k, v, cross_prob, grad_context, dq, dk, dv)
    weight_grads(context, low_grad, layout.cross_out, inner)
    for item in stores:
        item.wait()


def finish_kernel(s, groups, x, entry, dq, dk, dv, full, hidden_grad, grads, sums,
                  held, staged, sems, store_sem):
    w = s.width
    inner = full.shape[3]
    loads = [
        pltpu.make_async_copy(full.at[z, :, pl.ds(0, w), :], held.at[z, :, pl.ds(0, w), :],
                              sems.at[z]) for z in range(groups)]
    for load in loads:
        load.start()
    stores = []
    for which, d in enumerate((dq, dk, dv)):
        for z in range(groups):
            slot = len(stores)
            left = d[:, z * inner : (z + 1) * inner]
            staged[slot] = dot_tn(left, x[:, :w]).astype(low)
            item = pltpu.make_async_copy(
                staged.at[slot], grads.at[z, pl.ds(which * inner, inner), pl.ds(0, w)],
                store_sem.at[slot])
            item.start()
            stores.append(item)
    sums[0:1, :] = down_sum(dq[...].astype(wide))
    sums[1:2, :] = down_sum(dv[...].astype(wide))
    total = entry[:, :w]
    for z in range(groups):
        loads[z].wait()
        cols = slice(z * inner, (z + 1) * inner)
        for which, d in enumerate((dq, dk, dv)):
            total = total + dot_nt(d[:, cols], held[z, which, :w])
    hidden_grad[:, :w] = total.astype(low)
    if w < hidden_grad.shape[1]:
        hidden_grad[:, w:] = jnp.zeros((hidden_grad.shape[0], hidden_grad.shape[1] - w), low)
    for item in stores:
        item.wait()


def reduce_kernel(settings, totals, groups, stride, chunk, lags,
                  grads, layer_rows, hidden_rows, reduced, layer_full, hidden_full,
                  from_core, from_y, from_z, far, own, staged,
                  send_c, recv_c, send_y, recv_y, send_z, recv_z, send_f, recv_f,
                  own_sem, store_sem, send_a, recv_a, local):
    z = lax.axis_index("mp")
    copy = lax.axis_index("dp")
    side = lax.axis_index("stream")
    quarter = lax.rem(copy // stride, 4)
    base = lax.rem(copy, stride)
    y = quarter // 2
    core = lax.rem(quarter, 2)
    to_y = {"dp": (quarter ^ 2) * stride + base}
    to_c = {"dp": (quarter ^ 1) * stride + base}
    greet(groups, z, [to_y, to_c])
    lag_b, lag_c, lag_z = lags
    last = groups - 1

    cuts = 8
    piece_rows = layer_rows.shape[0] // cuts

    def piece(ref, k):
        return ref.at[pl.ds(pl.multiple_of(k * piece_rows, piece_rows), piece_rows)]

    def spread(ref_in, ref_out, which, k, way, hop, arrival=False):
        step = 1 - 2 * way
        origin = z - (hop + 1 if arrival else hop) * step
        dst = piece(ref_out.at[origin], k)
        src = piece(ref_in, k) if hop == 0 and not arrival else dst
        return pltpu.make_async_remote_copy(
            src, dst, send_a.at[which, k, way, hop], recv_a.at[which, k, way, hop],
            device_id={"mp": z + step}, device_id_type=MESH)

    def spread_sends(way, hop):
        if way == 0:
            return jnp.logical_and(z >= hop, z < last)
        return jnp.logical_and(z <= last - hop, z > 0)

    def spread_arrives(way, hop):
        return z >= hop + 1 if way == 0 else z <= last - 1 - hop

    def spreading(ref_in, ref_out, which, k):
        for hop in range(groups):
            now = k - hop

            @pl.when(jnp.logical_and(now >= 0, now < cuts))
            def _():
                for way in range(2):
                    if hop:
                        @pl.when(spread_arrives(way, hop - 1))
                        def _():
                            spread(ref_in, ref_out, which, now, way, hop - 1, True).wait_recv()
                    if hop < last:
                        @pl.when(spread_sends(way, hop))
                        def _():
                            spread(ref_in, ref_out, which, now, way, hop).start()

    mine = [pltpu.make_async_copy(a, b.at[z], local.at[k])
            for k, (a, b) in enumerate(((layer_rows, layer_full), (hidden_rows, hidden_full)))]
    for item in mine:
        item.start()

    def run(count, width, lanes_of, far_from):
        size = width[0]
        other = width[1]

        def rows(i):
            return pl.ds(pl.multiple_of(i * chunk, chunk), chunk)

        def core_copy(i, k):
            return pltpu.make_async_remote_copy(
                grads.at[:, rows(i), pl.ds(pl.multiple_of(lanes_of(1 - core, k), 128), other)],
                from_core.at[i, k, :, :, pl.ds(0, other)],
                send_c.at[i, k], recv_c.at[i, k], device_id=to_c, device_id_type=MESH)

        def core_arrival(i, k):
            block = from_core.at[i, k, :, :, pl.ds(0, size)]
            return pltpu.make_async_remote_copy(
                block, block, send_c.at[i, k], recv_c.at[i, k],
                device_id=to_c, device_id_type=MESH)

        def own_load(i, k):
            return pltpu.make_async_copy(
                grads.at[:, rows(i), pl.ds(pl.multiple_of(lanes_of(core, k), 128), size)],
                own.at[lax.rem(i, 2), k, :, :, pl.ds(0, size)], own_sem.at[lax.rem(i, 2), k])

        def y_copy(i):
            return pltpu.make_async_remote_copy(
                from_core.at[i, 1 - y, :, :, pl.ds(0, size)],
                from_y.at[i, :, :, pl.ds(0, size)],
                send_y.at[i], recv_y.at[i], device_id=to_y, device_id_type=MESH)

        def z_copy(i, way, t):
            step = 1 - 2 * way
            first = z == (0 if way == 0 else last)
            dst = from_z.at[i, way, t, :, pl.ds(0, size)]

            def make(src):
                return pltpu.make_async_remote_copy(
                    src, dst, send_z.at[i, way, t], recv_z.at[i, way, t],
                    device_id={"mp": z + step}, device_id_type=MESH)

            return first, make(from_core.at[i, y, t, :, pl.ds(0, size)]), make(dst)

        def z_wait(i, way, t):
            z_copy(i, way, t)[2].wait_recv()

        def stage_a(i):
            for k in range(2):
                core_copy(i, k).start()
                own_load(i, k).start()

        def stage_b(i):
            for k in range(2):
                core_arrival(i, k).wait_recv()
                own_load(i, k).wait()
                from_core[i, k, :, :, :size] += own[lax.rem(i, 2), k, :, :, :size]
            y_copy(i).start()

        def z_step(i, hop):
            for way in range(2):
                step = 1 - 2 * way
                t = z + step * (groups - hop)
                inside = t <= last if way == 0 else t >= 0

                @pl.when(inside)
                def _():
                    first, fresh, passed = z_copy(i, way, t)
                    pl.when(first)(fresh.start)

                    @pl.when(jnp.logical_not(first))
                    def _():
                        passed.wait_recv()
                        from_z[i, way, t, :, :size] += from_core[i, y, t, :, :size]
                        passed.start()

        def stage_c(i):
            y_copy(i).wait_recv()
            from_core[i, y, :, :, :size] += from_y[i, :, :, :size]
            z_step(i, 1)

        def out_store(i):
            slot = lax.rem(i, 2)
            return pltpu.make_async_copy(
                staged.at[slot, :, pl.ds(0, size)], reduced.at[rows(i), pl.ds(0, size)],
                store_sem.at[slot])

        def far_copy(i):
            return pltpu.make_async_remote_copy(
                far.at[0, i], far.at[1, i], send_f.at[i], recv_f.at[i],
                device_id=to_y, device_id_type=MESH)

        def far_store(i):
            slot = lax.rem(i, 2)
            return pltpu.make_async_copy(
                staged.at[slot, :, pl.ds(size, size)],
                reduced.at[rows(i), pl.ds(size, size)], store_sem.at[2 + slot])

        def final(i):
            for way in range(2):
                @pl.when(z != (0 if way == 0 else last))
                def _():
                    z_wait(i, way, z)

            @pl.when(z == 0)
            def _():
                from_z[i, 0, z, :, :size] = jnp.zeros((chunk, size), low)

            @pl.when(z == last)
            def _():
                from_z[i, 1, z, :, :size] = jnp.zeros((chunk, size), low)

            total = (from_core[i, y, z, :, :size].astype(wide)
                     + from_z[i, 0, z, :, :size].astype(wide)
                     + from_z[i, 1, z, :, :size].astype(wide))

            def keep():
                pl.when(i >= 2)(lambda: out_store(i - 2).wait())
                staged[lax.rem(i, 2), :, :size] = total
                out_store(i).start()

            if far_from is None:
                keep()
            else:
                pl.when(y == 0)(keep)

                @pl.when(y == 1)
                def _():
                    far[0, i] = total.astype(low)
                    far_copy(i).start()

        def land(i):
            @pl.when(y == 0)
            def _():
                far_copy(i).wait_recv()
                pl.when(i >= 2)(lambda: far_store(i - 2).wait())
                staged[lax.rem(i, 2), :, size:] = far[1, i].astype(wide)
                far_store(i).start()

        def at(i, stage):
            pl.when(jnp.logical_and(i >= 0, i < count))(lambda: stage(i))

        end_lag = lag_c + lag_z * groups + (2 if far_from is not None else 0)

        @pl.loop(0, count + end_lag)
        def _(j):
            at(j, stage_a)
            at(j - lag_b, stage_b)
            at(j - lag_c, stage_c)
            for hop in range(2, groups):
                at(j - lag_c - lag_z * (hop - 1), partial(lambda h, i: z_step(i, h), hop))
            at(j - lag_c - lag_z * (groups - 1), final)
            if far_from is not None:
                at(j - end_lag + 1, land)
            spreading(layer_rows, layer_full, 0, j)
            spreading(hidden_rows, hidden_full, 1, j - cuts)

        @pl.loop(0, count)
        def _(i):
            for k in range(2):
                core_copy(i, k).wait_send()
            y_copy(i).wait_send()
            for way in range(2):
                for hop in range(1, groups):
                    t = z + (1 - 2 * way) * (groups - hop)

                    @pl.when(t <= last if way == 0 else t >= 0)
                    def _():
                        z_copy(i, way, t)[1].wait_send()
            if far_from is not None:
                pl.when(y == 1)(lambda: far_copy(i).wait_send())

        def drain(store):
            for i in (count - 2, count - 1):
                store(i).wait()

        if far_from is None:
            drain(out_store)
        else:
            @pl.when(y == 0)
            def _():
                drain(out_store)
                drain(far_store)

    text, image = settings
    pl.when(side == 1)(lambda: run(
        totals[1] // chunk, (TILE, TILE), lambda c, k: (2 * k + c) * TILE, None))

    def text_lanes(c, k):
        return jnp.where(c == 0, k * 2 * TILE, TILE + k * 128)

    is_text = side == 0
    pl.when(jnp.logical_and(is_text, core == 0))(lambda: run(
        totals[0] // chunk, (TILE, 128), text_lanes, None))
    pl.when(jnp.logical_and(is_text, core == 1))(lambda: run(
        totals[0] // chunk, (128, TILE), text_lanes, True))

    for which, (ref_in, ref_out) in enumerate(((layer_rows, layer_full), (hidden_rows, hidden_full))):
        @pl.loop(0, cuts)
        def _(k):
            for way in range(2):
                for hop in range(last):
                    @pl.when(spread_sends(way, hop))
                    def _():
                        spread(ref_in, ref_out, which, k, way, hop).wait_send()
    for item in mine:
        item.wait()


def shards(
    hidden,
    cotangent,
    segments,
    cross_in,
    cross_bias,
    cross_out,
    up_weight,
    up_bias,
    down_weight,
    attend_in,
    attend_bias,
    attend_out,
    out_bias,
    norm_gains,
    norm_shifts,
):
    groups = lax.axis_size("mp")
    copies = lax.axis_size("dp")
    stride = copies // 4
    side = lax.axis_index("stream")
    member = lax.axis_index("mp")
    copy = lax.axis_index("dp")
    is_image = side == 1
    inner = cross_in.shape[3]
    padded = hidden.shape[2]
    units = up_weight.shape[2]
    length = segments.shape[2]
    text = Setting(TEXT_WIDTH, TEXT_HEADS, TEXT_FF, groups)
    image = Setting(IMAGE_WIDTH, IMAGE_HEADS, IMAGE_FF, groups)
    settings = (text, image)
    layouts = [Layout(s, inner) for s in settings]
    totals = [layout.total + 3 * inner for layout in layouts]
    rows_max = max(totals)
    rows_dev = segments.shape[1] // groups
    tokens = hidden.shape[1] // groups

    def shape(dims, kind=low):
        return jax.ShapeDtypeStruct(dims, kind)

    def by_stream(piece, *operands):
        return lax.cond(
            is_image,
            lambda *a: piece(image, layouts[1], *a),
            lambda *a: piece(text, layouts[0], *a),
            *operands,
        )

    dma = pltpu.SemaphoreType.DMA
    weights = (
        jnp.swapaxes(cross_in[0], 0, 1),
        cross_out[0],
        up_weight[0],
        down_weight[0],
        jnp.swapaxes(attend_in[0], 0, 1),
        attend_out[0],
    )
    count = len(weights)
    full = pl.pallas_call(
        partial(gather_kernel, settings, groups, stride),
        out_shape=tuple(shape((groups,) + w.shape) for w in weights),
        in_specs=[ANY] * count,
        out_specs=(ANY,) * count,
        scratch_shapes=[dma((count, 2, groups - 1))] * 4
        + [dma((count, 2, groups - 1, 2))] * 2
        + [dma((count,))],
        compiler_params=pltpu.CompilerParams(collective_id=0, has_side_effects=True),
        name="gather",
    )(*weights)
    f_cross_in, f_cross_out, f_up, f_down, f_attend_in, f_attend_out = full

    cross_line = lax.all_gather(cross_bias[0], "mp")
    cross_line = cross_line.transpose(1, 0, 2).reshape(2, groups * inner).astype(wide)
    attend_line = lax.all_gather(attend_bias[0], "mp")
    attend_line = attend_line.transpose(1, 0, 2).reshape(2, groups * inner).astype(wide)
    up_line = lax.all_gather(up_bias[0], "mp").astype(wide)

    own = lax.dynamic_slice_in_dim(hidden[0], member * tokens, tokens, 0)
    grad_out = lax.dynamic_slice_in_dim(cotangent[0], member * tokens, tokens, 0)
    seg = lax.dynamic_slice_in_dim(segments, member * rows_dev, rows_dev, 1)
    seg_own = lax.dynamic_index_in_dim(seg, side, 0, keepdims=False)
    seg_other = lax.dynamic_index_in_dim(seg, 1 - side, 0, keepdims=False)
    cross_allowed = (seg_own[:, :, None] == seg_other[:, None, :]).astype(wide)
    self_allowed = (seg_own[:, :, None] == seg_own[:, None, :]).astype(wide)
    cross_allowed = cross_allowed.reshape(tokens, length)
    self_allowed = self_allowed.reshape(tokens, length)

    co = groups * inner
    square = shape((tokens, co))

    def project(s, layout, own, bias, f_cross_in):
        return pl.pallas_call(
            partial(project_kernel, s, groups),
            out_shape=(square,) * 3,
            in_specs=[VMEM, VMEM, ANY],
            out_specs=(VMEM,) * 3,
            scratch_shapes=[pltpu.VMEM((groups, 3, padded, inner), low), dma((groups,))],
            compiler_params=pltpu.CompilerParams(vmem_limit_bytes=VMEM_LIMIT),
            name="project",
        )(own, bias, f_cross_in)

    queries, keys, values = by_stream(project, own, cross_line, f_cross_in)

    def swap(block):
        return lax.ppermute(block, "stream", [(0, 1), (1, 0)])

    pair_keys, pair_values = swap(keys), swap(values)

    def middle(s, layout, *operands):
        w, u = s.width, s.units
        all_units = groups * u
        heads = groups * s.per_group
        tiles = groups * layout.total // TILE
        operands = operands[:7] + (operands[7][:, :u].reshape(1, all_units),) + operands[8:]

        def real(*dims):
            return pltpu.VMEM(dims, wide)

        def half_size(*dims):
            return pltpu.VMEM(dims, low)

        out = pl.pallas_call(
            partial(middle_kernel, s, layout, groups, length),
            out_shape=(
                shape((tokens, padded)), shape((tokens, padded), wide), square, square, square,
                shape((groups, rows_max, padded)), shape((16, padded), wide),
                shape((1, all_units), wide), shape((2, co), wide),
            ),
            in_specs=[VMEM] * 12 + [ANY] * 5,
            out_specs=(VMEM,) * 5 + (ANY,) + (VMEM,) * 3,
            scratch_shapes=[
                half_size(co, w), half_size(groups, w, u), half_size(all_units, w),
                half_size(groups, 3, w, inner), half_size(co, w), half_size(tiles, TILE, w),
                half_size(tokens, co), real(CO_HEADS * rows_dev, length, length),
                real(tokens, w), real(tokens, w), real(tokens, w), real(tokens, w),
                real(tokens, 1), real(tokens, 1), real(tokens, 1),
                half_size(tokens, w), half_size(tokens, w),
                real(tokens, all_units), half_size(tokens, all_units),
                half_size(tokens, co), half_size(tokens, co), half_size(tokens, co),
                real(heads * rows_dev, length, length), half_size(tokens, co),
                half_size(tokens, w), half_size(tokens, co),
                half_size(tokens, co), half_size(tokens, co), half_size(tokens, co),
                half_size(tokens, all_units),
                dma((5 * groups,)), dma((tiles,)),
            ],
            compiler_params=pltpu.CompilerParams(vmem_limit_bytes=VMEM_LIMIT),
            name="middle",
        )(*operands)
        up_sums = out[7].reshape(groups, u)
        return out[:7] + (jnp.pad(up_sums, ((0, 0), (0, units - u))), out[8])

    layer_rows, entry, dq, pair_dk, pair_dv, grads, vectors, up_sums, attend_sums = by_stream(
        middle, own, grad_out, queries, pair_keys, pair_values, cross_allowed, self_allowed,
        up_line, attend_line, out_bias[0].astype(wide), norm_gains[0].astype(wide),
        norm_shifts[0].astype(wide), f_cross_out, f_up, f_down, f_attend_in, f_attend_out)
    dk, dv = swap(pair_dk), swap(pair_dv)

    def finish(s, layout, own, entry, dq, dk, dv, f_cross_in, grads):
        def kernel(x, e, a, b, c, f, g_in, hidden_grad, g, sums, *scratch):
            finish_kernel(s, groups, x, e, a, b, c, f, hidden_grad,
                          g.at[:, pl.ds(layout.total, 3 * inner)], sums, *scratch)

        return pl.pallas_call(
            kernel,
            out_shape=(shape((tokens, padded)), shape(grads.shape), shape((2, co), wide)),
            in_specs=[VMEM] * 5 + [ANY] * 2,
            out_specs=(VMEM, ANY, VMEM),
            scratch_shapes=[
                pltpu.VMEM((groups, 3, padded, inner), low),
                pltpu.VMEM((3 * groups, inner, s.width), low),
                dma((groups,)), dma((3 * groups,)),
            ],
            input_output_aliases={6: 1},
            compiler_params=pltpu.CompilerParams(vmem_limit_bytes=VMEM_LIMIT),
            name="finish",
        )(own, entry, dq, dk, dv, f_cross_in, grads)

    hidden_rows, grads, cross_sums = by_stream(
        finish, own, entry, dq, dk, dv, f_cross_in, grads)

    chunk = 128
    most = rows_max // chunk
    cuts = 8
    line = (groups, tokens, padded)
    reduced, layer_out, hidden_grad = pl.pallas_call(
        partial(reduce_kernel, settings, totals, groups, stride, chunk, (1, 3, 1)),
        out_shape=(shape((rows_max, TILE), wide), shape(line), shape(line)),
        in_specs=[ANY] * 3,
        out_specs=(ANY,) * 3,
        scratch_shapes=[
            pltpu.VMEM((most, 2, groups, chunk, TILE), low),
            pltpu.VMEM((most, groups, chunk, TILE), low),
            pltpu.VMEM((most, 2, groups, chunk, TILE), low),
            pltpu.VMEM((2, most, chunk, 128), low),
            pltpu.VMEM((2, 2, groups, chunk, TILE), low),
            pltpu.VMEM((2, chunk, TILE), wide),
            dma((most, 2)), dma((most, 2)), dma((most,)), dma((most,)),
            dma((most, 2, groups)), dma((most, 2, groups)), dma((most,)), dma((most,)),
            dma((2, 2)), dma((4,)),
            dma((2, cuts, 2, groups - 1)), dma((2, cuts, 2, groups - 1)), dma((2,)),
        ],
        compiler_params=pltpu.CompilerParams(
            collective_id=1, has_side_effects=True, vmem_limit_bytes=VMEM_LIMIT),
        name="reduce",
    )(grads, layer_rows, hidden_rows)

    if stride > 1:
        teams = [[q * stride + b for b in range(stride)] for q in range(4)]
        reduced = lax.psum_scatter(
            reduced.astype(low), "dp", scatter_dimension=1, axis_index_groups=teams, tiled=True
        ).astype(wide)
    columns = padded // copies
    real_block = copy * columns < jnp.where(is_image, IMAGE_WIDTH, TEXT_WIDTH)
    reduced = jnp.where(real_block, reduced, 0.0)

    def spread_rows(total, parts, width):
        return total.reshape(total.shape[:-1] + (groups, copies, width // copies))

    flat = jnp.concatenate([
        jnp.moveaxis(cross_sums.reshape(2, groups, copies, inner // copies), 0, 2).reshape(
            groups, copies, -1),
        jnp.moveaxis(attend_sums.reshape(2, groups, copies, inner // copies), 0, 2).reshape(
            groups, copies, -1),
        up_sums.reshape(groups, copies, units // copies),
        jnp.broadcast_to(
            jnp.moveaxis(vectors[:9].reshape(9, copies, columns), 0, 1).reshape(
                1, copies, 9 * columns), (groups, copies, 9 * columns)),
    ], axis=2)
    small = lax.psum_scatter(
        flat.reshape(groups * copies, -1), ("mp", "dp"), scatter_dimension=0, tiled=True)[0]
    part = inner // copies
    cross_bias_grad = small[: 2 * part].reshape(2, part)
    attend_bias_grad = small[2 * part : 4 * part].reshape(2, part)
    up_bias_grad = small[4 * part : 4 * part + units // copies]
    vector_grads = small[4 * part + units // copies :].reshape(9, columns)

    def unpack(s, layout, reduced):
        u = s.units

        def turned(start):
            block = reduced[start : start + 3 * inner].reshape(3, inner, columns)
            return block.transpose(2, 0, 1)

        return (
            turned(layout.total),
            reduced[layout.cross_out : layout.cross_out + inner],
            jnp.pad(reduced[layout.up : layout.up + u].T, ((0, 0), (0, units - u))),
            jnp.pad(reduced[layout.down : layout.down + u], ((0, units - u), (0, 0))),
            turned(layout.attend_in),
            reduced[layout.attend_out : layout.attend_out + inner],
        )

    g_cross_in, g_cross_out, g_up, g_down, g_attend_in, g_attend_out = by_stream(unpack, reduced)
    return (
        layer_out.reshape(1, groups * tokens, padded),
        hidden_grad.reshape(1, groups * tokens, padded),
        g_cross_in[None],
        cross_bias_grad[None],
        g_cross_out[None],
        g_up[None],
        up_bias_grad[None],
        g_down[None],
        g_attend_in[None],
        attend_bias_grad[None],
        g_attend_out[None],
        vector_grads[None, 0:3],
        vector_grads[None, 3:6],
        vector_grads[None, 6:9],
    )


def solution(mesh):
    placed = (
        P("stream", "dp", None),
        P("stream", "dp", None),
        P(None, "dp", None),
        P("stream", None, None, "mp"),
        P("stream", None, "mp"),
        P("stream", "mp", None),
        P("stream", None, "mp"),
        P("stream", "mp"),
        P("stream", "mp", None),
        P("stream", None, None, "mp"),
        P("stream", None, "mp"),
        P("stream", "mp", None),
        P("stream", None, None),
        P("stream", None, None),
        P("stream", None, None),
    )
    return jax.shard_map(
        shards,
        mesh=mesh,
        in_specs=placed,
        out_specs=(
            P("stream", "dp", None),
            P("stream", "dp", None),
            P("stream", "dp", None, "mp"),
            P("stream", None, ("mp", "dp")),
            P("stream", "mp", "dp"),
            P("stream", "dp", "mp"),
            P("stream", ("mp", "dp")),
            P("stream", "mp", "dp"),
            P("stream", "dp", None, "mp"),
            P("stream", None, ("mp", "dp")),
            P("stream", "mp", "dp"),
            P("stream", None, "dp"),
            P("stream", None, "dp"),
            P("stream", None, "dp"),
        ),
        check_vma=False,
    )
```

time: 1380 us -> 523 us (0.38)
  waiting for transfers between devices: 1080 us -> 21.6 us
  Pallas kernels: 0 us -> 402 us
  local copies, waits for them, and re-layouts: 110 us -> 26.2 us
  other arithmetic: 81.8 us -> 4.99 us
  matrix products: 62.2 us -> 0 us
  blocking collectives: 0 us -> 33.9 us
    psum x6 -> x0, waiting for transfers between devices: 724 us -> none  [the longest x3 469 us: across_heads(): return lax.psum(partial_out, 'mp')]
    pallas_call x0 -> x5, Pallas kernels: none -> 402 us  [the longest x1 172 us: shards(): pl.pallas_call(partial(gather_kernel, settings, groups, stride), out_shap...]
    unnamed x36 -> x2, waiting for transfers between devices: 170 us -> 0.02 us
    reduce_scatter x6 -> x0, waiting for transfers between devices: 154 us -> none  [the longest x1 29.9 us: shards(): lax.psum_scatter(attend_in_term.astype(jnp.bfloat16), 'dp', scatter_dimen...]
    dot_general x31 -> x0, matrix products: 62.2 us -> none  [the longest x1 9.51 us: feed_inner(): jnp.dot(activated, down_weight[0, :hidden_dev, :width_real], preferred_el...]
    reduce_sum x24 -> x0, other arithmetic: 35.3 us -> none  [the longest x6 17.3 us: normalize(): row_mean = jnp.mean(value_in, axis=-1, keepdims=True)]
    all_gather x0 -> x3, blocking collectives: none -> 33.9 us  [the longest x1 13 us: shards(): up_line = lax.all_gather(up_bias[0], 'mp').astype(wide)]
    pad x30 -> x0, local copies, waits for them, and re-layouts: 33.7 us -> none  [widen(): jnp.pad(value_in, [(0, want_size - have_size) for have_size, want_size in...]
  transfers between devices with their start and end apart: 28 -> 5, of which waited for: 24 -> 3; matrix products, arithmetic and copies ran while one was open for 8% -> 2% of each run, Pallas kernels for 0% -> 31%
where the time goes in v1:
time: 523 us; the launch traced here: 516 us
  Pallas kernels  402 us (77%)
  blocking collectives  33.9 us (6%)
  local copies, waits for them, and re-layouts  26.2 us (5%)
  waiting for transfers between devices  21.6 us (4%)
  between operations  14.4 us (3%)
  loops' own time  8.57 us (2%)
    pallas_call x1, Pallas kernels, shards(): pl.pallas_call(partial(gather_kernel, settings, groups, stride), out_shap...  172 us
    pallas_call x1, Pallas kernels, shards(): pl.pallas_call(partial(reduce_kernel, settings, totals, groups, stride, c...  162 us
    pallas_call x1, Pallas kernels, middle(): pl.pallas_call(partial(middle_kernel, s, layout, groups, length), out_sha...  55.6 us
    ppermute x4, waiting for transfers between devices, swap(): return lax.ppermute(block, 'stream', [(0, 1), (1, 0)])  21.6 us
    all_gather x1, blocking collectives, shards(): up_line = lax.all_gather(up_bias[0], 'mp').astype(wide)  13 us
    all_gather x1, blocking collectives, shards(): cross_line = lax.all_gather(cross_bias[0], 'mp')  12.8 us
  transfers between devices with their start and end apart: 5, of which 3 were waited for; matrix products, arithmetic and copies ran while one was open for 2% of the time, Pallas kernels for 31%

profile of v1, /device:TPU:0, one launch (start us, length us, event | category | flops | bytes accessed | tf_op | source)
XLA Modules:
  0.0 516.1 jit_solution(8258874909584700041)
XLA Ops:
  7.2 0.0 all-reduce.6.cloned.1.call-start
  7.2 12.8 %all_gather.11 = bf16[4,2,256]{2,1,0:T(2,128)(2,1)S(1)} all-gather(bf16[1,2,256]{2,1,0:T(2,128)(2,1)} %param.27), channel_id=1, replica_groups=mesh['stream'=2,'mp'=4,'dp'=4] {'mp'}, dimensions={0}, use_global_device_ids=true | all-gather | bytes 5120 | tf_op jit(solution)/shard_map/all_gather | solution.py:946
  20.1 1.1 dynamic-slice_bitcast_fusion.2
  21.2 172.1 %gather.1 = (bf16[4,3,1024,256]{3,2,1,0:T(8,128)(2,1)}, bf16[4,256,1024]{2,1,0:T(8,128)(2,1)}, bf16[4,1024,768]{2,1,0:T(8,128)(2,1)}, bf16[4,768,1024]{2,1,0:T(8...) custom-call(bf16[3,1024,256]{2,1,0:T(8,128)(2,1)} %bitcast.131, ...), custom_call_target="tpu_custom_call" | custom-call | tf_op jit(solution)/shard_map/gather/pallas_call | solution.py:933
  193.2 0.0 copy-start.7
  193.3 0.0 copy-start.8
  193.3 0.0 copy-start.4
  193.3 0.0 copy-start.5
  193.3 0.0 copy-start.6
  193.3 4.6 conditional.4
  193.3 4.5 project.2
  197.9 0.1 collective-permute-start
  198.0 2.0 collective-permute-start.1
  200.0 0.0 copy-done.7
  200.0 13.0 %all-gather = bf16[4,1,768]{2,1,0:T(2,128)(2,1)S(1)} all-gather(bf16[1,1,768]{2,1,0:T(2,128)(2,1)S(1)} %bitcast.155), channel_id=1, replica_groups=mesh['stream'=2,'mp'=4,'dp'=4] {'mp'}, dimensions={0}, use_global_device_ids=true | all-gather | bytes 7680 | tf_op jit(solution)/shard_map/all_gather | solution.py:950
  213.0 0.7 fusion.2
  213.7 0.1 fusion.1
  213.8 0.0 copy-done.8
  213.8 8.0 %all_gather.10 = bf16[4,2,256]{2,1,0:T(2,128)(2,1)S(1)} all-gather(bf16[1,2,256]{2,1,0:T(2,128)(2,1)S(1)} %copy-done.8), channel_id=1, replica_groups=mesh['stream'=2,'mp'=4,'dp'=4] {'mp'}, dimensions={0}, use_global_device_ids=true | all-gather | bytes 5120 | tf_op jit(solution)/shard_map/all_gather | solution.py:948
  221.8 0.0 collective-permute-done
  221.8 0.5 collective-permute-done.1
  222.3 0.0 copy-done.4
  222.3 70.3 %conditional.5 = (bf16[256,1024]{1,0:T(8,128)(2,1)}, f32[256,1024]{1,0:T(8,128)}, bf16[256,1024]{1,0:T(8,128)(2,1)}, bf16[256,1024]{1,0:T(8,128)(2,1)}, bf16[256...) conditional(s32[]{:T(128)} %convert_element_type.92, ...), branch_computations={%region_2.3_spmd, %region_3.4_spmd} | conditional | flops 11264 | bytes 1206364 | solution.py:916
  222.3 0.6 bitcast_convert_fusion
  223.0 2.0 dynamic-slice_bitcast_fusion.grad_out
  224.9 0.6 copy.65
  225.5 0.6 bitcast_convert_fusion.2.out_bias
  226.1 0.6 copy.64
  226.8 55.6 %middle.4 = (bf16[256,1024]{1,0:T(8,128)(2,1)}, f32[256,1024]{1,0:T(8,128)}, bf16[256,1024]{1,0:T(8,128)(2,1)}, bf16[256,1024]{1,0:T(8,128)(2,1)}, bf16[256,1024...) custom-call(bf16[256,1024]{1,0:T(8,128)(2,1)S(1)} %get-tuple-element, ...), custom_call_target="tpu_custom_call" | custom-call | tf_op jit(solution)/shard_map/cond/branch_0_fun/middle/pallas_call | solution.py:996
  282.4 0.5 broadcast.22
  282.9 1.4 reduce.15
  284.3 0.1 concatenate.4
  292.6 0.1 collective-permute-start.2
  292.7 2.0 collective-permute-start.3
  294.8 0.1 concatenate.16
  294.9 0.1 reshape.150
  295.0 0.1 concatenate.15
  295.0 12.7 %collective-permute-done.2 = bf16[256,1024]{1,0:T(8,128)(2,1)S(1)} collective-permute-done((bf16[256,1024]{1,0:T(8,128)(2,1)}, bf16[256,1024]{1,0:T(8,128)(2,1)S(1)}, u32[]{:S(2)}, u32[]{:S(2)}) %collective-permute-start.2) | collective-permute-done | bytes 524320 | tf_op jit(solution)/shard_map/ppermute | solution.py:979
  307.8 8.4 %collective-permute-done.3 = bf16[256,1024]{1,0:T(8,128)(2,1)} collective-permute-done((bf16[256,1024]{1,0:T(8,128)(2,1)}, bf16[256,1024]{1,0:T(8,128)(2,1)}, u32[]{:S(2)}, u32[]{:S(2)}) %collective-permute-start.3) | collective-permute-done | bytes 524320 | tf_op jit(solution)/shard_map/ppermute | solution.py:979
  316.2 8.3 %conditional.6 = ((bf16[256,1024]{1,0:T(8,128)(2,1)}, bf16[4,3584,1024]{2,1,0:T(8,128)(2,1)}, f32[2,1024]{1,0:T(2,128)S(1)})) conditional(s32[]{:T(128)} %convert_element_type.92, (bf16[256,1024]{1,0:T(8,128)(2,1)S(1)}, f32[256,1024]{1,0:T(8,128)}, bf16[256,1024]{1,0:T(8,128)(2,1)}, bf16[256,1024]{1,0:T(8,128)(2,1)S(1)}, bf16[256,1024]{1,0:T(8,128)(2,1)}, ...), branch_computations={%region_4.5_spmd, %region_5.6_spmd} | conditional | bytes 8 | solution.py:916
  316.2 8.2 %finish.2 = (bf16[256,1024]{1,0:T(8,128)(2,1)}, bf16[4,3584,1024]{2,1,0:T(8,128)(2,1)}, f32[2,1024]{1,0:T(2,128)S(1)}) custom-call(bf16[256,1024]{1,0:T(8,128)(2,1)S(1)} %get-tuple-element.303.x, f32[256,1024]{1,0:T(8,128)} %get-tuple-element.304.e, bf16[256,1024]{1,0:T(8,128)(2,1)} %get-tuple-element.305.a, ...), custom_call_target="tpu_custom_call", output_to_operand_aliasing={{1}: (6, {})} | custom-call | tf_op jit(solution)/shard_map/cond/branch_0_fun/finish/pallas_call | solution.py:1037
  324.4 0.1 reshape.149
  324.5 0.1 concatenate.14
  324.6 0.8 concatenate.17
  325.4 0.0 all-reduce.6.cloned.1.call-update
  325.4 0.6 dynamic-slice.8
  326.0 161.7 %reduce.17 = (f32[3584,256]{1,0:T(8,128)}, bf16[4,256,1024]{2,1,0:T(8,128)(2,1)}, bf16[4,256,1024]{2,1,0:T(8,128)(2,1)}) custom-call(bf16[4,3584,1024]{2,1,0:T(8,128)(2,1)} %get-tuple-element.381.grads, bf16[256,1024]{1,0:T(8,128)(2,1)} %get-tuple-element.382.layer_rows, bf16[256,1024]{1,0:T(8,128)(2,1)} %get-tuple-element.383.hidden_rows), custom_call_target="tpu_custom_call" | custom-call | tf_op jit(solution)/shard_map/reduce/pallas_call | solution.py:1059
  487.7 9.8 %conditional.7 = (f32[1,256,256]{2,1,0:T(8,128)}, f32[1,768,256]{2,1,0:T(8,128)}, f32[1,256,256]{2,1,0:T(8,128)}, f32[1,256,3,256]{3,1,2,0:T(8,128)}, f32[1,256,...) conditional(s32[]{:T(128)} %convert_element_type.92, (s32[]{:T(128)}, pred[]{:T(512)}, ...), branch_computations={%region_6.7_spmd, %region_7.8_spmd} | conditional | flops 917507 | bytes 34078832 | solution.py:916
  487.9 2.3 broadcast_select_fusion
  490.2 0.0 copy-start
  490.2 1.8 copy-done
  492.0 1.1 fusion.4
  493.0 1.1 copy.57
  494.2 0.3 copy.59
  494.5 1.1 copy.61
  495.6 1.9 slice_bitcast_fusion.2
  497.5 1.7 dynamic-slice_reduce_fusion
  499.2 0.6 broadcast_in_dim_reshape.6
  499.8 0.6 broadcast_in_dim_reshape.7
  500.5 2.0 dynamic-slice.11
  502.5 2.2 fusion.6
  504.6 3.1 copy.123
  507.7 0.0 copy-done.2
  507.7 1.3 copy.124
  (15 shorter events, 0.1 us)
Async XLA Ops:
  7.2 490.3 %all-reduce.6.cloned.1.call-start = ((), (), s32[]{:S(2)}) async-start(), calls=%async_computation | async-start | bytes 360448
  193.2 6.7 %copy-start.7 = (bf16[1,768]{1,0:T(2,128)(2,1)S(1)}, bf16[1,768]{1,0:T(2,128)(2,1)}, u32[]{:S(2)}) copy-start(bf16[1,768]{1,0:T(2,128)(2,1)} %param.30) | copy-start | bytes 4612
  193.3 20.6 %copy-start.8 = (bf16[1,2,256]{2,1,0:T(2,128)(2,1)S(1)}, bf16[1,2,256]{2,1,0:T(2,128)(2,1)}, u32[]{:S(2)}) copy-start(bf16[1,2,256]{2,1,0:T(2,128)(2,1)} %param.33) | copy-start | bytes 3076
  193.3 29.1 %copy-start.4 = (bf16[1,3,1024]{2,1,0:T(4,128)(2,1)S(1)}, bf16[1,3,1024]{2,1,0:T(4,128)(2,1)}, u32[]{:S(2)}) copy-start(bf16[1,3,1024]{2,1,0:T(4,128)(2,1)} %param.35) | copy-start | bytes 18436
  193.3 29.0 %copy-start.5 = (bf16[1,3,1024]{2,1,0:T(4,128)(2,1)S(1)}, bf16[1,3,1024]{2,1,0:T(4,128)(2,1)}, u32[]{:S(2)}) copy-start(bf16[1,3,1024]{2,1,0:T(4,128)(2,1)} %param.36) | copy-start | bytes 18436
  193.3 29.0 %copy-start.6 = (bf16[1,3,1024]{2,1,0:T(4,128)(2,1)S(1)}, bf16[1,3,1024]{2,1,0:T(4,128)(2,1)}, u32[]{:S(2)}) copy-start(bf16[1,3,1024]{2,1,0:T(4,128)(2,1)} %param.37) | copy-start | bytes 18436
  197.9 23.9 %collective-permute-start = (bf16[256,1024]{1,0:T(8,128)(2,1)}, bf16[256,1024]{1,0:T(8,128)(2,1)S(1)}, u32[]{:S(2)}, u32[]{:S(2)}) collective-permute-start(bf16[256,1024]{1,0:T(8,128)(2,1)} %get-tuple-element.369), channel_id=1, source_target_pairs={{0,16},{16,0},{1,17},{17,1},{2,18},{18,2},{3,19},{19,3},{4,20},{20... | collective-permute-start | bytes 1572872 | tf_op jit(solution)/shard_map/ppermute | solution.py:979
  198.0 24.4 %collective-permute-start.1 = (bf16[256,1024]{1,0:T(8,128)(2,1)}, bf16[256,1024]{1,0:T(8,128)(2,1)}, u32[]{:S(2)}, u32[]{:S(2)}) collective-permute-start(bf16[256,1024]{1,0:T(8,128)(2,1)} %get-tuple-element.370), channel_id=1, source_target_pairs={{0,16},{16,0},{1,17},{17,1},{2,18},{18,2},{3,19},{19,3},{4,20},{20... | collective-permute-start | bytes 1572872 | tf_op jit(solution)/shard_map/ppermute | solution.py:979
  292.6 15.1 %collective-permute-start.2 = (bf16[256,1024]{1,0:T(8,128)(2,1)}, bf16[256,1024]{1,0:T(8,128)(2,1)S(1)}, u32[]{:S(2)}, u32[]{:S(2)}) collective-permute-start(bf16[256,1024]{1,0:T(8,128)(2,1)} %get-tuple-element.378), channel_id=1, source_target_pairs={{0,16},{16,0},{1,17},{17,1},{2,18},{18,2},{3,19},{19,3},{4,20},{20... | collective-permute-start | bytes 1572872 | tf_op jit(solution)/shard_map/ppermute | solution.py:979
  292.7 23.4 %collective-permute-start.3 = (bf16[256,1024]{1,0:T(8,128)(2,1)}, bf16[256,1024]{1,0:T(8,128)(2,1)}, u32[]{:S(2)}, u32[]{:S(2)}) collective-permute-start(bf16[256,1024]{1,0:T(8,128)(2,1)} %get-tuple-element.379), channel_id=1, source_target_pairs={{0,16},{16,0},{1,17},{17,1},{2,18},{18,2},{3,19},{19,3},{4,20},{20... | collective-permute-start | bytes 1572872 | tf_op jit(solution)/shard_map/ppermute | solution.py:979
  316.2 9.3 %copy-start.9 = (u32[32]{0:T(128)S(1)}, u32[32]{0:T(128)}, u32[]{:S(2)}) copy-start(u32[32]{0:T(128)} %constant.121) | copy-start | bytes 388
  490.2 1.8 copy-start
  497.5 11.6 %copy-start.3 = (f32[1,256,768]{2,1,0:T(8,128)}, f32[1,256,768]{2,1,0:T(8,128)S(1)}, u32[]{:S(2)}) copy-start(f32[1,256,768]{2,1,0:T(8,128)S(1)} %get-tuple-element.601) | copy-start | bytes 2359300
  497.5 10.2 %copy-start.2 = (bf16[4,256,1024]{2,1,0:T(8,128)(2,1)S(1)}, bf16[4,256,1024]{2,1,0:T(8,128)(2,1)}, u32[]{:S(2)}) copy-start(bf16[4,256,1024]{2,1,0:T(8,128)(2,1)} %get-tuple-element.385) | copy-start | bytes 6291460
Sparse Core Ops, SparseCore 0:
  325.5 88.7 all-reduce.5

commit v2 on v0

v2 whole, which is shorter than its diff:
```python
import math
from functools import partial
from typing import Any, NamedTuple

import jax
import jax.numpy as jnp
from jax import lax
from jax.experimental import pallas as pl
from jax.experimental.pallas import tpu as pltpu
from jax.sharding import PartitionSpec as P

TEXT_WIDTH = 768
TEXT_HEADS = 12
TEXT_FF = 3072
IMAGE_WIDTH = 1024
IMAGE_HEADS = 8
IMAGE_FF = 1024
CO_HEADS = 8

norm_eps = 1e-12
masked_score = -1000000000.0
low = jnp.bfloat16
wide = jnp.float32
ANY = pl.BlockSpec(memory_space=pl.ANY)
VMEM = pl.BlockSpec(memory_space=pltpu.VMEM)
MESH = pl.DeviceIdType.MESH
VMEM_LIMIT = 65400 * 1024
TILE = 256


def dot(left, right):
    return jnp.dot(left, right, preferred_element_type=wide)


def dot_nt(left, right):
    return lax.dot_general(left, right, (((1,), (1,)), ((), ())), preferred_element_type=wide)


def dot_tn(left, right):
    return lax.dot_general(left, right, (((0,), (0,)), ((), ())), preferred_element_type=wide)


class Setting:
    def __init__(self, width, count, units, groups):
        self.width = width
        self.head = width // count
        self.units = units // groups
        self.lanes = width // groups
        self.parts = width // TILE
        self.per_group = count // groups


class Layout:
    def __init__(self, s, inner):
        self.attend_out = 0
        self.attend_in = inner
        self.down = 4 * inner
        self.up = 4 * inner + s.units
        self.cross_out = 4 * inner + 2 * s.units
        self.total = 5 * inner + 2 * s.units


def lane(start, size=TILE):
    return pl.ds(pl.multiple_of(start, 128), size)


def norm_back(normal, inverse, gain, incoming, w):
    scaled = incoming * gain
    first = jnp.sum(scaled, axis=-1, keepdims=True) * (1.0 / w)
    second = jnp.sum(scaled * normal, axis=-1, keepdims=True) * (1.0 / w)
    return inverse * (scaled - first - normal * second)


def down_sum(value):
    return jnp.sum(value, axis=0, keepdims=True)


def softmax_t(scores, allowed, scale):
    scores = jnp.where(allowed, scores, masked_score / scale)
    top = jnp.max(scores, axis=0, keepdims=True)
    exponent = jnp.exp2((scores - top) * (scale * math.log2(math.e)))
    return exponent * (1.0 / jnp.sum(exponent, axis=0, keepdims=True))


def score_grad_t(p, grad):
    return (p * (grad - jnp.sum(grad * p, axis=0, keepdims=True))).astype(low)


def halves(value):
    index = lax.broadcasted_iota(jnp.int32, value.shape, 1)
    zero = jnp.zeros_like(value)
    return jnp.concatenate(
        [jnp.where(index < 64, value, zero), jnp.where(index >= 64, value, zero)], axis=0)


def lower(value):
    index = lax.broadcasted_iota(jnp.int32, value.shape, 1)
    return jnp.where(index < 64, value, jnp.zeros_like(value))


def side_by_side(parts, axis=1):
    return parts[0] if len(parts) == 1 else jnp.concatenate(parts, axis=axis)


def split(value, count):
    size = value.shape[1] // count
    return [value[:, n * size : (n + 1) * size] for n in range(count)]


def block_kinds(head, heads):
    if head == 128:
        return [0] * heads
    return [2] * (heads // 2) + [1] * (heads % 2)


def spread_heads(kind, value):
    return halves(value) if kind == 2 else lower(value) if kind == 1 else value


def attend_forward(group, kinds, scale, length, rows, q, k, v, allowed, prob, context):
    heads = sum(max(kind, 1) for kind in kinds)
    base = group * len(kinds) * 128
    ats = [slice(r * length, (r + 1) * length) for r in range(rows)]
    step = 0
    for b, kind in enumerate(kinds):
        cols = lane(base + b * 128, 128)
        count = max(kind, 1)
        groups = [ats]
        for members in groups:
            scores = side_by_side(
                [dot_nt(k[at, cols], spread_heads(kind, q[at, cols])) for at in members])
            masks = side_by_side([allowed[at, :] for at in members for _ in range(count)])
            p = softmax_t(scores, masks > 0, scale)
            low_p = p.astype(low)
            tiles = split(p, count * len(members))
            low_tiles = split(low_p, count * len(members))
            out = [
                dot_tn(side_by_side(low_tiles[n * count : (n + 1) * count], 0),
                       spread_heads(kind, v[at, cols]))
                for n, at in enumerate(members)]
            for n, at in enumerate(members):
                r = ats.index(at)
                context[at, cols] = out[n].astype(low)
                for c in range(count):
                    prob[group * heads * rows + r * heads + step + c] = tiles[n * count + c]
        step += count


def attend_backward(group, kinds, scale, length, rows, q, k, v, prob, grad, dq, dk, dv):
    heads = sum(max(kind, 1) for kind in kinds)
    base = group * len(kinds) * 128
    ats = [slice(r * length, (r + 1) * length) for r in range(rows)]
    step = 0
    for b, kind in enumerate(kinds):
        cols = lane(base + b * 128, 128)
        count = max(kind, 1)
        groups = [ats]
        for members in groups:
            dcs = [spread_heads(kind, grad[at, cols]) for at in members]
            qs = [spread_heads(kind, q[at, cols]) for at in members]
            gp = side_by_side([dot_nt(v[at, cols], dc) for at, dc in zip(members, dcs)])
            p = side_by_side([
                prob[group * heads * rows + ats.index(at) * heads + step + c]
                for at in members for c in range(count)])
            low_p = split(p.astype(low), len(members))
            ds = split(score_grad_t(p, gp), len(members))
            grad_v = [dot(a, dc) for a, dc in zip(low_p, dcs)]
            grad_k = [dot(a, two) * scale for a, two in zip(ds, qs)]
            grad_q = [dot_tn(a, k[at, cols]) * scale for a, at in zip(ds, members)]
            for n, at in enumerate(members):
                value = grad_q[n]
                if kind:
                    index = lax.broadcasted_iota(jnp.int32, (length, 128), 1)
                    other = value[length:] if kind == 2 else jnp.zeros((length, 128), wide)
                    value = jnp.where(index < 64, value[:length], other)
                dq[at, cols] = value.astype(low)
                dk[at, cols] = grad_k[n].astype(low)
                dv[at, cols] = grad_v[n].astype(low)
        step += count
class Refs:
    def __init__(self, *groups):
        for group in groups:
            self.__dict__.update(group._asdict())


class Inputs(NamedTuple):
    cross_in: Any
    cross_out: Any
    up: Any
    down: Any
    attend_in: Any
    attend_out: Any
    hidden: Any
    cotangent: Any
    cross_bias: Any
    attend_bias: Any
    up_bias: Any
    out_bias: Any
    gains: Any
    shifts: Any
    cross_allowed: Any
    self_allowed: Any


class Results(NamedTuple):
    layer_full: Any
    hidden_full: Any
    reduced: Any
    small_out: Any
    f_cross_in: Any
    f_cross_out: Any
    f_up: Any
    f_down: Any
    f_attend_in: Any
    f_attend_out: Any
    grads: Any


class Scratch(NamedTuple):
    w_in: Any
    w_cross_out: Any
    w_attend_out: Any
    w_up: Any
    w_down: Any
    x: Any
    grad_out: Any
    q: Any
    k: Any
    v: Any
    pair_k: Any
    pair_v: Any
    back_k: Any
    back_v: Any
    cross_prob: Any
    self_prob: Any
    context: Any
    context2: Any
    acc: Any
    n1: Any
    n2: Any
    n3: Any
    r1: Any
    r2: Any
    r3: Any
    h1: Any
    h2: Any
    slope: Any
    active: Any
    dz: Any
    q2: Any
    k2: Any
    v2: Any
    d1: Any
    d2: Any
    d3: Any
    low_grad: Any
    grad_context: Any
    layer_rows: Any
    hidden_rows: Any
    zero: Any
    staged: Any
    from_core: Any
    from_y: Any
    from_z: Any
    far: Any
    own: Any
    staged_out: Any
    small_in: Any
    small_got: Any
    small_sum: Any
    small_sem: Any
    a_cross_bias: Any
    a_attend_bias: Any
    a_up_bias: Any
    send_gz: Any
    recv_gz: Any
    send_gy: Any
    recv_gy: Any
    send_gc: Any
    recv_gc: Any
    weight_sem: Any
    enter_sem: Any
    send_b: Any
    recv_b: Any
    send_x: Any
    recv_x: Any
    store_sem: Any
    send_c: Any
    recv_c: Any
    send_y: Any
    recv_y: Any
    send_z: Any
    recv_z: Any
    send_f: Any
    recv_f: Any
    own_sem: Any
    out_sem: Any
    send_a: Any
    recv_a: Any
    local_sem: Any
    send_s: Any
    recv_s: Any
    free: Any


class Plan(NamedTuple):
    groups: Any
    copies: Any
    inner: Any
    length: Any
    rows: Any
    tokens: Any
    units: Any
    chunk: Any
    slots: Any
    cuts: Any
    ring: Any
    lags: Any
    when: Any


def layer_kernel(settings, layouts, plan, *refs):
    first, second = len(Inputs._fields), len(Inputs._fields) + len(Results._fields)
    r = Refs(Inputs(*refs[:first]), Results(*refs[first:second]), Scratch(*refs[second:]))
    side = lax.axis_index("stream")
    greet(plan, r)
    for which, s in enumerate(settings):
        pl.when(side == which)(partial(run_stream, which, s, layouts[which], plan, r))


def peer_of(plan, offset):
    groups, copies = plan.groups, plan.copies
    me = lax.axis_index("mp") * copies + lax.axis_index("dp")
    index = lax.rem(me + offset, groups * copies)
    return me, index, {"mp": index // copies, "dp": lax.rem(index, copies)}


def greet(plan, r):
    barrier = pltpu.get_barrier_semaphore()
    count = plan.groups * plan.copies

    @pl.loop(1, count)
    def _(offset):
        pl.semaphore_signal(barrier, inc=1, device_id=peer_of(plan, offset)[2], device_id_type=MESH)

    pl.semaphore_signal(barrier, inc=1, device_id={"stream": 1 - lax.axis_index("stream")},
                        device_id_type=MESH)
    pl.semaphore_wait(barrier, count)


class Gather:
    def __init__(self, s, plan, r):
        self.groups, self.r = plan.groups, r
        stride, copy = plan.copies // 4, lax.axis_index("dp")
        self.z = lax.axis_index("mp")
        self.quarter = lax.rem(copy // stride, 4)
        base = lax.rem(copy, stride)
        self.to_y = {"dp": (self.quarter ^ 2) * stride + base}
        self.to_c = {"dp": (self.quarter ^ 1) * stride + base}
        self.at_end = jnp.logical_or(self.z == 0, self.z == self.groups - 1)
        w, u, inner = s.width, s.units, plan.inner

        def projection(ref, part):
            return ref.at[:, pl.ds(part * (w // 4), w // 4), :]

        def leave(ref, part):
            return ref.at[pl.ds(part * (inner // 4), inner // 4), pl.ds(0, w)]

        def enter(ref, part):
            return ref.at[pl.ds(part * (w // 4), w // 4), pl.ds(0, u)]

        def fall(ref, part):
            return ref.at[pl.ds(part * (u // 4), u // 4), pl.ds(0, w)]

        self.pieces = [
            (r.cross_in, r.f_cross_in, projection),
            (r.cross_out, r.f_cross_out, leave),
            (r.up, r.f_up, enter),
            (r.down, r.f_down, fall),
            (r.attend_in, r.f_attend_in, projection),
            (r.attend_out, r.f_attend_out, leave),
        ]

    def z_copy(self, p, way, hop):
        step = 1 - 2 * way
        origin = self.z - hop * step
        source, full, cut = self.pieces[p]
        dst = cut(full.at[origin], self.quarter)
        src = cut(source, self.quarter) if hop == 0 else dst
        return pltpu.make_async_remote_copy(
            src, dst, self.r.send_gz.at[p, way, hop], self.r.recv_gz.at[p, way, hop],
            device_id={"mp": self.z + step}, device_id_type=MESH)

    def block(self, p, way, hop, whose):
        source, full, cut = self.pieces[p]
        return cut(full.at[self.z - (hop + 1) * (1 - 2 * way)], whose)

    def z_arrival(self, p, way, hop):
        block = self.block(p, way, hop, self.quarter)
        return pltpu.make_async_remote_copy(
            block, block, self.r.send_gz.at[p, way, hop], self.r.recv_gz.at[p, way, hop],
            device_id={"mp": self.z - (1 - 2 * way)}, device_id_type=MESH)

    def y_copy(self, p, way, hop, mine=True):
        block = self.block(p, way, hop, self.quarter if mine else self.quarter ^ 2)
        return pltpu.make_async_remote_copy(
            block, block, self.r.send_gy.at[p, way, hop], self.r.recv_gy.at[p, way, hop],
            device_id=self.to_y, device_id_type=MESH)

    def c_copy(self, p, way, hop, which, mine=True):
        whose = (self.quarter if mine else self.quarter ^ 1) ^ (2 * which)
        block = self.block(p, way, hop, whose)
        return pltpu.make_async_remote_copy(
            block, block, self.r.send_gc.at[p, way, hop, which],
            self.r.recv_gc.at[p, way, hop, which], device_id=self.to_c, device_id_type=MESH)

    def sends(self, way, hop):
        last = self.groups - 1
        if way == 0:
            return jnp.logical_and(self.z >= hop, self.z < last)
        return jnp.logical_and(self.z <= last - hop, self.z > 0)

    def arrives(self, way, hop):
        return self.z >= hop + 1 if way == 0 else self.z <= self.groups - 2 - hop

    def each(self, test, action, hops=None):
        for hop in range(self.groups - 1) if hops is None else hops:
            for way in range(2):
                pl.when(test(way, hop))(partial(action, way, hop))

    def own(self, p):
        for way in range(2):
            pl.when(self.sends(way, 0))(lambda: self.z_copy(p, way, 0).start())

    def begin(self, ahead):
        for p in range(ahead):
            self.own(p)
        for p in range(ahead, len(self.pieces)):
            pl.when(self.at_end)(partial(self.own, p))

    def later(self, p):
        if p < len(self.pieces):
            pl.when(jnp.logical_not(self.at_end))(partial(self.own, p))

    def received(self, p, *hops):
        def action(way, hop):
            self.z_arrival(p, way, hop).wait_recv()
            if hop + 1 < self.groups - 1:
                pl.when(self.sends(way, hop + 1))(lambda: self.z_copy(p, way, hop + 1).start())
            self.y_copy(p, way, hop).start()
            self.c_copy(p, way, hop, 0).start()

        self.each(self.arrives, action, hops or None)

    def shared(self, p, *hops):
        def action(way, hop):
            self.y_copy(p, way, hop, mine=False).wait_recv()
            self.c_copy(p, way, hop, 1).start()

        self.each(self.arrives, action, hops or None)

    def settled(self, p, weights, name, *hops):
        def action(way, hop):
            for which in range(2):
                self.c_copy(p, way, hop, which, mine=False).wait_recv()
            for item in weights.copies(name, self.z - (hop + 1) * (1 - 2 * way), False):
                item.start()

        self.each(self.arrives, action, hops or None)

    def drained(self, p):
        self.each(self.sends, lambda way, hop: self.z_copy(p, way, hop).wait_send())

        def action(way, hop):
            self.y_copy(p, way, hop).wait_send()
            for which in range(2):
                self.c_copy(p, way, hop, which).wait_send()

        self.each(self.arrives, action)


class Weights:
    def __init__(self, s, plan, r):
        self.s, self.r, self.plan = s, r, plan
        self.z = lax.axis_index("mp")
        w, u, inner, groups = s.width, s.units, plan.inner, plan.groups
        self.kinds = {
            "cross_in": (0, r.cross_in, r.f_cross_in, r.w_in, 3),
            "cross_out": (1, r.cross_out, r.f_cross_out, r.w_cross_out, s.parts),
            "up": (2, r.up, r.f_up, r.w_up, u // TILE),
            "down": (3, r.down, r.f_down, r.w_down, s.parts),
            "attend_in": (4, r.attend_in, r.f_attend_in, r.w_in, 3),
            "attend_out": (5, r.attend_out, r.f_attend_out, r.w_attend_out, s.parts),
        }

    def copies(self, name, z, own):
        number, arg, full, held, blocks = self.kinds[name]
        source = arg if own else full.at[z]
        s, groups, inner = self.s, self.plan.groups, self.plan.inner
        for b in range(blocks):
            if name in ("cross_in", "attend_in"):
                src = source.at[b, pl.ds(0, s.width), :]
                row, size = (z * 3 + b) * s.width, s.width
            elif name == "up":
                src = source.at[pl.ds(0, s.width), pl.ds(b * TILE, TILE)]
                row, size = (z * blocks + b) * s.width, s.width
            else:
                size = s.units if name == "down" else inner
                src = source.at[pl.ds(0, size), pl.ds(b * TILE, TILE)]
                row = (b * groups + z) * size
            yield pltpu.make_async_copy(
                src, held.at[pl.ds(pl.multiple_of(row, TILE), size)], self.r.weight_sem.at[number, z, b])

    def load(self, name, which="all"):
        for z in range(self.plan.groups):
            if which in ("all", "own"):
                @pl.when(self.z == z)
                def _():
                    for item in self.copies(name, z, True):
                        item.start()

            if which in ("all", "rest"):
                @pl.when(self.z != z)
                def _():
                    for item in self.copies(name, z, False):
                        item.start()

    def wait(self, name):
        for z in range(self.plan.groups):
            for item in self.copies(name, z, False):
                item.wait()


class Outputs:
    def __init__(self, s, plan, r):
        self.s, self.r, self.groups, self.cuts = s, r, plan.groups, plan.cuts
        self.z = lax.axis_index("mp")
        self.last = self.groups - 1
        self.rows = plan.tokens // self.cuts
        self.pairs = ((r.layer_rows, r.layer_full), (r.hidden_rows, r.hidden_full))

    def cut(self, ref, k):
        return ref.at[pl.ds(pl.multiple_of(k * self.rows, self.rows), self.rows),
                      pl.ds(0, self.s.width)]

    def copy(self, which, k, way, hop, arrival=False):
        step = 1 - 2 * way
        origin = self.z - (hop + 1 if arrival else hop) * step
        rows, full = self.pairs[which]
        dst = self.cut(full.at[origin], k)
        src = self.cut(rows, k) if hop == 0 and not arrival else dst
        return pltpu.make_async_remote_copy(
            src, dst, self.r.send_a.at[which, k, way, hop], self.r.recv_a.at[which, k, way, hop],
            device_id={"mp": self.z + step}, device_id_type=MESH)

    def sends(self, way, hop):
        if way == 0:
            return jnp.logical_and(self.z >= hop, self.z < self.last)
        return jnp.logical_and(self.z <= self.last - hop, self.z > 0)

    def arrives(self, way, hop):
        return self.z >= hop + 1 if way == 0 else self.z <= self.last - 1 - hop

    def step(self, which, k):
        for hop in range(self.groups):
            now = k - hop

            @pl.when(jnp.logical_and(now >= 0, now < self.cuts))
            def _():
                for way in range(2):
                    if hop:
                        pl.when(self.arrives(way, hop - 1))(
                            lambda: self.copy(which, now, way, hop - 1, True).wait_recv())
                    if hop < self.last:
                        pl.when(self.sends(way, hop))(
                            lambda: self.copy(which, now, way, hop).start())

    def local(self, which):
        rows, full = self.pairs[which]
        width = self.s.width
        items = [pltpu.make_async_copy(rows.at[:, pl.ds(0, width)],
                                       full.at[self.z, :, pl.ds(0, width)],
                                       self.r.local_sem.at[which, self.groups])]
        padded = full.shape[2]
        if width < padded:
            items += [pltpu.make_async_copy(
                self.r.zero, full.at[z, :, pl.ds(width, padded - width)],
                self.r.local_sem.at[which, z]) for z in range(self.groups)]
        return items

    def drained(self):
        for which in range(2):
            @pl.loop(0, self.cuts)
            def _(k):
                for way in range(2):
                    for hop in range(self.last):
                        pl.when(self.sends(way, hop))(
                            lambda: self.copy(which, k, way, hop).wait_send())
            for item in self.local(which):
                item.wait()


class Reduce:
    def __init__(self, which, s, layout, plan, r):
        self.text = which == 0
        self.r, self.groups, self.chunk = r, plan.groups, plan.chunk
        self.slots, self.lags = plan.slots, plan.lags
        self.count = (layout.total + 3 * plan.inner) // self.chunk
        stride, copy = plan.copies // 4, lax.axis_index("dp")
        quarter = lax.rem(copy // stride, 4)
        base = lax.rem(copy, stride)
        self.z = lax.axis_index("mp")
        self.y, self.core = quarter // 2, lax.rem(quarter, 2)
        self.to_y = {"dp": (quarter ^ 2) * stride + base}
        self.to_c = {"dp": (quarter ^ 1) * stride + base}
        self.last = self.groups - 1

    def widths(self, action):
        if not self.text:
            action(TILE, TILE, False)
        else:
            pl.when(self.core == 0)(partial(action, TILE, 128, False))
            pl.when(self.core == 1)(partial(action, 128, TILE, True))

    def first_lane(self, core, y):
        if self.text:
            return pl.multiple_of(jnp.where(core == 0, y * 2 * TILE, TILE + y * 128), 128)
        return pl.multiple_of((2 * y + core) * TILE, 128)

    def rows(self, i):
        return pl.ds(pl.multiple_of(i * self.chunk, self.chunk), self.chunk)

    def slot(self, i):
        return lax.rem(i, self.slots)

    def core_copy(self, i, k, other):
        n = self.slot(i)
        return pltpu.make_async_remote_copy(
            self.r.grads.at[:, self.rows(i), pl.ds(self.first_lane(1 - self.core, k), other)],
            self.r.from_core.at[n, k, :, :, pl.ds(0, other)],
            self.r.send_c.at[n, k], self.r.recv_c.at[n, k],
            device_id=self.to_c, device_id_type=MESH)

    def core_arrival(self, i, k, size):
        n = self.slot(i)
        block = self.r.from_core.at[n, k, :, :, pl.ds(0, size)]
        return pltpu.make_async_remote_copy(
            block, block, self.r.send_c.at[n, k], self.r.recv_c.at[n, k],
            device_id=self.to_c, device_id_type=MESH)

    def own_load(self, i, k, size):
        n = lax.rem(i, 4)
        return pltpu.make_async_copy(
            self.r.grads.at[:, self.rows(i), pl.ds(self.first_lane(self.core, k), size)],
            self.r.own.at[n, k, :, :, pl.ds(0, size)], self.r.own_sem.at[n, k])

    def y_copy(self, i, size):
        n = self.slot(i)
        return pltpu.make_async_remote_copy(
            self.r.from_core.at[n, 1 - self.y, :, :, pl.ds(0, size)],
            self.r.from_y.at[n, :, :, pl.ds(0, size)],
            self.r.send_y.at[n], self.r.recv_y.at[n], device_id=self.to_y, device_id_type=MESH)

    def z_copy(self, i, way, t, size, fresh):
        n = self.slot(i)
        dst = self.r.from_z.at[n, way, t, :, pl.ds(0, size)]
        src = self.r.from_core.at[n, self.y, t, :, pl.ds(0, size)] if fresh else dst
        return pltpu.make_async_remote_copy(
            src, dst, self.r.send_z.at[n, way, t], self.r.recv_z.at[n, way, t],
            device_id={"mp": self.z + 1 - 2 * way}, device_id_type=MESH)

    def far_copy(self, i):
        n = self.slot(i)
        return pltpu.make_async_remote_copy(
            self.r.far.at[0, n], self.r.far.at[1, n], self.r.send_f.at[n], self.r.recv_f.at[n],
            device_id=self.to_y, device_id_type=MESH)

    def out_store(self, i, start, size):
        n = lax.rem(i, 2)
        return pltpu.make_async_copy(
            self.r.staged_out.at[n, :, pl.ds(start, size)],
            self.r.reduced.at[self.rows(i), pl.ds(start, size)],
            self.r.out_sem.at[1 if start else 0, n])

    def credit(self, i, sem):
        pl.when(i >= self.slots)(lambda: pl.semaphore_wait(sem, 1))

    def stage_a(self, i):
        self.credit(i, self.r.free.at[0])

        def action(size, other, far):
            for k in range(2):
                self.core_copy(i, k, other).start()
                self.own_load(i, k, size).start()

        self.widths(action)

    def stage_b(self, i):
        n = self.slot(i)

        def action(size, other, far):
            for k in range(2):
                self.core_arrival(i, k, size).wait_recv()
                self.own_load(i, k, size).wait()
                self.r.from_core[n, k, :, :, :size] += self.r.own[lax.rem(i, 4), k, :, :, :size]
            self.credit(i, self.r.free.at[1])
            self.y_copy(i, size).start()

        self.widths(action)

    def z_step(self, hop, i):
        n = self.slot(i)

        def action(size, other, far):
            for way in range(2):
                t = self.z + (1 - 2 * way) * (self.groups - hop)

                @pl.when(t <= self.last if way == 0 else t >= 0)
                def _():
                    first = self.z == (0 if way == 0 else self.last)
                    pl.when(first)(lambda: self.z_copy(i, way, t, size, True).start())

                    @pl.when(jnp.logical_not(first))
                    def _():
                        self.z_copy(i, way, t, size, False).wait_recv()
                        self.r.from_z[n, way, t, :, :size] += (
                            self.r.from_core[n, self.y, t, :, :size])
                        self.z_copy(i, way, t, size, False).start()

        self.widths(action)

    def stage_c(self, i):
        n = self.slot(i)

        def action(size, other, far):
            self.y_copy(i, size).wait_recv()
            self.r.from_core[n, self.y, :, :, :size] += self.r.from_y[n, :, :, :size]

        self.widths(action)
        pl.when(self.z < self.last)(lambda: self.credit(i, self.r.free.at[2]))
        pl.when(self.z > 0)(lambda: self.credit(i, self.r.free.at[3]))
        self.z_step(1, i)

    def final(self, i):
        n = self.slot(i)

        def action(size, other, far):
            for way in range(2):
                edge = 0 if way == 0 else self.last

                @pl.when(self.z != edge)
                def _():
                    self.z_copy(i, way, self.z, size, False).wait_recv()

                @pl.when(self.z == edge)
                def _():
                    self.r.from_z[n, way, self.z, :, :size] = jnp.zeros((self.chunk, size), low)

            total = (self.r.from_core[n, self.y, self.z, :, :size].astype(wide)
                     + self.r.from_z[n, 0, self.z, :, :size].astype(wide)
                     + self.r.from_z[n, 1, self.z, :, :size].astype(wide))

            def keep():
                pl.when(i >= 2)(lambda: self.out_store(i - 2, 0, size).wait())
                self.r.staged_out[lax.rem(i, 2), :, :size] = total
                self.out_store(i, 0, size).start()

            if far:
                pl.when(self.y == 0)(keep)

                @pl.when(self.y == 1)
                def _():
                    pl.when(i >= self.slots)(lambda: self.far_copy(i - self.slots).wait_send())
                    self.credit(i, self.r.free.at[4])
                    self.r.far[0, n] = total.astype(low)
                    self.far_copy(i).start()
            else:
                keep()
            for k in range(2):
                self.core_copy(i, k, other).wait_send()
            self.y_copy(i, size).wait_send()
            for way in range(2):
                for hop in range(1, self.groups):
                    t = self.z + (1 - 2 * way) * (self.groups - hop)
                    pl.when(t <= self.last if way == 0 else t >= 0)(
                        lambda: self.z_copy(i, way, t, size, True).wait_send())

        self.widths(action)

        @pl.when(i < self.count - self.slots)
        def _():
            def tell(index, target):
                pl.semaphore_signal(self.r.free.at[index], inc=1, device_id=target,
                                    device_id_type=MESH)

            tell(0, self.to_c)
            tell(1, self.to_y)
            pl.when(self.z > 0)(lambda: tell(2, {"mp": self.z - 1}))
            pl.when(self.z < self.last)(lambda: tell(3, {"mp": self.z + 1}))

    def land(self, i):
        n = self.slot(i)

        def action(size, other, far):
            if not far:
                return

            @pl.when(self.y == 0)
            def _():
                self.far_copy(i).wait_recv()
                pl.when(i >= 2)(lambda: self.out_store(i - 2, size, size).wait())
                self.r.staged_out[lax.rem(i, 2), :, size : 2 * size] = self.r.far[1, n].astype(wide)
                self.out_store(i, size, size).start()

                @pl.when(i < self.count - self.slots)
                def _():
                    pl.semaphore_signal(self.r.free.at[4], inc=1, device_id=self.to_y,
                                        device_id_type=MESH)

        self.widths(action)

    def iteration(self, j):
        lag_b, lag_c, lag_z, lag_f = self.lags

        def at(i, stage):
            pl.when(jnp.logical_and(i >= 0, i < self.count))(lambda: stage(i))

        at(j, self.stage_a)
        at(j - lag_b, self.stage_b)
        at(j - lag_c, self.stage_c)
        for hop in range(2, self.groups):
            at(j - lag_c - lag_z * (hop - 1), partial(self.z_step, hop))
        done = lag_c + lag_z * (self.groups - 1)
        at(j - done, self.final)
        if self.text:
            at(j - done - lag_f, self.land)

    def iterations(self):
        lag_b, lag_c, lag_z, lag_f = self.lags
        return self.count + lag_c + lag_z * (self.groups - 1) + (lag_f if self.text else 0)

    def drained(self):
        def action(size, other, far):
            pair = (self.count - 2, self.count - 1)
            if not far:
                for i in pair:
                    self.out_store(jnp.int32(i), 0, size).wait()
                return

            @pl.when(self.y == 0)
            def _():
                for i in pair:
                    self.out_store(jnp.int32(i), 0, size).wait()
                    self.out_store(jnp.int32(i), size, size).wait()

            @pl.when(self.y == 1)
            def _():
                @pl.loop(self.count - self.slots, self.count)
                def _(i):
                    self.far_copy(i).wait_send()

        self.widths(action)


class Small:
    def __init__(self, plan, r):
        self.plan, self.r = plan, r
        self.count = plan.groups * plan.copies
        self.per_row = max(1, self.count // 16)
        self.width = r.small_in.shape[1] // self.per_row

    def piece(self, ref, index):
        row, part = index // self.per_row, lax.rem(index, self.per_row)
        return ref.at[pl.ds(row, 1), pl.ds(pl.multiple_of(part * self.width, 128), self.width)]

    def copy(self, offset, first):
        me, peer, target = peer_of(self.plan, offset)
        if first:
            src, dst = self.piece(self.r.small_in, peer), self.r.small_got.at[me]
        else:
            src, dst = self.r.small_sum, self.piece(self.r.small_out, me)
        n = 0 if first else 1
        return pltpu.make_async_remote_copy(
            src, dst, self.r.send_s.at[n, offset], self.r.recv_s.at[n, offset],
            device_id=target, device_id_type=MESH)

    def every(self, action):
        @pl.loop(1, self.count)
        def _(offset):
            action(offset)

    def start(self):
        self.every(lambda offset: self.copy(offset, True).start())

    def local(self, first):
        me = peer_of(self.plan, 0)[0]
        pair = ((self.piece(self.r.small_in, me), self.r.small_got.at[me]) if first
                else (self.r.small_sum, self.piece(self.r.small_out, me)))
        return pltpu.make_async_copy(*pair, self.r.small_sem.at[0 if first else 1])

    def middle(self):
        self.local(True).start()
        self.every(lambda offset: self.copy(offset, True).wait_recv())
        self.local(True).wait()
        self.r.small_sum[...] = jnp.sum(self.r.small_got[...], axis=0)
        self.local(False).start()
        self.every(lambda offset: self.copy(offset, False).start())

    def finish(self):
        self.local(False).wait()
        self.every(lambda offset: self.copy(offset, False).wait_recv())
        for first in (True, False):
            self.every(lambda offset: self.copy(offset, first).wait_send())


def run_stream(which, s, layout, plan, r):
    groups, inner, length = plan.groups, plan.inner, plan.length
    rows_dev = plan.rows
    tokens = plan.tokens
    w, u = s.width, s.units
    z = lax.axis_index("mp")
    side = lax.axis_index("stream")
    gather = Gather(s, plan, r)
    weights = Weights(s, plan, r)
    outputs = Outputs(s, plan, r)
    reduce = Reduce(which, s, layout, plan, r)
    small = Small(plan, r)

    gather.begin(2)
    own_rows = pl.ds(pl.multiple_of(z * tokens, tokens), tokens)
    enter = [pltpu.make_async_copy(r.hidden.at[own_rows], r.x, r.enter_sem.at[0]),
             pltpu.make_async_copy(r.cotangent.at[own_rows], r.grad_out, r.enter_sem.at[1])]
    for item in enter:
        item.start()
    weights.load("cross_in", "own")
    for name in ("cross_out", "up", "down", "attend_out"):
        weights.load(name, "own")

    def bias_copy(step, kind):
        ref, full = ((r.cross_bias, r.a_cross_bias), (r.attend_bias, r.a_attend_bias),
                     (r.up_bias, r.a_up_bias))[kind]
        return pltpu.make_async_remote_copy(
            ref, full.at[z], r.send_b.at[kind, step], r.recv_b.at[kind, step],
            device_id={"mp": lax.rem(z + step, groups)}, device_id_type=MESH)

    for kind, (ref, full) in enumerate(((r.cross_bias, r.a_cross_bias),
                                        (r.attend_bias, r.a_attend_bias),
                                        (r.up_bias, r.a_up_bias))):
        for step in range(1, groups):
            bias_copy(step, kind).start()
        full[z] = ref[...]

    r.zero[...] = jnp.zeros_like(r.zero)

    def swap(source, target, number):
        return pltpu.make_async_remote_copy(
            source, target, r.send_x.at[number], r.recv_x.at[number],
            device_id={"stream": 1 - side}, device_id_type=MESH)

    self_kinds = block_kinds(s.head, s.per_group)
    cross_kinds = block_kinds(128, CO_HEADS // groups)
    self_scale, cross_scale = 1.0 / math.sqrt(s.head), 1.0 / math.sqrt(128)

    def in_block(index):
        return pl.ds(pl.multiple_of(index * w, TILE), w)

    def project(part, source, target, bias_ref, line):
        @pl.loop(0, groups)
        def _(g):
            cols = lane(g * inner, inner)
            value = dot(source[:, :w], r.w_in[in_block(g * 3 + part), :])
            if line is not None:
                value = value + bias_ref[g, line : line + 1].astype(wide)
            target[:, cols] = value.astype(low)

    def vector(ref, line, cols=slice(0, w)):
        return ref[line : line + 1, cols].astype(wide)

    def scaled(normal, line, cols):
        return normal[:, cols] * vector(r.gains, line, cols) + vector(r.shifts, line, cols)

    def leave(source, size, weight, residual, line):
        @pl.loop(0, s.parts)
        def _(j):
            cols = lane(j * TILE)
            at = pl.ds(pl.multiple_of(j * size, TILE), size)
            r.acc[:, cols] = (dot(source[:, :size], weight[at, :]) + residual(cols)
                              + vector(r.out_bias, line, cols))

    def norm(normal, inverse):
        summed = r.acc[:, :w]
        mean = jnp.sum(summed, axis=-1, keepdims=True) * (1.0 / w)
        centred = summed - mean
        scale = lax.rsqrt(
            jnp.sum(centred * centred, axis=-1, keepdims=True) * (1.0 / w) + norm_eps)
        normal[:, :w] = centred * scale
        inverse[...] = scale

    def cross_part(begin, end):
        @pl.loop(begin, end)
        def _(g):
            attend_forward(g, cross_kinds, cross_scale, length, rows_dev, r.q, r.pair_k, r.pair_v,
                           r.cross_allowed, r.cross_prob, r.context)

    def feed_part(begin, end):
        @pl.loop(begin, end)
        def _(g):
            for j in range(u // TILE):
                cols = lane(g * u + j * TILE)
                value = (dot(r.h1[:, :w], r.w_up[in_block(g * (u // TILE) + j), :])
                         + r.a_up_bias[g, 0:1, j * TILE : (j + 1) * TILE].astype(wide))
                bell = 0.5 * (1.0 + lax.erf(value * math.sqrt(0.5)))
                r.active[:, cols] = (value * bell).astype(low)
                r.slope[:, cols] = bell + value * (
                    jnp.exp(-0.5 * value * value) * (1.0 / math.sqrt(2.0 * math.pi)))

    gather.received(0)
    gather.later(2)
    gather.received(1)
    gather.later(3)
    gather.shared(0)
    gather.received(2, 0, 1)
    for kind in range(3):
        for step in range(1, groups):
            bias_copy(step, kind).wait()
    for item in enter:
        item.wait()
    gather.settled(0, weights, "cross_in")
    gather.received(2, 2)
    gather.later(4)
    gather.shared(1)
    weights.wait("cross_in")
    project(1, r.x, r.k, None, None)
    swap(r.k, r.pair_k, 0).start()
    project(2, r.x, r.v, r.a_cross_bias, 1)
    swap(r.v, r.pair_v, 1).start()
    gather.received(3, 0, 1)
    project(0, r.x, r.q, r.a_cross_bias, 0)
    weights.load("attend_in", "own")
    gather.settled(1, weights, "cross_out")
    gather.received(3, 2)
    gather.later(5)
    gather.shared(2)
    gather.settled(2, weights, "up")
    gather.received(4, 0, 1)
    swap(r.k, r.pair_k, 0).wait()
    swap(r.v, r.pair_v, 1).wait()
    cross_part(0, groups // 2)
    gather.received(5, 0)
    cross_part(groups // 2, groups)
    gather.received(4, 2)
    gather.received(5, 1)
    gather.shared(3)
    gather.settled(3, weights, "down")
    weights.wait("cross_out")
    leave(r.context, groups * inner, r.w_cross_out, lambda cols: r.x[:, cols].astype(wide), 0)
    norm(r.n1, r.r1)
    r.h1[:, :w] = scaled(r.n1, 0, slice(0, w)).astype(low)
    gather.received(5, 2)
    gather.shared(4, 0, 1)
    weights.wait("up")
    feed_part(0, groups // 2)
    gather.shared(4, 2)
    gather.settled(4, weights, "attend_in", 0, 1)
    feed_part(groups // 2, groups)
    gather.shared(5)
    gather.settled(4, weights, "attend_in", 2)
    gather.settled(5, weights, "attend_out")
    weights.wait("down")
    leave(r.active, groups * u, r.w_down, lambda cols: scaled(r.n1, 0, cols), 1)
    norm(r.n2, r.r2)
    r.h2[:, :w] = scaled(r.n2, 1, slice(0, w)).astype(low)
    weights.wait("attend_in")
    project(0, r.h2, r.q2, r.a_attend_bias, 0)
    project(1, r.h2, r.k2, None, None)
    project(2, r.h2, r.v2, r.a_attend_bias, 1)

    @pl.loop(0, groups)
    def _(g):
        attend_forward(g, self_kinds, self_scale, length, rows_dev, r.q2, r.k2, r.v2,
                       r.self_allowed, r.self_prob, r.context2)

    weights.wait("attend_out")
    leave(r.context2, groups * inner, r.w_attend_out, lambda cols: scaled(r.n2, 1, cols), 2)
    norm(r.n3, r.r3)
    r.layer_rows[:, :w] = scaled(r.n3, 2, slice(0, w)).astype(low)
    for item in outputs.local(0):
        item.start()
    for p in range(len(gather.pieces)):
        gather.drained(p)

    def stores(row):
        return [
            pltpu.make_async_copy(
                r.staged.at[g, :, pl.ds(0, w)],
                r.grads.at[g, pl.ds(pl.multiple_of(row, TILE), TILE), pl.ds(0, w)],
                r.store_sem.at[g])
            for g in range(groups)]

    def weight_grads(left, right, row, size):
        def step(k):
            for g, item in enumerate(stores(row + k * TILE)):
                r.staged[g, :, :w] = dot_tn(
                    left[:, lane(g * size + k * TILE)], right[:, :w]).astype(low)
                item.start()

        return step

    def flush():
        for item in stores(0):
            item.wait()

    def back_norm(incoming, normal, inverse, line):
        r.small_in[3 + line : 4 + line, :w] = down_sum(incoming * normal[:, :w])
        r.small_in[6 + line : 7 + line, :w] = down_sum(incoming)
        out = norm_back(normal[:, :w], inverse[...], vector(r.gains, line), incoming, w)
        r.acc[:, :w] = out
        r.low_grad[:, :w] = out.astype(low)
        r.small_in[line : line + 1, :w] = down_sum(out.astype(low).astype(wide))

    def leave_back(weight, size, row, count):
        total = None
        for j in range(s.parts):
            at = pl.ds(pl.multiple_of(j * size + row, TILE), count)
            part = dot_nt(r.low_grad[:, j * TILE : (j + 1) * TILE], weight[at, :])
            total = part if total is None else total + part
        return total

    def enter_back(d, weight, blocks):
        def step(g):
            total = r.acc[:, :w]
            for b, (ref, start) in enumerate(d(g)):
                total = total + dot_nt(ref[:, lane(start)], weight[in_block(g * blocks + b), :])
            r.acc[:, :w] = total

        return step

    def context_back(weight):
        def step(g):
            r.grad_context[:, lane(g * inner, inner)] = leave_back(
                weight, groups * inner, g * inner, inner).astype(low)

        return step

    def self_step(g):
        attend_backward(g, self_kinds, self_scale, length, rows_dev, r.q2, r.k2, r.v2,
                        r.self_prob, r.grad_context, r.d1, r.d2, r.d3)

    def cross_step(g):
        attend_backward(g, cross_kinds, cross_scale, length, rows_dev, r.q, r.pair_k, r.pair_v,
                        r.cross_prob, r.grad_context, r.d1, r.d2, r.d3)

    def second_norm(_):
        r.small_in[12:13, :] = down_sum(r.d1[...].astype(wide))
        r.small_in[13:14, :] = down_sum(r.d3[...].astype(wide))
        weights.load("cross_in")
        back_norm(r.acc[:, :w], r.n2, r.r2, 1)

    def slope_step(g):
        for j in range(u // TILE):
            cols = lane(g * u + j * TILE)
            value = leave_back(r.w_down, groups * u, g * u + j * TILE, TILE)
            r.dz[:, cols] = (value * r.slope[:, cols]).astype(low)

    def first_norm(_):
        back_norm(r.acc[:, :w], r.n1, r.r1, 0)
        units, width = plan.units, r.small_in.shape[1]
        for g in range(groups):
            for j in range(u // TILE):
                start = g * units + j * TILE
                r.small_in[9 + start // width : 10 + start // width,
                           start % width : start % width + TILE] = down_sum(
                    r.dz[:, g * u + j * TILE : g * u + (j + 1) * TILE].astype(wide))

    def pair_send(_):
        r.small_in[14:15, :] = down_sum(r.d1[...].astype(wide))
        weights.wait("cross_in")
        swap(r.d2, r.back_k, 2).start()
        swap(r.d3, r.back_v, 3).start()

    def pair_take(_):
        swap(r.d2, r.back_k, 2).wait()
        swap(r.d3, r.back_v, 3).wait()
        r.small_in[15:16, :] = down_sum(r.back_v[...].astype(wide))
        small.start()

    def hidden_store(_):
        r.hidden_rows[:, :w] = r.acc[:, :w].astype(low)
        for item in outputs.local(1):
            item.start()

    def attend_grads(k):
        for which_one, d in enumerate((r.d1, r.d2, r.d3)):
            pl.when(k == which_one)(lambda: weight_grads(
                d, r.h2, layout.attend_in + which_one * inner, inner)(0))

    def cross_grads(k):
        for which_one, d in enumerate((r.back_k, r.back_v)):
            pl.when(k == which_one)(lambda: weight_grads(
                d, r.x, layout.total + (1 + which_one) * inner, inner)(0))

    r.small_in[...] = jnp.zeros_like(r.small_in)
    back_norm(r.grad_out[:, :w].astype(wide), r.n3, r.r3, 2)
    pl.loop(0, groups)(context_back(r.w_attend_out))
    weight_grads(r.context2, r.low_grad, layout.attend_out, inner)(0)
    nb = u // TILE
    take = plan.when[which]
    schedule = (
        (0, 4, 2, False, self_step),
        (2, 3, 1, True, attend_grads),
        (2, 4, 2, False, enter_back(lambda g: [(d, g * inner) for d in (r.d1, r.d2, r.d3)],
                                    r.w_in, 3)),
        (4, 1, 1, False, second_norm),
        (5, 4, 2, False, slope_step),
        (5, nb, 1, True, weight_grads(r.active, r.low_grad, layout.down, u)),
        (5 + nb, nb, 1, True, weight_grads(r.dz, r.h1, layout.up, u)),
        (7, 4, 2, False, enter_back(lambda g: [(r.dz, g * u + b * TILE) for b in range(nb)],
                                    r.w_up, nb)),
        (9, 1, 1, False, first_norm),
        (10, 4, 2, False, context_back(r.w_cross_out)),
        (12, 4, 2, False, cross_step),
        (14, 1, 1, False, pair_send),
        (11, 1, 1, True, weight_grads(r.context, r.low_grad, layout.cross_out, inner)),
        (15, 1, 1, True, weight_grads(r.d1, r.x, layout.total, inner)),
        (take, 1, 1, False, pair_take),
        (take, 2, 1, True, cross_grads),
        (take + 2, 4, 2, False, enter_back(
            lambda g: [(d, g * inner) for d in (r.d1, r.back_k, r.back_v)], r.w_in, 3)),
        (take + 4, 1, 1, False, hidden_store),
        (take + 5, 1, 1, False, lambda _: small.middle()),
    )
    storing = sorted({start + n for start, steps, per, keeps, _ in schedule if keeps
                      for n in range(steps)})
    assert len(storing) == sum(steps for _, steps, _, keeps, _ in schedule if keeps)
    hidden_at = take + 5

    @pl.loop(0, max(reduce.iterations(), hidden_at + plan.cuts + groups))
    def _(j):
        flushes = j == 0
        for n in storing:
            flushes = jnp.logical_or(flushes, j == n + 1)
        pl.when(flushes)(flush)
        for start, steps, per, _, step in schedule:
            @pl.when(jnp.logical_and(j >= start, j < start + steps // per))
            def _():
                if per == 1:
                    step(j - start)
                else:
                    pl.loop(0, per)(lambda n: step((j - start) * per + n))
        reduce.iteration(j)
        outputs.step(0, j - 1)
        outputs.step(1, j - hidden_at)

    reduce.drained()
    outputs.drained()
    small.finish()


def shards(
    hidden,
    cotangent,
    segments,
    cross_in,
    cross_bias,
    cross_out,
    up_weight,
    up_bias,
    down_weight,
    attend_in,
    attend_bias,
    attend_out,
    out_bias,
    norm_gains,
    norm_shifts,
):
    groups = lax.axis_size("mp")
    copies = lax.axis_size("dp")
    stride = copies // 4
    side = lax.axis_index("stream")
    member = lax.axis_index("mp")
    copy = lax.axis_index("dp")
    is_image = side == 1
    inner = cross_in.shape[3]
    padded = hidden.shape[2]
    units = up_weight.shape[2]
    length = segments.shape[2]
    text = Setting(TEXT_WIDTH, TEXT_HEADS, TEXT_FF, groups)
    image = Setting(IMAGE_WIDTH, IMAGE_HEADS, IMAGE_FF, groups)
    settings = (text, image)
    layouts = [Layout(s, inner) for s in settings]
    rows_max = max(layout.total for layout in layouts) + 3 * inner
    rows_dev = segments.shape[1] // groups
    tokens = hidden.shape[1] // groups
    co = groups * inner

    def shape(dims, kind=low):
        return jax.ShapeDtypeStruct(dims, kind)

    seg = lax.dynamic_slice_in_dim(segments, member * rows_dev, rows_dev, 1)
    seg_own = lax.dynamic_index_in_dim(seg, side, 0, keepdims=False)
    seg_other = lax.dynamic_index_in_dim(seg, 1 - side, 0, keepdims=False)
    cross_allowed = (seg_other[:, :, None] == seg_own[:, None, :]).astype(wide)
    self_allowed = (seg_own[:, :, None] == seg_own[:, None, :]).astype(wide)

    dma = pltpu.SemaphoreType.DMA

    def real(*dims):
        return pltpu.VMEM(dims, wide)

    def short(*dims):
        return pltpu.VMEM(dims, low)

    chunk, slots, cuts, ring = 64, 20, 8, 4
    widest = max(s.units for s in settings) * groups
    up_rows = max(groups * s.units * s.width for s in settings) // TILE
    heads = max(groups * s.per_group for s in settings)
    pieces, hops = 6, groups - 1
    peers = groups * copies
    small_width = padded // max(1, peers // 16)
    scratch = Scratch(
        w_in=short(groups * 3 * padded, inner),
        w_cross_out=short(padded // TILE * co, TILE),
        w_attend_out=short(padded // TILE * co, TILE),
        w_up=short(up_rows, TILE),
        w_down=short(up_rows, TILE),
        x=short(tokens, padded),
        grad_out=short(tokens, padded),
        q=short(tokens, co),
        k=short(tokens, co),
        v=short(tokens, co),
        pair_k=short(tokens, co),
        pair_v=short(tokens, co),
        back_k=short(tokens, co),
        back_v=short(tokens, co),
        cross_prob=real(CO_HEADS * rows_dev, length, length),
        self_prob=real(heads * rows_dev, length, length),
        context=short(tokens, co),
        context2=short(tokens, co),
        acc=real(tokens, padded),
        n1=real(tokens, padded),
        n2=real(tokens, padded),
        n3=real(tokens, padded),
        r1=real(tokens, 1),
        r2=real(tokens, 1),
        r3=real(tokens, 1),
        h1=short(tokens, padded),
        h2=short(tokens, padded),
        slope=real(tokens, widest),
        active=short(tokens, widest),
        dz=short(tokens, widest),
        q2=short(tokens, co),
        k2=short(tokens, co),
        v2=short(tokens, co),
        d1=short(tokens, co),
        d2=short(tokens, co),
        d3=short(tokens, co),
        low_grad=short(tokens, padded),
        grad_context=short(tokens, co),
        layer_rows=short(tokens, padded),
        hidden_rows=short(tokens, padded),
        zero=short(tokens, IMAGE_WIDTH - TEXT_WIDTH),
        staged=short(ring, TILE, padded),
        from_core=short(slots, 2, groups, chunk, TILE),
        from_y=short(slots, groups, chunk, TILE),
        from_z=short(slots, 2, groups, chunk, TILE),
        far=short(2, slots, chunk, 128),
        own=short(4, 2, groups, chunk, TILE),
        staged_out=real(2, chunk, TILE),
        small_in=real(16, padded),
        small_got=real(peers, 1, small_width),
        small_sum=real(1, small_width),
        small_sem=dma((2,)),
        a_cross_bias=short(groups, 2, inner),
        a_attend_bias=short(groups, 2, inner),
        a_up_bias=short(groups, 1, units),
        send_gz=dma((pieces, 2, hops)),
        recv_gz=dma((pieces, 2, hops)),
        send_gy=dma((pieces, 2, hops)),
        recv_gy=dma((pieces, 2, hops)),
        send_gc=dma((pieces, 2, hops, 2)),
        recv_gc=dma((pieces, 2, hops, 2)),
        weight_sem=dma((pieces, groups, 4)),
        enter_sem=dma((2,)),
        send_b=dma((3, groups)),
        recv_b=dma((3, groups)),
        send_x=dma((4,)),
        recv_x=dma((4,)),
        store_sem=dma((ring,)),
        send_c=dma((slots, 2)),
        recv_c=dma((slots, 2)),
        send_y=dma((slots,)),
        recv_y=dma((slots,)),
        send_z=dma((slots, 2, groups)),
        recv_z=dma((slots, 2, groups)),
        send_f=dma((slots,)),
        recv_f=dma((slots,)),
        own_sem=dma((4, 2)),
        out_sem=dma((2, 2)),
        send_a=dma((2, cuts, 2, hops)),
        recv_a=dma((2, cuts, 2, hops)),
        local_sem=dma((2, groups + 1)),
        send_s=dma((2, peers)),
        recv_s=dma((2, peers)),
        free=pltpu.SemaphoreType.REGULAR((5,)),
    )
    plan = Plan(
        groups=groups, copies=copies, inner=inner, length=length, rows=rows_dev,
        tokens=tokens, units=units, chunk=chunk, slots=slots, cuts=cuts,
        ring=ring, lags=(3, 8, 2, 2),
        when=(26, 24),
    )
    weights = (
        jnp.swapaxes(cross_in[0], 0, 1),
        cross_out[0],
        up_weight[0],
        down_weight[0],
        jnp.swapaxes(attend_in[0], 0, 1),
        attend_out[0],
    )
    line = shape((groups, tokens, padded))
    out = pl.pallas_call(
        partial(layer_kernel, settings, layouts, plan),
        out_shape=(
            line, line, shape((rows_max, TILE), wide), shape((16, padded), wide),
        ) + tuple(shape((groups,) + w.shape) for w in weights)
        + (shape((groups, rows_max, padded)),),
        in_specs=[ANY] * 8 + [VMEM] * 8,
        out_specs=(ANY,) * 3 + (VMEM,) + (ANY,) * 7,
        scratch_shapes=list(scratch),
        compiler_params=pltpu.CompilerParams(
            collective_id=0, has_side_effects=True, vmem_limit_bytes=VMEM_LIMIT),
        name="layer",
    )(*weights, hidden[0], cotangent[0], cross_bias[0], attend_bias[0], up_bias,
      out_bias[0], norm_gains[0], norm_shifts[0],
      cross_allowed.reshape(tokens, length), self_allowed.reshape(tokens, length))
    layer_out, hidden_grad, reduced, small = out[:4]

    if stride > 1:
        teams = [[q * stride + b for b in range(stride)] for q in range(4)]
        reduced = lax.psum_scatter(
            reduced.astype(low), "dp", scatter_dimension=1, axis_index_groups=teams, tiled=True
        ).astype(wide)
    columns = padded // copies
    real_block = copy * columns < jnp.where(is_image, IMAGE_WIDTH, TEXT_WIDTH)
    reduced = jnp.where(real_block, reduced, 0.0)

    part = inner // copies
    vector_grads = lax.dynamic_slice_in_dim(small[:9], copy * columns, columns, 1)
    up_bias_grad = lax.dynamic_slice_in_dim(
        small[9:12].reshape(groups * units), (member * copies + copy) * (units // copies),
        units // copies, 0)
    pair_grads = lax.dynamic_slice_in_dim(
        small[12:16], (member * copies + copy) * part, part, 1)

    def unpack(s, layout, reduced):
        u = s.units

        def turned(start):
            block = reduced[start : start + 3 * inner].reshape(3, inner, columns)
            return block.transpose(2, 0, 1)

        return (
            turned(layout.total),
            reduced[layout.cross_out : layout.cross_out + inner],
            jnp.pad(reduced[layout.up : layout.up + u].T, ((0, 0), (0, units - u))),
            jnp.pad(reduced[layout.down : layout.down + u], ((0, units - u), (0, 0))),
            turned(layout.attend_in),
            reduced[layout.attend_out : layout.attend_out + inner],
        )

    g_cross_in, g_cross_out, g_up, g_down, g_attend_in, g_attend_out = lax.cond(
        is_image, partial(unpack, image, layouts[1]), partial(unpack, text, layouts[0]), reduced)
    return (
        layer_out.reshape(1, groups * tokens, padded),
        hidden_grad.reshape(1, groups * tokens, padded),
        g_cross_in[None],
        pair_grads[None, 2:4],
        g_cross_out[None],
        g_up[None],
        up_bias_grad[None],
        g_down[None],
        g_attend_in[None],
        pair_grads[None, 0:2],
        g_attend_out[None],
        vector_grads[None, 0:3],
        vector_grads[None, 3:6],
        vector_grads[None, 6:9],
    )


def solution(mesh):
    placed = (
        P("stream", "dp", None),
        P("stream", "dp", None),
        P(None, "dp", None),
        P("stream", None, None, "mp"),
        P("stream", None, "mp"),
        P("stream", "mp", None),
        P("stream", None, "mp"),
        P("stream", "mp"),
        P("stream", "mp", None),
        P("stream", None, None, "mp"),
        P("stream", None, "mp"),
        P("stream", "mp", None),
        P("stream", None, None),
        P("stream", None, None),
        P("stream", None, None),
    )
    return jax.shard_map(
        shards,
        mesh=mesh,
        in_specs=placed,
        out_specs=(
            P("stream", "dp", None),
            P("stream", "dp", None),
            P("stream", "dp", None, "mp"),
            P("stream", None, ("mp", "dp")),
            P("stream", "mp", "dp"),
            P("stream", "dp", "mp"),
            P("stream", ("mp", "dp")),
            P("stream", "mp", "dp"),
            P("stream", "dp", None, "mp"),
            P("stream", None, ("mp", "dp")),
            P("stream", "mp", "dp"),
            P("stream", None, "dp"),
            P("stream", None, "dp"),
            P("stream", None, "dp"),
        ),
        check_vma=False,
    )
```

time: 1380 us -> 349 us (0.25)
  waiting for transfers between devices: 1080 us -> 0 us
  Pallas kernels: 0 us -> 323 us
  local copies, waits for them, and re-layouts: 110 us -> 14.8 us
  other arithmetic: 81.8 us -> 3.12 us
  matrix products: 62.2 us -> 0 us
  between operations: 15.2 us -> 1.26 us
    psum x6 -> x0, waiting for transfers between devices: 724 us -> none  [the longest x3 469 us: across_heads(): return lax.psum(partial_out, 'mp')]
    pallas_call x0 -> x1, Pallas kernels: none -> 323 us  [shards(): pl.pallas_call(partial(layer_kernel, settings, layouts, plan), out_shape=...]
    unnamed x36 -> x0, waiting for transfers between devices: 170 us -> none
    reduce_scatter x6 -> x0, waiting for transfers between devices: 154 us -> none  [the longest x1 29.9 us: shards(): lax.psum_scatter(attend_in_term.astype(jnp.bfloat16), 'dp', scatter_dimen...]
    dot_general x31 -> x0, matrix products: 62.2 us -> none  [the longest x1 9.51 us: feed_inner(): jnp.dot(activated, down_weight[0, :hidden_dev, :width_real], preferred_el...]
    ppermute x4 -> x0, waiting for transfers between devices: 35.6 us -> none  [partner(): return lax.ppermute(block, axis, route)]
    reduce_sum x24 -> x0, other arithmetic: 35.3 us -> none  [the longest x6 17.3 us: normalize(): row_mean = jnp.mean(value_in, axis=-1, keepdims=True)]
    pad x30 -> x0, local copies, waits for them, and re-layouts: 33.7 us -> none  [widen(): jnp.pad(value_in, [(0, want_size - have_size) for have_size, want_size in...]
  transfers between devices with their start and end apart: 28 -> 0, of which waited for: 24 -> 0; matrix products, arithmetic and copies ran while one was open for 8% -> 0% of each run, Pallas kernels for 0% -> 0%
where the time goes in v2:
time: 349 us; the launch traced here: 342 us
  Pallas kernels  323 us (93%)
  local copies, waits for them, and re-layouts  14.8 us (4%)
    pallas_call x1, Pallas kernels, shards(): pl.pallas_call(partial(layer_kernel, settings, layouts, plan), out_shape=...  323 us

profile of v2, /device:TPU:0, one launch (start us, length us, event | category | flops | bytes accessed | tf_op | source)
XLA Modules:
  0.0 342.0 jit_solution(1240020124979669455)
XLA Ops:
  0.7 0.7 fusion.2
  1.4 0.8 fusion.1
  2.2 322.9 %layer.1 = (bf16[4,256,1024]{2,1,0:T(8,128)(2,1)}, bf16[4,256,1024]{2,1,0:T(8,128)(2,1)}, f32[3584,256]{1,0:T(8,128)}, f32[16,1024]{1,0:T(8,128)}, bf16[4,3,1024...) custom-call(bf16[3,1024,256]{2,1,0:T(8,128)(2,1)} %bitcast.92, ...), custom_call_target="tpu_custom_call" | custom-call | tf_op jit(solution)/shard_map/layer/pallas_call | solution.py:1421
  325.1 0.0 copy-start.6
  325.1 8.8 %conditional.1 = (f32[1,256,256]{2,1,0:T(8,128)S(1)}, f32[1,768,256]{2,1,0:T(8,128)S(1)}, f32[1,256,256]{2,1,0:T(8,128)S(1)}, f32[1,256,3,256]{3,1,2,0:T(8,128)}...) conditional(s32[]{:T(128)} %convert_element_type.17, (pred[]{:T(512)}, s32[]{:T(128)}, ...), branch_computations={%region_0.1_spmd, %region_1.2_spmd} | conditional | flops 917506 | bytes 34078820 | solution.py:1471
  325.1 2.3 broadcast_select_fusion
  327.4 0.0 copy-start
  327.4 1.8 copy-done
  329.2 0.2 fusion.4
  329.4 1.1 copy.35
  330.6 1.1 copy.37
  331.7 1.1 copy.39
  332.9 1.1 slice_bitcast_fusion.2
  333.9 0.0 copy-start.3
  333.9 0.0 copy-start.4
  333.9 0.0 copy-start.5
  334.0 0.0 copy-start.2
  334.0 0.0 copy-done.6
  334.0 0.6 dynamic_slice.22
  334.7 0.1 constant_dynamic-slice_fusion
  334.7 0.6 slice_bitcast_fusion.7
  335.3 0.1 dynamic-slice_bitcast_fusion
  335.4 0.6 copy.32
  336.0 0.6 copy.33
  336.6 0.6 copy.34
  337.1 3.1 copy.55
  340.2 0.0 copy-done.2
  340.2 1.3 copy.56
  341.5 0.0 copy-done.3
  341.5 0.0 copy-done.4
  341.5 0.0 copy-done.5
  (3 shorter events, 0.0 us)
Async XLA Ops:
  325.1 8.9 %copy-start.6 = (f32[16,1024]{1,0:T(8,128)S(1)}, f32[16,1024]{1,0:T(8,128)}, u32[]{:S(2)}) copy-start(f32[16,1024]{1,0:T(8,128)} %get-tuple-element.84) | copy-start | bytes 196612
  327.4 1.8 copy-start
  333.9 7.6 %copy-start.3 = (f32[1,768,256]{2,1,0:T(8,128)}, f32[1,768,256]{2,1,0:T(8,128)S(1)}, u32[]{:S(2)}) copy-start(f32[1,768,256]{2,1,0:T(8,128)S(1)} %get-tuple-element.162) | copy-start | bytes 2359300
  333.9 7.6 %copy-start.4 = (f32[1,256,256]{2,1,0:T(8,128)}, f32[1,256,256]{2,1,0:T(8,128)S(1)}, u32[]{:S(2)}) copy-start(f32[1,256,256]{2,1,0:T(8,128)S(1)} %get-tuple-element.165) | copy-start | bytes 786436
  333.9 7.6 %copy-start.5 = (f32[1,256,256]{2,1,0:T(8,128)}, f32[1,256,256]{2,1,0:T(8,128)S(1)}, u32[]{:S(2)}) copy-start(f32[1,256,256]{2,1,0:T(8,128)S(1)} %get-tuple-element.159) | copy-start | bytes 786436
  334.0 6.3 %copy-start.2 = (bf16[4,256,1024]{2,1,0:T(8,128)(2,1)S(1)}, bf16[4,256,1024]{2,1,0:T(8,128)(2,1)}, u32[]{:S(2)}) copy-start(bf16[4,256,1024]{2,1,0:T(8,128)(2,1)} %get-tuple-element.81) | copy-start | bytes 6291460

commit v3 on v2

--- a/solution.py
+++ b/solution.py
@@ -51,13 +51,15 @@
 
 
 class Layout:
-    def __init__(self, s, inner):
+    def __init__(self, inner, units):
+        self.units = units
         self.attend_out = 0
         self.attend_in = inner
         self.down = 4 * inner
-        self.up = 4 * inner + s.units
-        self.cross_out = 4 * inner + 2 * s.units
-        self.total = 5 * inner + 2 * s.units
+        self.up = 4 * inner + units
+        self.cross_out = 4 * inner + 2 * units
+        self.cross_in = 5 * inner + 2 * units
+        self.total = 8 * inner + 2 * units
 
 
 def lane(start, size=TILE):
@@ -229,8 +231,7 @@
     v: Any
     pair_k: Any
     pair_v: Any
-    back_k: Any
-    back_v: Any
+    back: Any
     cross_prob: Any
     self_prob: Any
     context: Any
@@ -250,9 +251,7 @@
     q2: Any
     k2: Any
     v2: Any
-    d1: Any
-    d2: Any
-    d3: Any
+    d: Any
     low_grad: Any
     grad_context: Any
     layer_rows: Any
@@ -301,6 +300,7 @@
     send_s: Any
     recv_s: Any
     free: Any
+    zero_sem: Any
 
 
 class Plan(NamedTuple):
@@ -317,15 +317,16 @@
     ring: Any
     lags: Any
     when: Any
-
-
-def layer_kernel(settings, layouts, plan, *refs):
+    forward: Any
+
+
+def layer_kernel(settings, layout, plan, *refs):
     first, second = len(Inputs._fields), len(Inputs._fields) + len(Results._fields)
     r = Refs(Inputs(*refs[:first]), Results(*refs[first:second]), Scratch(*refs[second:]))
     side = lax.axis_index("stream")
     greet(plan, r)
     for which, s in enumerate(settings):
-        pl.when(side == which)(partial(run_stream, which, s, layouts[which], plan, r))
+        pl.when(side == which)(partial(run_stream, which, s, layout, plan, r))
 
 
 def peer_of(plan, offset):
@@ -346,6 +347,61 @@
     pl.semaphore_signal(barrier, inc=1, device_id={"stream": 1 - lax.axis_index("stream")},
                         device_id_type=MESH)
     pl.semaphore_wait(barrier, count)
+
+
+class Piece(NamedTuple):
+    own: Any
+    gathered: Any
+    every: Any
+    whole: Any
+    ref: Any
+    full: Any
+    held: Any
+    place: Any
+
+
+def pieces_of(s, plan, r):
+    w, u, inner, groups = s.width, s.units, plan.inner, plan.groups
+    pieces, named = [], {}
+
+    def add(name, ref, full, held, cut, whole, place):
+        named.setdefault(name, []).append(len(pieces))
+        pieces.append(Piece(
+            lambda part: cut(ref, (), part), lambda z, part: cut(full, (z,), part),
+            lambda part: cut(full, (slice(None),), part), whole, ref, full, held, place))
+
+    def matrix(name, b, ref, full):
+        add(name, ref, full, r.w_in,
+            lambda a, at, part: a.at[at + (b, pl.ds(part * (w // 4), w // 4), slice(None))],
+            lambda a: [a.at[b, pl.ds(0, w), :]],
+            lambda z: [pl.ds(pl.multiple_of((z * 3 + b) * w, TILE), w)])
+
+    def rows(name, j, size, ref, full, held):
+        add(name, ref, full, held,
+            lambda a, at, part: a.at[
+                at + (pl.ds(j * TILE + part * (TILE // 4), TILE // 4), pl.ds(0, w))],
+            lambda a: [a.at[pl.ds(j * TILE, TILE), pl.ds(b * TILE, TILE)] for b in range(s.parts)],
+            lambda z: [pl.ds(pl.multiple_of((b * groups + z) * size + j * TILE, TILE), TILE)
+                       for b in range(s.parts)])
+
+    def columns(name, j, ref, full, held):
+        add(name, ref, full, held,
+            lambda a, at, part: a.at[at + (pl.ds(part * (w // 4), w // 4), pl.ds(j * TILE, TILE))],
+            lambda a: [a.at[pl.ds(0, w), pl.ds(j * TILE, TILE)]],
+            lambda z: [pl.ds(pl.multiple_of((z * (u // TILE) + j) * w, TILE), w)])
+
+    matrix("k", 1, r.cross_in, r.f_cross_in)
+    matrix("v", 2, r.cross_in, r.f_cross_in)
+    matrix("q", 0, r.cross_in, r.f_cross_in)
+    rows("cross_out", 0, inner, r.cross_out, r.f_cross_out, r.w_cross_out)
+    for j in range(u // TILE):
+        columns("up", j, r.up, r.f_up, r.w_up)
+    for j in range(u // TILE):
+        rows("down", j, u, r.down, r.f_down, r.w_down)
+    for b in range(3):
+        matrix("attend_in", b, r.attend_in, r.f_attend_in)
+    rows("attend_out", 0, inner, r.attend_out, r.f_attend_out, r.w_attend_out)
+    return pieces, named
 
 
 class Gather:
@@ -358,42 +414,20 @@
         self.to_y = {"dp": (self.quarter ^ 2) * stride + base}
         self.to_c = {"dp": (self.quarter ^ 1) * stride + base}
         self.at_end = jnp.logical_or(self.z == 0, self.z == self.groups - 1)
-        w, u, inner = s.width, s.units, plan.inner
-
-        def projection(ref, part):
-            return ref.at[:, pl.ds(part * (w // 4), w // 4), :]
-
-        def leave(ref, part):
-            return ref.at[pl.ds(part * (inner // 4), inner // 4), pl.ds(0, w)]
-
-        def enter(ref, part):
-            return ref.at[pl.ds(part * (w // 4), w // 4), pl.ds(0, u)]
-
-        def fall(ref, part):
-            return ref.at[pl.ds(part * (u // 4), u // 4), pl.ds(0, w)]
-
-        self.pieces = [
-            (r.cross_in, r.f_cross_in, projection),
-            (r.cross_out, r.f_cross_out, leave),
-            (r.up, r.f_up, enter),
-            (r.down, r.f_down, fall),
-            (r.attend_in, r.f_attend_in, projection),
-            (r.attend_out, r.f_attend_out, leave),
-        ]
+        self.pieces, self.named = pieces_of(s, plan, r)
 
     def z_copy(self, p, way, hop):
         step = 1 - 2 * way
         origin = self.z - hop * step
-        source, full, cut = self.pieces[p]
-        dst = cut(full.at[origin], self.quarter)
-        src = cut(source, self.quarter) if hop == 0 else dst
+        piece = self.pieces[p]
+        dst = piece.gathered(origin, self.quarter)
+        src = piece.own(self.quarter) if hop == 0 else dst
         return pltpu.make_async_remote_copy(
             src, dst, self.r.send_gz.at[p, way, hop], self.r.recv_gz.at[p, way, hop],
             device_id={"mp": self.z + step}, device_id_type=MESH)
 
     def block(self, p, way, hop, whose):
-        source, full, cut = self.pieces[p]
-        return cut(full.at[self.z - (hop + 1) * (1 - 2 * way)], whose)
+        return self.pieces[p].gathered(self.z - (hop + 1) * (1 - 2 * way), whose)
 
     def z_arrival(self, p, way, hop):
         block = self.block(p, way, hop, self.quarter)
@@ -407,12 +441,12 @@
             block, block, self.r.send_gy.at[p, way, hop], self.r.recv_gy.at[p, way, hop],
             device_id=self.to_y, device_id_type=MESH)
 
-    def c_copy(self, p, way, hop, which, mine=True):
+    def c_copy(self, p, which, mine=True):
         whose = (self.quarter if mine else self.quarter ^ 1) ^ (2 * which)
-        block = self.block(p, way, hop, whose)
+        block = self.pieces[p].every(whose)
         return pltpu.make_async_remote_copy(
-            block, block, self.r.send_gc.at[p, way, hop, which],
-            self.r.recv_gc.at[p, way, hop, which], device_id=self.to_c, device_id_type=MESH)
+            block, block, self.r.send_gc.at[p, which], self.r.recv_gc.at[p, which],
+            device_id=self.to_c, device_id_type=MESH)
 
     def sends(self, way, hop):
         last = self.groups - 1
@@ -438,9 +472,23 @@
         for p in range(ahead, len(self.pieces)):
             pl.when(self.at_end)(partial(self.own, p))
 
-    def later(self, p):
-        if p < len(self.pieces):
-            pl.when(jnp.logical_not(self.at_end))(partial(self.own, p))
+    def wave(self, i, ahead):
+        count, last = len(self.pieces), self.groups - 2
+        for hop in range(self.groups - 1):
+            if 0 <= i - hop < count:
+                self.received(i - hop, hop)
+        if 0 <= i - last < count:
+            self.c_copy(i - last, 0).start()
+        if i + ahead < count:
+            pl.when(jnp.logical_not(self.at_end))(partial(self.own, i + ahead))
+        for hop in range(self.groups - 1):
+            if 0 <= i - hop - 1 < count:
+                self.shared(i - hop - 1, hop)
+        if 0 <= i - last - 1 < count:
+            self.c_copy(i - last - 1, 1).start()
+
+    def waves(self):
+        return len(self.pieces) + self.groups - 1
 
     def received(self, p, *hops):
         def action(way, hop):
@@ -448,87 +496,70 @@
             if hop + 1 < self.groups - 1:
                 pl.when(self.sends(way, hop + 1))(lambda: self.z_copy(p, way, hop + 1).start())
             self.y_copy(p, way, hop).start()
-            self.c_copy(p, way, hop, 0).start()
 
         self.each(self.arrives, action, hops or None)
 
     def shared(self, p, *hops):
         def action(way, hop):
             self.y_copy(p, way, hop, mine=False).wait_recv()
-            self.c_copy(p, way, hop, 1).start()
 
         self.each(self.arrives, action, hops or None)
 
-    def settled(self, p, weights, name, *hops):
-        def action(way, hop):
-            for which in range(2):
-                self.c_copy(p, way, hop, which, mine=False).wait_recv()
-            for item in weights.copies(name, self.z - (hop + 1) * (1 - 2 * way), False):
-                item.start()
-
-        self.each(self.arrives, action, hops or None)
+    def settled(self, weights, *names):
+        for name in names:
+            for p in self.named[name]:
+                for which in range(2):
+                    self.c_copy(p, which, mine=False).wait_recv()
+
+                def action(way, hop):
+                    for item in weights.copies(p, self.z - (hop + 1) * (1 - 2 * way), False):
+                        item.start()
+
+                self.each(self.arrives, action)
 
     def drained(self, p):
         self.each(self.sends, lambda way, hop: self.z_copy(p, way, hop).wait_send())
 
-        def action(way, hop):
-            self.y_copy(p, way, hop).wait_send()
-            for which in range(2):
-                self.c_copy(p, way, hop, which).wait_send()
-
-        self.each(self.arrives, action)
+        self.each(self.arrives, lambda way, hop: self.y_copy(p, way, hop).wait_send())
+        for which in range(2):
+            self.c_copy(p, which).wait_send()
 
 
 class Weights:
     def __init__(self, s, plan, r):
-        self.s, self.r, self.plan = s, r, plan
+        self.r, self.groups = r, plan.groups
         self.z = lax.axis_index("mp")
-        w, u, inner, groups = s.width, s.units, plan.inner, plan.groups
-        self.kinds = {
-            "cross_in": (0, r.cross_in, r.f_cross_in, r.w_in, 3),
-            "cross_out": (1, r.cross_out, r.f_cross_out, r.w_cross_out, s.parts),
-            "up": (2, r.up, r.f_up, r.w_up, u // TILE),
-            "down": (3, r.down, r.f_down, r.w_down, s.parts),
-            "attend_in": (4, r.attend_in, r.f_attend_in, r.w_in, 3),
-            "attend_out": (5, r.attend_out, r.f_attend_out, r.w_attend_out, s.parts),
-        }
-
-    def copies(self, name, z, own):
-        number, arg, full, held, blocks = self.kinds[name]
-        source = arg if own else full.at[z]
-        s, groups, inner = self.s, self.plan.groups, self.plan.inner
-        for b in range(blocks):
-            if name in ("cross_in", "attend_in"):
-                src = source.at[b, pl.ds(0, s.width), :]
-                row, size = (z * 3 + b) * s.width, s.width
-            elif name == "up":
-                src = source.at[pl.ds(0, s.width), pl.ds(b * TILE, TILE)]
-                row, size = (z * blocks + b) * s.width, s.width
-            else:
-                size = s.units if name == "down" else inner
-                src = source.at[pl.ds(0, size), pl.ds(b * TILE, TILE)]
-                row = (b * groups + z) * size
-            yield pltpu.make_async_copy(
-                src, held.at[pl.ds(pl.multiple_of(row, TILE), size)], self.r.weight_sem.at[number, z, b])
-
-    def load(self, name, which="all"):
-        for z in range(self.plan.groups):
-            if which in ("all", "own"):
-                @pl.when(self.z == z)
-                def _():
-                    for item in self.copies(name, z, True):
-                        item.start()
-
-            if which in ("all", "rest"):
-                @pl.when(self.z != z)
-                def _():
-                    for item in self.copies(name, z, False):
-                        item.start()
-
-    def wait(self, name):
-        for z in range(self.plan.groups):
-            for item in self.copies(name, z, False):
-                item.wait()
+        self.pieces, self.named = pieces_of(s, plan, r)
+
+    def copies(self, p, z, own):
+        piece = self.pieces[p]
+        blocks = piece.whole(piece.ref if own else piece.full.at[z])
+        for b, (src, rows) in enumerate(zip(blocks, piece.place(z))):
+            yield pltpu.make_async_copy(src, piece.held.at[rows], self.r.weight_sem.at[p, z, b])
+
+    def load_own(self, *names):
+        for name in names:
+            for p in self.named[name]:
+                for item in self.copies(p, self.z, True):
+                    item.start()
+
+    def load_rest(self, *names):
+        for name in names:
+            for p in self.named[name]:
+                @pl.loop(0, self.groups)
+                def _(z):
+                    @pl.when(self.z != z)
+                    def _():
+                        for item in self.copies(p, z, False):
+                            item.start()
+
+    def wait(self, *names):
+        for name in names:
+            for p in self.named[name]:
+                @pl.loop(0, self.groups)
+                def _(z):
+                    for item in self.copies(p, z, False):
+                        item.wait()
 
 
 class Outputs:
@@ -561,8 +592,14 @@
     def arrives(self, way, hop):
         return self.z >= hop + 1 if way == 0 else self.z <= self.last - 1 - hop
 
-    def step(self, which, k):
-        for hop in range(self.groups):
+    def begin(self, which):
+        @pl.loop(0, self.cuts)
+        def _(k):
+            for way in range(2):
+                pl.when(self.sends(way, 0))(lambda: self.copy(which, k, way, 0).start())
+
+    def step(self, which, k, begun=False):
+        for hop in range(1 if begun else 0, self.groups):
             now = k - hop
 
             @pl.when(jnp.logical_and(now >= 0, now < self.cuts))
@@ -605,7 +642,11 @@
         self.text = which == 0
         self.r, self.groups, self.chunk = r, plan.groups, plan.chunk
         self.slots, self.lags = plan.slots, plan.lags
-        self.count = (layout.total + 3 * plan.inner) // self.chunk
+        self.inner, self.used = plan.inner, s.lanes // self.chunk
+        self.narrow = 4 * self.used
+        self.feed = s.units // self.chunk
+        self.layout = layout
+        self.count = self.narrow + 2 * self.feed + plan.inner // self.chunk * 4
         stride, copy = plan.copies // 4, lax.axis_index("dp")
         quarter = lax.rem(copy // stride, 4)
         base = lax.rem(copy, stride)
@@ -628,7 +669,14 @@
         return pl.multiple_of((2 * y + core) * TILE, 128)
 
     def rows(self, i):
-        return pl.ds(pl.multiple_of(i * self.chunk, self.chunk), self.chunk)
+        early = (i // self.used) * self.inner + lax.rem(i, self.used) * self.chunk
+        n = i - self.narrow
+        late = jnp.where(
+            n < self.feed, self.layout.down + n * self.chunk,
+            jnp.where(n < 2 * self.feed, self.layout.up + (n - self.feed) * self.chunk,
+                      self.layout.cross_out + (n - 2 * self.feed) * self.chunk))
+        start = jnp.where(i < self.narrow, early, late)
+        return pl.ds(pl.multiple_of(start, self.chunk), self.chunk)
 
     def slot(self, i):
         return lax.rem(i, self.slots)
@@ -819,6 +867,22 @@
 
         self.widths(action)
 
+    def zeros(self, s, zero):
+        blocks = [(4 * self.chunk * n + self.used * self.chunk, self.inner - self.used * self.chunk)
+                  for n in range(4)] if self.used * self.chunk < self.inner else []
+        for start in (self.layout.down, self.layout.up):
+            blocks += [(row, TILE) for row in range(start + s.units, start + self.layout.units, TILE)]
+        number = 0
+        for always, group in ((True, blocks), (False, [(row, TILE) for row in range(
+                0, self.layout.total, TILE)] if self.text else [])):
+            test = self.y + self.core == 2
+            for row, size in group:
+                yield (jnp.logical_not(test) if always and self.text else test if self.text
+                       else self.y >= 0, pltpu.make_async_copy(
+                    zero.at[pl.ds(0, size), pl.ds(0, TILE)],
+                    self.r.reduced.at[pl.ds(row, size)], self.r.zero_sem.at[number]))
+                number += 1
+
     def iteration(self, j):
         lag_b, lag_c, lag_z, lag_f = self.lags
 
@@ -932,9 +996,7 @@
              pltpu.make_async_copy(r.cotangent.at[own_rows], r.grad_out, r.enter_sem.at[1])]
     for item in enter:
         item.start()
-    weights.load("cross_in", "own")
-    for name in ("cross_out", "up", "down", "attend_out"):
-        weights.load(name, "own")
+    weights.load_own("k", "v", "q", "cross_out", "up", "down", "attend_out")
 
     def bias_copy(step, kind):
         ref, full = ((r.cross_bias, r.a_cross_bias), (r.attend_bias, r.a_attend_bias),
@@ -951,6 +1013,9 @@
         full[z] = ref[...]
 
     r.zero[...] = jnp.zeros_like(r.zero)
+    r.acc[:, :TILE] = jnp.zeros((tokens, TILE), wide)
+    for test, item in reduce.zeros(s, r.acc):
+        pl.when(test)(item.start)
 
     def swap(source, target, number):
         return pltpu.make_async_remote_copy(
@@ -987,14 +1052,26 @@
             r.acc[:, cols] = (dot(source[:, :size], weight[at, :]) + residual(cols)
                               + vector(r.out_bias, line, cols))
 
-    def norm(normal, inverse):
-        summed = r.acc[:, :w]
-        mean = jnp.sum(summed, axis=-1, keepdims=True) * (1.0 / w)
-        centred = summed - mean
-        scale = lax.rsqrt(
-            jnp.sum(centred * centred, axis=-1, keepdims=True) * (1.0 / w) + norm_eps)
-        normal[:, :w] = centred * scale
-        inverse[...] = scale
+    strip = 64
+
+    def strips(action):
+        @pl.loop(0, tokens // strip)
+        def _(k):
+            action(pl.ds(pl.multiple_of(k * strip, strip), strip))
+
+    def norm(normal, inverse, line, low_out):
+        def action(at):
+            summed = r.acc[at, :w]
+            mean = jnp.sum(summed, axis=-1, keepdims=True) * (1.0 / w)
+            centred = summed - mean
+            scale = lax.rsqrt(
+                jnp.sum(centred * centred, axis=-1, keepdims=True) * (1.0 / w) + norm_eps)
+            normal[at, :w] = centred * scale
+            inverse[at, :] = scale
+            low_out[at, :w] = (
+                centred * scale * vector(r.gains, line) + vector(r.shifts, line)).astype(low)
+
+        strips(action)
 
     def cross_part(begin, end):
         @pl.loop(begin, end)
@@ -1014,62 +1091,65 @@
                 r.slope[:, cols] = bell + value * (
                     jnp.exp(-0.5 * value * value) * (1.0 / math.sqrt(2.0 * math.pi)))
 
-    gather.received(0)
-    gather.later(2)
-    gather.received(1)
-    gather.later(3)
-    gather.shared(0)
-    gather.received(2, 0, 1)
-    for kind in range(3):
-        for step in range(1, groups):
-            bias_copy(step, kind).wait()
-    for item in enter:
-        item.wait()
-    gather.settled(0, weights, "cross_in")
-    gather.received(2, 2)
-    gather.later(4)
-    gather.shared(1)
-    weights.wait("cross_in")
-    project(1, r.x, r.k, None, None)
-    swap(r.k, r.pair_k, 0).start()
-    project(2, r.x, r.v, r.a_cross_bias, 1)
-    swap(r.v, r.pair_v, 1).start()
-    gather.received(3, 0, 1)
-    project(0, r.x, r.q, r.a_cross_bias, 0)
-    weights.load("attend_in", "own")
-    gather.settled(1, weights, "cross_out")
-    gather.received(3, 2)
-    gather.later(5)
-    gather.shared(2)
-    gather.settled(2, weights, "up")
-    gather.received(4, 0, 1)
-    swap(r.k, r.pair_k, 0).wait()
-    swap(r.v, r.pair_v, 1).wait()
-    cross_part(0, groups // 2)
-    gather.received(5, 0)
-    cross_part(groups // 2, groups)
-    gather.received(4, 2)
-    gather.received(5, 1)
-    gather.shared(3)
-    gather.settled(3, weights, "down")
-    weights.wait("cross_out")
-    leave(r.context, groups * inner, r.w_cross_out, lambda cols: r.x[:, cols].astype(wide), 0)
-    norm(r.n1, r.r1)
-    r.h1[:, :w] = scaled(r.n1, 0, slice(0, w)).astype(low)
-    gather.received(5, 2)
-    gather.shared(4, 0, 1)
-    weights.wait("up")
-    feed_part(0, groups // 2)
-    gather.shared(4, 2)
-    gather.settled(4, weights, "attend_in", 0, 1)
-    feed_part(groups // 2, groups)
-    gather.shared(5)
-    gather.settled(4, weights, "attend_in", 2)
-    gather.settled(5, weights, "attend_out")
+    def do_key():
+        gather.settled(weights, "k")
+        for item in enter:
+            item.wait()
+        weights.wait("k")
+        project(1, r.x, r.k, None, None)
+        swap(r.k, r.pair_k, 0).start()
+
+    def do_value():
+        gather.settled(weights, "v")
+        for kind in range(3):
+            for step in range(1, groups):
+                bias_copy(step, kind).wait()
+        weights.wait("v")
+        project(2, r.x, r.v, r.a_cross_bias, 1)
+        swap(r.v, r.pair_v, 1).start()
+
+    def do_query():
+        gather.settled(weights, "q")
+        weights.wait("q")
+        project(0, r.x, r.q, r.a_cross_bias, 0)
+        weights.load_own("attend_in")
+
+    def do_cross_first():
+        gather.settled(weights, "cross_out")
+        swap(r.k, r.pair_k, 0).wait()
+        swap(r.v, r.pair_v, 1).wait()
+        cross_part(0, groups // 2)
+
+    def do_cross_second():
+        cross_part(groups // 2, groups)
+        gather.settled(weights, "up")
+
+    def do_first_norm():
+        for test, item in reduce.zeros(s, r.acc):
+            pl.when(test)(item.wait)
+        weights.wait("cross_out")
+        leave(r.context, groups * inner, r.w_cross_out, lambda cols: r.x[:, cols].astype(wide), 0)
+        norm(r.n1, r.r1, 0, r.h1)
+
+    def do_feed_first():
+        weights.wait("up")
+        feed_part(0, groups // 2)
+        gather.settled(weights, "down")
+
+    def do_feed_second():
+        feed_part(groups // 2, groups)
+
+    work = dict(zip(plan.forward[which], (
+        do_key, do_value, do_query, do_cross_first, do_cross_second, do_first_norm,
+        do_feed_first, do_feed_second)))
+    for i in range(gather.waves() + 1):
+        gather.wave(i, 2)
+        if i in work:
+            work[i]()
     weights.wait("down")
     leave(r.active, groups * u, r.w_down, lambda cols: scaled(r.n1, 0, cols), 1)
-    norm(r.n2, r.r2)
-    r.h2[:, :w] = scaled(r.n2, 1, slice(0, w)).astype(low)
+    norm(r.n2, r.r2, 1, r.h2)
+    gather.settled(weights, "attend_in", "attend_out")
     weights.wait("attend_in")
     project(0, r.h2, r.q2, r.a_attend_bias, 0)
     project(1, r.h2, r.k2, None, None)
@@ -1082,41 +1162,42 @@
 
     weights.wait("attend_out")
     leave(r.context2, groups * inner, r.w_attend_out, lambda cols: scaled(r.n2, 1, cols), 2)
-    norm(r.n3, r.r3)
-    r.layer_rows[:, :w] = scaled(r.n3, 2, slice(0, w)).astype(low)
+    norm(r.n3, r.r3, 2, r.layer_rows)
+    outputs.begin(0)
     for item in outputs.local(0):
         item.start()
     for p in range(len(gather.pieces)):
         gather.drained(p)
 
-    def stores(row):
-        return [
-            pltpu.make_async_copy(
-                r.staged.at[g, :, pl.ds(0, w)],
-                r.grads.at[g, pl.ds(pl.multiple_of(row, TILE), TILE), pl.ds(0, w)],
-                r.store_sem.at[g])
-            for g in range(groups)]
+    def store(row, g):
+        return pltpu.make_async_copy(
+            r.staged.at[g, :, pl.ds(0, w)],
+            r.grads.at[g, pl.ds(pl.multiple_of(row, TILE), TILE), pl.ds(0, w)],
+            r.store_sem.at[g])
 
     def weight_grads(left, right, row, size):
         def step(k):
-            for g, item in enumerate(stores(row + k * TILE)):
-                r.staged[g, :, :w] = dot_tn(
-                    left[:, lane(g * size + k * TILE)], right[:, :w]).astype(low)
-                item.start()
+            @pl.loop(0, groups)
+            def _(g):
+                r.staged[g, :, :w] = dot_tn(left(lane(g * size + k * TILE)), right[:, :w]).astype(low)
+                store(row + k * TILE, g).start()
 
         return step
 
     def flush():
-        for item in stores(0):
-            item.wait()
-
-    def back_norm(incoming, normal, inverse, line):
-        r.small_in[3 + line : 4 + line, :w] = down_sum(incoming * normal[:, :w])
-        r.small_in[6 + line : 7 + line, :w] = down_sum(incoming)
-        out = norm_back(normal[:, :w], inverse[...], vector(r.gains, line), incoming, w)
-        r.acc[:, :w] = out
-        r.low_grad[:, :w] = out.astype(low)
-        r.small_in[line : line + 1, :w] = down_sum(out.astype(low).astype(wide))
+        pl.loop(0, groups)(lambda g: store(0, g).wait())
+
+    def back_norm(source, normal, inverse, line):
+        def action(at):
+            incoming = source[at, :w].astype(wide)
+            r.small_in[3 + line : 4 + line, :w] += down_sum(incoming * normal[at, :w])
+            r.small_in[6 + line : 7 + line, :w] += down_sum(incoming)
+            out = norm_back(normal[at, :w], inverse[at, :], vector(r.gains, line), incoming, w)
+            r.acc[at, :w] = out
+            r.low_grad[at, :w] = out.astype(low)
+            r.small_in[line : line + 1, :w] += down_sum(out.astype(low).astype(wide))
+
+        strips(action)
 
     def leave_back(weight, size, row, count):
         total = None
@@ -1144,17 +1225,18 @@
 
     def self_step(g):
         attend_backward(g, self_kinds, self_scale, length, rows_dev, r.q2, r.k2, r.v2,
-                        r.self_prob, r.grad_context, r.d1, r.d2, r.d3)
+                        r.self_prob, r.grad_context, r.d.at[0], r.d.at[1], r.d.at[2])
 
     def cross_step(g):
         attend_backward(g, cross_kinds, cross_scale, length, rows_dev, r.q, r.pair_k, r.pair_v,
-                        r.cross_prob, r.grad_context, r.d1, r.d2, r.d3)
+                        r.cross_prob, r.grad_context, r.d.at[0], r.d.at[1], r.d.at[2])
 
     def second_norm(_):
-        r.small_in[12:13, :] = down_sum(r.d1[...].astype(wide))
-        r.small_in[13:14, :] = down_sum(r.d3[...].astype(wide))
-        weights.load("cross_in")
-        back_norm(r.acc[:, :w], r.n2, r.r2, 1)
+        r.small_in[12:13, :] = down_sum(r.d[0].astype(wide))
+        r.small_in[13:14, :] = down_sum(r.d[2].astype(wide))
+        weights.load_own("q", "k", "v")
+        weights.load_rest("q", "k", "v")
+        back_norm(r.acc, r.n2, r.r2, 1)
 
     def slope_step(g):
         for j in range(u // TILE):
@@ -1163,7 +1245,7 @@
             r.dz[:, cols] = (value * r.slope[:, cols]).astype(low)
 
     def first_norm(_):
-        back_norm(r.acc[:, :w], r.n1, r.r1, 0)
+        back_norm(r.acc, r.n1, r.r1, 0)
         units, width = plan.units, r.small_in.shape[1]
         for g in range(groups):
             for j in range(u // TILE):
@@ -1173,15 +1255,15 @@
                     r.dz[:, g * u + j * TILE : g * u + (j + 1) * TILE].astype(wide))
 
     def pair_send(_):
-        r.small_in[14:15, :] = down_sum(r.d1[...].astype(wide))
-        weights.wait("cross_in")
-        swap(r.d2, r.back_k, 2).start()
-        swap(r.d3, r.back_v, 3).start()
+        r.small_in[14:15, :] = down_sum(r.d[0].astype(wide))
+        weights.wait("q", "k", "v")
+        swap(r.d.at[1], r.back.at[0], 2).start()
+        swap(r.d.at[2], r.back.at[1], 3).start()
 
     def pair_take(_):
-        swap(r.d2, r.back_k, 2).wait()
-        swap(r.d3, r.back_v, 3).wait()
-        r.small_in[15:16, :] = down_sum(r.back_v[...].astype(wide))
+        swap(r.d.at[1], r.back.at[0], 2).wait()
+        swap(r.d.at[2], r.back.at[1], 3).wait()
+        r.small_in[15:16, :] = down_sum(r.back[1].astype(wide))
         small.start()
 
     def hidden_store(_):
@@ -1190,42 +1272,42 @@
             item.start()
 
     def attend_grads(k):
-        for which_one, d in enumerate((r.d1, r.d2, r.d3)):
-            pl.when(k == which_one)(lambda: weight_grads(
-                d, r.h2, layout.attend_in + which_one * inner, inner)(0))
+        weight_grads(lambda cols: r.d[k, :, cols], r.h2, layout.attend_in + k * inner, inner)(0)
 
     def cross_grads(k):
-        for which_one, d in enumerate((r.back_k, r.back_v)):
-            pl.when(k == which_one)(lambda: weight_grads(
-                d, r.x, layout.total + (1 + which_one) * inner, inner)(0))
+        weight_grads(lambda cols: r.back[k, :, cols], r.x,
+                     layout.cross_in + (1 + k) * inner, inner)(0)
+
+    def of(ref):
+        return lambda cols: ref[:, cols]
 
     r.small_in[...] = jnp.zeros_like(r.small_in)
-    back_norm(r.grad_out[:, :w].astype(wide), r.n3, r.r3, 2)
+    back_norm(r.grad_out, r.n3, r.r3, 2)
     pl.loop(0, groups)(context_back(r.w_attend_out))
-    weight_grads(r.context2, r.low_grad, layout.attend_out, inner)(0)
+    weight_grads(of(r.context2), r.low_grad, layout.attend_out, inner)(0)
     nb = u // TILE
     take = plan.when[which]
     schedule = (
         (0, 4, 2, False, self_step),
         (2, 3, 1, True, attend_grads),
-        (2, 4, 2, False, enter_back(lambda g: [(d, g * inner) for d in (r.d1, r.d2, r.d3)],
+        (2, 4, 2, False, enter_back(lambda g: [(d, g * inner) for d in (r.d.at[0], r.d.at[1], r.d.at[2])],
                                     r.w_in, 3)),
         (4, 1, 1, False, second_norm),
         (5, 4, 2, False, slope_step),
-        (5, nb, 1, True, weight_grads(r.active, r.low_grad, layout.down, u)),
-        (5 + nb, nb, 1, True, weight_grads(r.dz, r.h1, layout.up, u)),
+        (5, nb, 1, True, weight_grads(of(r.active), r.low_grad, layout.down, u)),
+        (5 + nb, nb, 1, True, weight_grads(of(r.dz), r.h1, layout.up, u)),
         (7, 4, 2, False, enter_back(lambda g: [(r.dz, g * u + b * TILE) for b in range(nb)],
                                     r.w_up, nb)),
         (9, 1, 1, False, first_norm),
         (10, 4, 2, False, context_back(r.w_cross_out)),
         (12, 4, 2, False, cross_step),
         (14, 1, 1, False, pair_send),
-        (11, 1, 1, True, weight_grads(r.context, r.low_grad, layout.cross_out, inner)),
-        (15, 1, 1, True, weight_grads(r.d1, r.x, layout.total, inner)),
+        (11, 1, 1, True, weight_grads(of(r.context), r.low_grad, layout.cross_out, inner)),
+        (15, 1, 1, True, weight_grads(of(r.d.at[0]), r.x, layout.cross_in, inner)),
         (take, 1, 1, False, pair_take),
         (take, 2, 1, True, cross_grads),
         (take + 2, 4, 2, False, enter_back(
-            lambda g: [(d, g * inner) for d in (r.d1, r.back_k, r.back_v)], r.w_in, 3)),
+            lambda g: [(d, g * inner) for d in (r.d.at[0], r.back.at[0], r.back.at[1])], r.w_in, 3)),
         (take + 4, 1, 1, False, hidden_store),
         (take + 5, 1, 1, False, lambda _: small.middle()),
     )
@@ -1248,7 +1330,7 @@
                 else:
                     pl.loop(0, per)(lambda n: step((j - start) * per + n))
         reduce.iteration(j)
-        outputs.step(0, j - 1)
+        outputs.step(0, j, True)
         outputs.step(1, j - hidden_at)
 
     reduce.drained()
@@ -1279,7 +1361,6 @@
     side = lax.axis_index("stream")
     member = lax.axis_index("mp")
     copy = lax.axis_index("dp")
-    is_image = side == 1
     inner = cross_in.shape[3]
     padded = hidden.shape[2]
     units = up_weight.shape[2]
@@ -1287,8 +1368,8 @@
     text = Setting(TEXT_WIDTH, TEXT_HEADS, TEXT_FF, groups)
     image = Setting(IMAGE_WIDTH, IMAGE_HEADS, IMAGE_FF, groups)
     settings = (text, image)
-    layouts = [Layout(s, inner) for s in settings]
-    rows_max = max(layout.total for layout in layouts) + 3 * inner
+    layout = Layout(inner, units)
+    rows_max = layout.total
     rows_dev = segments.shape[1] // groups
     tokens = hidden.shape[1] // groups
     co = groups * inner
@@ -1314,7 +1395,7 @@
     widest = max(s.units for s in settings) * groups
     up_rows = max(groups * s.units * s.width for s in settings) // TILE
     heads = max(groups * s.per_group for s in settings)
-    pieces, hops = 6, groups - 1
+    pieces, hops = 8 + 2 * max(s.units for s in settings) // TILE, groups - 1
     peers = groups * copies
     small_width = padded // max(1, peers // 16)
     scratch = Scratch(
@@ -1330,8 +1411,7 @@
         v=short(tokens, co),
         pair_k=short(tokens, co),
         pair_v=short(tokens, co),
-        back_k=short(tokens, co),
-        back_v=short(tokens, co),
+        back=short(2, tokens, co),
         cross_prob=real(CO_HEADS * rows_dev, length, length),
         self_prob=real(heads * rows_dev, length, length),
         context=short(tokens, co),
@@ -1351,9 +1431,7 @@
         q2=short(tokens, co),
         k2=short(tokens, co),
         v2=short(tokens, co),
-        d1=short(tokens, co),
-        d2=short(tokens, co),
-        d3=short(tokens, co),
+        d=short(3, tokens, co),
         low_grad=short(tokens, padded),
         grad_context=short(tokens, co),
         layer_rows=short(tokens, padded),
@@ -1377,8 +1455,8 @@
         recv_gz=dma((pieces, 2, hops)),
         send_gy=dma((pieces, 2, hops)),
         recv_gy=dma((pieces, 2, hops)),
-        send_gc=dma((pieces, 2, hops, 2)),
-        recv_gc=dma((pieces, 2, hops, 2)),
+        send_gc=dma((pieces, 2)),
+        recv_gc=dma((pieces, 2)),
         weight_sem=dma((pieces, groups, 4)),
         enter_sem=dma((2,)),
         send_b=dma((3, groups)),
@@ -1402,12 +1480,14 @@
         send_s=dma((2, peers)),
         recv_s=dma((2, peers)),
         free=pltpu.SemaphoreType.REGULAR((5,)),
+        zero_sem=dma((4 + rows_max // TILE,)),
     )
     plan = Plan(
         groups=groups, copies=copies, inner=inner, length=length, rows=rows_dev,
         tokens=tokens, units=units, chunk=chunk, slots=slots, cuts=cuts,
         ring=ring, lags=(3, 8, 2, 2),
         when=(26, 24),
+        forward=((4, 5, 6, 10, 11, 12, 13, 14), (4, 5, 6, 8, 9, 10, 11, 12)),
     )
     weights = (
         jnp.swapaxes(cross_in[0], 0, 1),
@@ -1419,7 +1499,7 @@
     )
     line = shape((groups, tokens, padded))
     out = pl.pallas_call(
-        partial(layer_kernel, settings, layouts, plan),
+        partial(layer_kernel, settings, layout, plan),
         out_shape=(
             line, line, shape((rows_max, TILE), wide), shape((16, padded), wide),
         ) + tuple(shape((groups,) + w.shape) for w in weights)
@@ -1441,9 +1521,6 @@
             reduced.astype(low), "dp", scatter_dimension=1, axis_index_groups=teams, tiled=True
         ).astype(wide)
     columns = padded // copies
-    real_block = copy * columns < jnp.where(is_image, IMAGE_WIDTH, TEXT_WIDTH)
-    reduced = jnp.where(real_block, reduced, 0.0)
-
     part = inner // copies
     vector_grads = lax.dynamic_slice_in_dim(small[:9], copy * columns, columns, 1)
     up_bias_grad = lax.dynamic_slice_in_dim(
@@ -1452,24 +1529,14 @@
     pair_grads = lax.dynamic_slice_in_dim(
         small[12:16], (member * copies + copy) * part, part, 1)
 
-    def unpack(s, layout, reduced):
-        u = s.units
-
-        def turned(start):
-            block = reduced[start : start + 3 * inner].reshape(3, inner, columns)
-            return block.transpose(2, 0, 1)
-
-        return (
-            turned(layout.total),
-            reduced[layout.cross_out : layout.cross_out + inner],
-            jnp.pad(reduced[layout.up : layout.up + u].T, ((0, 0), (0, units - u))),
-            jnp.pad(reduced[layout.down : layout.down + u], ((0, units - u), (0, 0))),
-            turned(layout.attend_in),
-            reduced[layout.attend_out : layout.attend_out + inner],
-        )
-
-    g_cross_in, g_cross_out, g_up, g_down, g_attend_in, g_attend_out = lax.cond(
-        is_image, partial(unpack, image, layouts[1]), partial(unpack, text, layouts[0]), reduced)
+    def turned(start):
+        return reduced[start : start + 3 * inner].reshape(3, inner, columns).transpose(2, 0, 1)
+
+    g_cross_in, g_attend_in = turned(layout.cross_in), turned(layout.attend_in)
+    g_cross_out = reduced[layout.cross_out : layout.cross_out + inner]
+    g_attend_out = reduced[layout.attend_out : layout.attend_out + inner]
+    g_up = reduced[layout.up : layout.up + units].T
+    g_down = reduced[layout.down : layout.down + units]
     return (
         layer_out.reshape(1, groups * tokens, padded),
         hidden_grad.reshape(1, groups * tokens, padded),

time: 349 us -> 304 us (0.87); the launches traced: 342 us -> 304 us
  Pallas kernels: 323 us -> 286 us
    pallas_call x1, Pallas kernels: 323 us -> 286 us  [shards(): pl.pallas_call(partial(layer_kernel, settings, layout, plan), out_shape=(...]
    cond x5 -> x0, local copies, waits for them, and re-layouts: 5.23 us -> none
where the time goes in v3:
time: 304 us
  Pallas kernels  286 us (94%)
  local copies, waits for them, and re-layouts  15.9 us (5%)
    pallas_call x1, Pallas kernels, shards(): pl.pallas_call(partial(layer_kernel, settings, layout, plan), out_shape=(...  286 us
    unnamed x12, local copies, waits for them, and re-layouts  6.56 us

profile of v3, /device:TPU:0, one launch (start us, length us, event | category | flops | bytes accessed | tf_op | source)
XLA Modules:
  0.0 303.7 jit_solution(6030202145418239528)
XLA Ops:
  0.7 0.7 fusion.2
  1.4 0.8 fusion.1
  2.2 286.4 %layer.1 = (bf16[4,256,1024]{2,1,0:T(8,128)(2,1)}, bf16[4,256,1024]{2,1,0:T(8,128)(2,1)}, f32[3584,256]{1,0:T(8,128)}, f32[16,1024]{1,0:T(8,128)}, bf16[4,3,1024...) custom-call(bf16[3,1024,256]{2,1,0:T(8,128)(2,1)} %bitcast.68, ...), custom_call_target="tpu_custom_call" | custom-call | tf_op jit(solution)/shard_map/layer/pallas_call | solution.py:1501
  288.6 3.0 %fusion.4 = (f32[768,256]{1,0:T(8,128)S(1)}, f32[1,768,256]{2,1,0:T(8,128)}, f32[1,256,768]{1,2,0:T(8,128)S(1)}, f32[768,256]{1,0:T(8,128)S(1)}) fusion(f32[3584,256]{1,0:T(8,128)} %get-tuple-element.20), kind=kLoop, calls=%fused_computation.18 | loop fusion | bytes 6291456 | tf_op jit(solution)/shard_map/slice | solution.py:1533
  291.6 1.1 copy.29
  292.8 0.0 copy-start.2
  292.8 1.1 copy.30
  293.9 0.0 copy-start.1
  293.9 1.1 copy.31
  295.1 1.9 slice_bitcast_fusion.2
  296.9 0.0 copy-done.2
  297.0 0.6 dynamic_slice.22
  297.6 0.1 constant_dynamic-slice_fusion
  297.7 0.6 slice_bitcast_fusion.4
  298.2 0.1 dynamic-slice_bitcast_fusion
  298.3 0.6 copy.32
  298.9 0.6 copy.33
  299.5 0.6 copy.34
  300.1 0.0 copy-done.1
  300.1 0.0 copy-start
  300.1 1.3 copy.37
  301.4 1.0 copy-done
  302.4 1.3 copy.38
  (3 shorter events, 0.0 us)
Async XLA Ops:
  292.8 4.2 %copy-start.2 = (f32[16,1024]{1,0:T(8,128)S(1)}, f32[16,1024]{1,0:T(8,128)}, u32[]{:S(2)}) copy-start(f32[16,1024]{1,0:T(8,128)} %get-tuple-element.21) | copy-start | bytes 196612
  293.9 6.2 %copy-start.1 = (bf16[4,256,1024]{2,1,0:T(8,128)(2,1)S(1)}, bf16[4,256,1024]{2,1,0:T(8,128)(2,1)}, u32[]{:S(2)}) copy-start(bf16[4,256,1024]{2,1,0:T(8,128)(2,1)} %get-tuple-element.18) | copy-start | bytes 6291460
  300.1 2.3 copy-start

commit v4 on v3

--- a/solution.py
+++ b/solution.py
@@ -23,9 +23,11 @@
 wide = jnp.float32
 ANY = pl.BlockSpec(memory_space=pl.ANY)
 VMEM = pl.BlockSpec(memory_space=pltpu.VMEM)
+HBM = pl.BlockSpec(memory_space=pltpu.HBM)
 MESH = pl.DeviceIdType.MESH
 VMEM_LIMIT = 65400 * 1024
 TILE = 256
+PACE = 3
 
 
 def dot(left, right):
@@ -353,6 +355,7 @@
     own: Any
     gathered: Any
     every: Any
+    sized: Any
     whole: Any
     ref: Any
     full: Any
@@ -364,29 +367,30 @@
     w, u, inner, groups = s.width, s.units, plan.inner, plan.groups
     pieces, named = [], {}
 
-    def add(name, ref, full, held, cut, whole, place):
+    def add(name, size, ref, full, held, cut, whole, place):
         named.setdefault(name, []).append(len(pieces))
         pieces.append(Piece(
-            lambda part: cut(ref, (), part), lambda z, part: cut(full, (z,), part),
-            lambda part: cut(full, (slice(None),), part), whole, ref, full, held, place))
+            lambda part: cut(ref, (), part * size, size),
+            lambda z, part: cut(full, (z,), part * size, size),
+            lambda part: cut(full, (slice(None),), part * size, size),
+            lambda n: cut(full, (pl.ds(0, min(n, 2)),), 0, n * size // min(n, 2)), whole, ref, full, held, place))
 
     def matrix(name, b, ref, full):
-        add(name, ref, full, r.w_in,
-            lambda a, at, part: a.at[at + (b, pl.ds(part * (w // 4), w // 4), slice(None))],
+        add(name, w // 4, ref, full, r.w_in,
+            lambda a, at, start, size: a.at[at + (b, pl.ds(start, size), slice(None))],
             lambda a: [a.at[b, pl.ds(0, w), :]],
             lambda z: [pl.ds(pl.multiple_of((z * 3 + b) * w, TILE), w)])
 
-    def rows(name, j, size, ref, full, held):
-        add(name, ref, full, held,
-            lambda a, at, part: a.at[
-                at + (pl.ds(j * TILE + part * (TILE // 4), TILE // 4), pl.ds(0, w))],
+    def rows(name, j, count, ref, full, held):
+        add(name, TILE // 4, ref, full, held,
+            lambda a, at, start, size: a.at[at + (pl.ds(j * TILE + start, size), pl.ds(0, w))],
             lambda a: [a.at[pl.ds(j * TILE, TILE), pl.ds(b * TILE, TILE)] for b in range(s.parts)],
-            lambda z: [pl.ds(pl.multiple_of((b * groups + z) * size + j * TILE, TILE), TILE)
+            lambda z: [pl.ds(pl.multiple_of((b * groups + z) * count + j * TILE, TILE), TILE)
                        for b in range(s.parts)])
 
     def columns(name, j, ref, full, held):
-        add(name, ref, full, held,
-            lambda a, at, part: a.at[at + (pl.ds(part * (w // 4), w // 4), pl.ds(j * TILE, TILE))],
+        add(name, w // 4, ref, full, held,
+            lambda a, at, start, size: a.at[at + (pl.ds(start, size), pl.ds(j * TILE, TILE))],
             lambda a: [a.at[pl.ds(0, w), pl.ds(j * TILE, TILE)]],
             lambda z: [pl.ds(pl.multiple_of((z * (u // TILE) + j) * w, TILE), w)])
 
@@ -423,7 +427,7 @@
         dst = piece.gathered(origin, self.quarter)
         src = piece.own(self.quarter) if hop == 0 else dst
         return pltpu.make_async_remote_copy(
-            src, dst, self.r.send_gz.at[p, way, hop], self.r.recv_gz.at[p, way, hop],
+            src, dst, self.r.send_gz.at[p], self.r.recv_gz.at[p, origin],
             device_id={"mp": self.z + step}, device_id_type=MESH)
 
     def block(self, p, way, hop, whose):
@@ -431,22 +435,33 @@
 
     def z_arrival(self, p, way, hop):
         block = self.block(p, way, hop, self.quarter)
+        origin = self.z - (hop + 1) * (1 - 2 * way)
         return pltpu.make_async_remote_copy(
-            block, block, self.r.send_gz.at[p, way, hop], self.r.recv_gz.at[p, way, hop],
+            block, block, self.r.send_gz.at[p], self.r.recv_gz.at[p, origin],
             device_id={"mp": self.z - (1 - 2 * way)}, device_id_type=MESH)
 
-    def y_copy(self, p, way, hop, mine=True):
-        block = self.block(p, way, hop, self.quarter if mine else self.quarter ^ 2)
+    def y_copy(self, p, way, hop):
+        block = self.block(p, way, hop, self.quarter)
         return pltpu.make_async_remote_copy(
-            block, block, self.r.send_gy.at[p, way, hop], self.r.recv_gy.at[p, way, hop],
+            block, block, self.r.send_gy.at[p], self.r.recv_gy.at[p],
             device_id=self.to_y, device_id_type=MESH)
 
-    def c_copy(self, p, which, mine=True):
-        whose = (self.quarter if mine else self.quarter ^ 1) ^ (2 * which)
-        block = self.pieces[p].every(whose)
+    def c_copy(self, p, which):
+        block = self.pieces[p].every(self.quarter ^ (2 * which))
         return pltpu.make_async_remote_copy(
-            block, block, self.r.send_gc.at[p, which], self.r.recv_gc.at[p, which],
+            block, block, self.r.send_gc.at[p], self.r.recv_gc.at[p],
             device_id=self.to_c, device_id_type=MESH)
+
+    def total(self, p, n, send, recv, target):
+        block = self.pieces[p].sized(n)
+        return pltpu.make_async_remote_copy(
+            block, block, send.at[p], recv.at[p], device_id=target, device_id_type=MESH)
+
+    def y_all(self, p):
+        return self.total(p, self.groups - 1, self.r.send_gy, self.r.recv_gy, self.to_y)
+
+    def c_all(self, p):
+        return self.total(p, 2 * self.groups, self.r.send_gc, self.r.recv_gc, self.to_c)
 
     def sends(self, way, hop):
         last = self.groups - 1
@@ -481,10 +496,8 @@
             self.c_copy(i - last, 0).start()
         if i + ahead < count:
             pl.when(jnp.logical_not(self.at_end))(partial(self.own, i + ahead))
-        for hop in range(self.groups - 1):
-            if 0 <= i - hop - 1 < count:
-                self.shared(i - hop - 1, hop)
         if 0 <= i - last - 1 < count:
+            self.y_all(i - last - 1).wait_recv()
             self.c_copy(i - last - 1, 1).start()
 
     def waves(self):
@@ -499,17 +512,10 @@
 
         self.each(self.arrives, action, hops or None)
 
-    def shared(self, p, *hops):
-        def action(way, hop):
-            self.y_copy(p, way, hop, mine=False).wait_recv()
-
-        self.each(self.arrives, action, hops or None)
-
     def settled(self, weights, *names):
         for name in names:
             for p in self.named[name]:
-                for which in range(2):
-                    self.c_copy(p, which, mine=False).wait_recv()
+                self.c_all(p).wait_recv()
 
                 def action(way, hop):
                     for item in weights.copies(p, self.z - (hop + 1) * (1 - 2 * way), False):
@@ -518,11 +524,11 @@
                 self.each(self.arrives, action)
 
     def drained(self, p):
-        self.each(self.sends, lambda way, hop: self.z_copy(p, way, hop).wait_send())
-
-        self.each(self.arrives, lambda way, hop: self.y_copy(p, way, hop).wait_send())
-        for which in range(2):
-            self.c_copy(p, which).wait_send()
+        for test, n in ((self.at_end, 1), (jnp.logical_not(self.at_end), self.groups + 1)):
+            pl.when(test)(lambda: self.total(
+                p, n, self.r.send_gz, self.r.recv_gy, self.to_y).wait_send())
+        self.y_all(p).wait_send()
+        self.c_all(p).wait_send()
 
 
 class Weights:
@@ -534,8 +540,8 @@
     def copies(self, p, z, own):
         piece = self.pieces[p]
         blocks = piece.whole(piece.ref if own else piece.full.at[z])
-        for b, (src, rows) in enumerate(zip(blocks, piece.place(z))):
-            yield pltpu.make_async_copy(src, piece.held.at[rows], self.r.weight_sem.at[p, z, b])
+        for src, rows in zip(blocks, piece.place(z)):
+            yield pltpu.make_async_copy(src, piece.held.at[rows], self.r.weight_sem.at[p])
 
     def load_own(self, *names):
         for name in names:
@@ -556,10 +562,11 @@
     def wait(self, *names):
         for name in names:
             for p in self.named[name]:
-                @pl.loop(0, self.groups)
-                def _(z):
-                    for item in self.copies(p, z, False):
-                        item.wait()
+                piece = self.pieces[p]
+                blocks = piece.whole(piece.ref)
+                rows = self.groups * len(blocks) * blocks[0].shape[0]
+                held = piece.held.at[pl.ds(0, rows)]
+                pltpu.make_async_copy(held, held, self.r.weight_sem.at[p]).wait()
 
 
 class Outputs:
@@ -581,7 +588,7 @@
         dst = self.cut(full.at[origin], k)
         src = self.cut(rows, k) if hop == 0 and not arrival else dst
         return pltpu.make_async_remote_copy(
-            src, dst, self.r.send_a.at[which, k, way, hop], self.r.recv_a.at[which, k, way, hop],
+            src, dst, self.r.send_a.at[which, way], self.r.recv_a.at[which, k, origin],
             device_id={"mp": self.z + step}, device_id_type=MESH)
 
     def sends(self, way, hop):
@@ -600,7 +607,7 @@
 
     def step(self, which, k, begun=False):
         for hop in range(1 if begun else 0, self.groups):
-            now = k - hop
+            now = k - PACE * hop
 
             @pl.when(jnp.logical_and(now >= 0, now < self.cuts))
             def _():
@@ -625,16 +632,18 @@
                 self.r.local_sem.at[which, z]) for z in range(self.groups)]
         return items
 
-    def drained(self):
-        for which in range(2):
-            @pl.loop(0, self.cuts)
-            def _(k):
-                for way in range(2):
-                    for hop in range(self.last):
-                        pl.when(self.sends(way, hop))(
-                            lambda: self.copy(which, k, way, hop).wait_send())
-            for item in self.local(which):
-                item.wait()
+    def drained(self, which):
+        full = self.pairs[which][1]
+        for way in range(2):
+            count = self.z + 1 if way == 0 else self.groups - self.z
+            for n in range(1, self.groups):
+                block = full.at[pl.ds(0, n), :, pl.ds(0, self.s.width)]
+                pl.when(jnp.logical_and(self.sends(way, 0), count == n))(
+                    lambda: pltpu.make_async_remote_copy(
+                        block, block, self.r.send_a.at[which, way], self.r.recv_a.at[which, 0, 0],
+                        device_id={"mp": self.z + 1 - 2 * way}, device_id_type=MESH).wait_send())
+        for item in self.local(which):
+            item.wait()
 
 
 class Reduce:
@@ -686,21 +695,26 @@
         return pltpu.make_async_remote_copy(
             self.r.grads.at[:, self.rows(i), pl.ds(self.first_lane(1 - self.core, k), other)],
             self.r.from_core.at[n, k, :, :, pl.ds(0, other)],
-            self.r.send_c.at[n, k], self.r.recv_c.at[n, k],
+            self.r.send_c.at[n], self.r.recv_c.at[n],
             device_id=self.to_c, device_id_type=MESH)
 
-    def core_arrival(self, i, k, size):
+    def core_both(self, i, size):
         n = self.slot(i)
-        block = self.r.from_core.at[n, k, :, :, pl.ds(0, size)]
+        block = self.r.from_core.at[n, :, :, :, pl.ds(0, size)]
         return pltpu.make_async_remote_copy(
-            block, block, self.r.send_c.at[n, k], self.r.recv_c.at[n, k],
+            block, block, self.r.send_c.at[n], self.r.recv_c.at[n],
             device_id=self.to_c, device_id_type=MESH)
 
     def own_load(self, i, k, size):
         n = lax.rem(i, 4)
         return pltpu.make_async_copy(
             self.r.grads.at[:, self.rows(i), pl.ds(self.first_lane(self.core, k), size)],
-            self.r.own.at[n, k, :, :, pl.ds(0, size)], self.r.own_sem.at[n, k])
+            self.r.own.at[n, k, :, :, pl.ds(0, size)], self.r.own_sem.at[n])
+
+    def own_both(self, i, size):
+        n = lax.rem(i, 4)
+        block = self.r.own.at[n, :, :, :, pl.ds(0, size)]
+        return pltpu.make_async_copy(block, block, self.r.own_sem.at[n])
 
     def y_copy(self, i, size):
         n = self.slot(i)
@@ -711,10 +725,11 @@
 
     def z_copy(self, i, way, t, size, fresh):
         n = self.slot(i)
-        dst = self.r.from_z.at[n, way, t, :, pl.ds(0, size)]
+        place = t + 1 - way
+        dst = self.r.from_z.at[n, place, :, pl.ds(0, size)]
         src = self.r.from_core.at[n, self.y, t, :, pl.ds(0, size)] if fresh else dst
         return pltpu.make_async_remote_copy(
-            src, dst, self.r.send_z.at[n, way, t], self.r.recv_z.at[n, way, t],
+            src, dst, self.r.send_z.at[n], self.r.recv_z.at[n, place],
             device_id={"mp": self.z + 1 - 2 * way}, device_id_type=MESH)
 
     def far_copy(self, i):
@@ -747,9 +762,9 @@
         n = self.slot(i)
 
         def action(size, other, far):
+            self.core_both(i, size).wait_recv()
+            self.own_both(i, size).wait()
             for k in range(2):
-                self.core_arrival(i, k, size).wait_recv()
-                self.own_load(i, k, size).wait()
                 self.r.from_core[n, k, :, :, :size] += self.r.own[lax.rem(i, 4), k, :, :, :size]
             self.credit(i, self.r.free.at[1])
             self.y_copy(i, size).start()
@@ -771,7 +786,7 @@
                     @pl.when(jnp.logical_not(first))
                     def _():
                         self.z_copy(i, way, t, size, False).wait_recv()
-                        self.r.from_z[n, way, t, :, :size] += (
+                        self.r.from_z[n, t + 1 - way, :, :size] += (
                             self.r.from_core[n, self.y, t, :, :size])
                         self.z_copy(i, way, t, size, False).start()
 
@@ -802,15 +817,15 @@
 
                 @pl.when(self.z == edge)
                 def _():
-                    self.r.from_z[n, way, self.z, :, :size] = jnp.zeros((self.chunk, size), low)
+                    self.r.from_z[n, self.z + 1 - way, :, :size] = jnp.zeros((self.chunk, size), low)
 
             total = (self.r.from_core[n, self.y, self.z, :, :size].astype(wide)
-                     + self.r.from_z[n, 0, self.z, :, :size].astype(wide)
-                     + self.r.from_z[n, 1, self.z, :, :size].astype(wide))
+                     + self.r.from_z[n, self.z + 1, :, :size].astype(wide)
+                     + self.r.from_z[n, self.z, :, :size].astype(wide))
 
             def keep():
                 pl.when(i >= 2)(lambda: self.out_store(i - 2, 0, size).wait())
-                self.r.staged_out[lax.rem(i, 2), :, :size] = total
+                self.r.staged_out[lax.rem(i, 2), :, :size] = total.astype(low)
                 self.out_store(i, 0, size).start()
 
             if far:
@@ -824,14 +839,12 @@
                     self.far_copy(i).start()
             else:
                 keep()
-            for k in range(2):
-                self.core_copy(i, k, other).wait_send()
+            self.core_both(i, other).wait_send()
             self.y_copy(i, size).wait_send()
-            for way in range(2):
-                for hop in range(1, self.groups):
-                    t = self.z + (1 - 2 * way) * (self.groups - hop)
-                    pl.when(t <= self.last if way == 0 else t >= 0)(
-                        lambda: self.z_copy(i, way, t, size, True).wait_send())
+            block = self.r.from_z.at[n, pl.ds(0, self.last), :, pl.ds(0, size)]
+            pltpu.make_async_remote_copy(
+                block, block, self.r.send_z.at[n], self.r.recv_z.at[n, 0],
+                device_id=self.to_y, device_id_type=MESH).wait_send()
 
         self.widths(action)
 
@@ -857,7 +870,7 @@
             def _():
                 self.far_copy(i).wait_recv()
                 pl.when(i >= 2)(lambda: self.out_store(i - 2, size, size).wait())
-                self.r.staged_out[lax.rem(i, 2), :, size : 2 * size] = self.r.far[1, n].astype(wide)
+                self.r.staged_out[lax.rem(i, 2), :, size : 2 * size] = self.r.far[1, n]
                 self.out_store(i, size, size).start()
 
                 @pl.when(i < self.count - self.slots)
@@ -945,8 +958,15 @@
             src, dst = self.r.small_sum, self.piece(self.r.small_out, me)
         n = 0 if first else 1
         return pltpu.make_async_remote_copy(
-            src, dst, self.r.send_s.at[n, offset], self.r.recv_s.at[n, offset],
+            src, dst, self.r.send_s.at[n], self.r.recv_s.at[n],
             device_id=target, device_id_type=MESH)
+
+    def all(self, first):
+        n = 0 if first else 1
+        block = self.r.small_got.at[pl.ds(0, self.count - 1)]
+        return pltpu.make_async_remote_copy(
+            block, block, self.r.send_s.at[n], self.r.recv_s.at[n],
+            device_id=peer_of(self.plan, 1)[2], device_id_type=MESH)
 
     def every(self, action):
         @pl.loop(1, self.count)
@@ -964,7 +984,7 @@
 
     def middle(self):
         self.local(True).start()
-        self.every(lambda offset: self.copy(offset, True).wait_recv())
+        self.all(True).wait_recv()
         self.local(True).wait()
         self.r.small_sum[...] = jnp.sum(self.r.small_got[...], axis=0)
         self.local(False).start()
@@ -972,9 +992,9 @@
 
     def finish(self):
         self.local(False).wait()
-        self.every(lambda offset: self.copy(offset, False).wait_recv())
+        self.all(False).wait_recv()
         for first in (True, False):
-            self.every(lambda offset: self.copy(offset, first).wait_send())
+            self.all(first).wait_send()
 
 
 def run_stream(which, s, layout, plan, r):
@@ -1002,7 +1022,7 @@
         ref, full = ((r.cross_bias, r.a_cross_bias), (r.attend_bias, r.a_attend_bias),
                      (r.up_bias, r.a_up_bias))[kind]
         return pltpu.make_async_remote_copy(
-            ref, full.at[z], r.send_b.at[kind, step], r.recv_b.at[kind, step],
+            ref, full.at[z], r.send_b.at[kind], r.recv_b.at[kind],
             device_id={"mp": lax.rem(z + step, groups)}, device_id_type=MESH)
 
     for kind, (ref, full) in enumerate(((r.cross_bias, r.a_cross_bias),
@@ -1013,8 +1033,8 @@
         full[z] = ref[...]
 
     r.zero[...] = jnp.zeros_like(r.zero)
-    r.acc[:, :TILE] = jnp.zeros((tokens, TILE), wide)
-    for test, item in reduce.zeros(s, r.acc):
+    r.low_grad[:, :TILE] = jnp.zeros((tokens, TILE), low)
+    for test, item in reduce.zeros(s, r.low_grad):
         pl.when(test)(item.start)
 
     def swap(source, target, number):
@@ -1101,9 +1121,11 @@
 
     def do_value():
         gather.settled(weights, "v")
-        for kind in range(3):
-            for step in range(1, groups):
-                bias_copy(step, kind).wait()
+        for kind, full in enumerate((r.a_cross_bias, r.a_attend_bias, r.a_up_bias)):
+            block = full.at[pl.ds(0, groups - 1)]
+            pltpu.make_async_remote_copy(
+                block, block, r.send_b.at[kind], r.recv_b.at[kind],
+                device_id={"mp": lax.rem(z + 1, groups)}, device_id_type=MESH).wait()
         weights.wait("v")
         project(2, r.x, r.v, r.a_cross_bias, 1)
         swap(r.v, r.pair_v, 1).start()
@@ -1125,7 +1147,7 @@
         gather.settled(weights, "up")
 
     def do_first_norm():
-        for test, item in reduce.zeros(s, r.acc):
+        for test, item in reduce.zeros(s, r.low_grad):
             pl.when(test)(item.wait)
         weights.wait("cross_out")
         leave(r.context, groups * inner, r.w_cross_out, lambda cols: r.x[:, cols].astype(wide), 0)
@@ -1166,8 +1188,6 @@
     outputs.begin(0)
     for item in outputs.local(0):
         item.start()
-    for p in range(len(gather.pieces)):
-        gather.drained(p)
 
     def store(row, g):
         return pltpu.make_async_copy(
@@ -1270,6 +1290,10 @@
         r.hidden_rows[:, :w] = r.acc[:, :w].astype(low)
         for item in outputs.local(1):
             item.start()
+
+    def drain_gather(_):
+        for p in range(len(gather.pieces)):
+            gather.drained(p)
 
     def attend_grads(k):
         weight_grads(lambda cols: r.d[k, :, cols], r.h2, layout.attend_in + k * inner, inner)(0)
@@ -1310,13 +1334,16 @@
             lambda g: [(d, g * inner) for d in (r.d.at[0], r.back.at[0], r.back.at[1])], r.w_in, 3)),
         (take + 4, 1, 1, False, hidden_store),
         (take + 5, 1, 1, False, lambda _: small.middle()),
+        (17, 1, 1, False, drain_gather),
+        (take + 6, 1, 1, False, lambda _: outputs.drained(0)),
+        (take + 12, 1, 1, False, lambda _: small.finish()),
     )
     storing = sorted({start + n for start, steps, per, keeps, _ in schedule if keeps
                       for n in range(steps)})
     assert len(storing) == sum(steps for _, steps, _, keeps, _ in schedule if keeps)
     hidden_at = take + 5
 
-    @pl.loop(0, max(reduce.iterations(), hidden_at + plan.cuts + groups))
+    @pl.loop(0, max(reduce.iterations(), hidden_at + plan.cuts + PACE * groups))
     def _(j):
         flushes = j == 0
         for n in storing:
@@ -1334,8 +1361,80 @@
         outputs.step(1, j - hidden_at)
 
     reduce.drained()
-    outputs.drained()
-    small.finish()
+    outputs.drained(1)
+
+
+def place_kernel(layout, groups, copies, layer_in, hidden_in, reduced, small, layer_out, hidden_out,
+                 cross_in, attend_in, cross_out, attend_out, up, down,
+                 cross_bias, attend_bias, up_bias, out_bias, gains, shifts,
+                 held, rows, tall, flat_out, turned, load_sem, store_sem):
+    inner = cross_out.shape[0]
+    units = down.shape[0]
+    copy = lax.axis_index("dp")
+    me = lax.axis_index("mp") * copies + copy
+    blocks = layout.total // inner
+    loads = [pltpu.make_async_copy(
+        reduced.at[pl.ds(n * inner, inner)], rows.at[n], load_sem.at[n]) for n in range(blocks)]
+    stores = []
+
+    def store(src, dst):
+        stores.append(pltpu.make_async_copy(src, dst, store_sem.at[len(stores)]))
+        stores[-1].start()
+
+    large = [(pair, z) for pair in ((layer_in, layer_out, 0), (hidden_in, hidden_out, 1))
+             for z in range(groups)]
+    carries = [pltpu.make_async_copy(source.at[z], held.at[n, z], load_sem.at[blocks + k])
+               for k, ((source, _, n), z) in enumerate(large)]
+    for item in loads + carries:
+        item.start()
+
+    def turn(n, slot):
+        loads[n].wait()
+        turned[slot] = rows[n].astype(wide).T
+
+    def keep(n, slot):
+        loads[n].wait()
+        flat_out[slot] = rows[n].astype(wide)
+
+    first = {name: getattr(layout, name) // inner for name in (
+        "attend_out", "attend_in", "down", "up", "cross_out", "cross_in")}
+    keep(first["attend_out"], 0)
+    store(flat_out.at[0], attend_out)
+    for k in range(3):
+        turn(first["attend_in"] + k, k)
+        store(turned.at[k], attend_in.at[k])
+    for j in range(units // inner):
+        keep(first["down"] + j, 2 + j)
+        store(flat_out.at[2 + j], down.at[pl.ds(j * inner, inner)])
+    for j in range(units // inner):
+        loads[first["up"] + j].wait()
+        tall[:, j * inner : (j + 1) * inner] = rows[first["up"] + j].astype(wide).T
+    store(tall, up)
+    for item, ((_, target, n), z) in zip(carries, large):
+        item.wait()
+        store(held.at[n, z], target.at[z])
+    keep(first["cross_out"], 1)
+    store(flat_out.at[1], cross_out)
+    for k in range(3):
+        turn(first["cross_in"] + k, 3 + k)
+        store(turned.at[3 + k], cross_in.at[k])
+
+    def share(value, start, size):
+        width = value.shape[1]
+        return pltpu.roll(value, lax.rem(width - start, width), 1)[:, :size]
+
+    columns = down.shape[1]
+    values = share(small[...], copy * columns, columns)
+    for ref, row in ((out_bias, 0), (gains, 3), (shifts, 6)):
+        for k in range(3):
+            ref[k] = values[row + k : row + k + 1]
+    sides = share(small[...], me * (inner // copies), inner // copies)
+    attend_bias[...] = sides[12:14]
+    cross_bias[...] = sides[14:16]
+    flat = jnp.concatenate([small[9:10], small[10:11], small[11:12]], axis=1)
+    up_bias[...] = share(flat, me * (units // copies), units // copies)
+    for item in stores:
+        item.wait()
 
 
 def shards(
@@ -1440,10 +1539,10 @@
         staged=short(ring, TILE, padded),
         from_core=short(slots, 2, groups, chunk, TILE),
         from_y=short(slots, groups, chunk, TILE),
-        from_z=short(slots, 2, groups, chunk, TILE),
+        from_z=short(slots, groups + 1, chunk, TILE),
         far=short(2, slots, chunk, 128),
         own=short(4, 2, groups, chunk, TILE),
-        staged_out=real(2, chunk, TILE),
+        staged_out=short(2, chunk, TILE),
         small_in=real(16, padded),
         small_got=real(peers, 1, small_width),
         small_sum=real(1, small_width),
@@ -1451,34 +1550,34 @@
         a_cross_bias=short(groups, 2, inner),
         a_attend_bias=short(groups, 2, inner),
         a_up_bias=short(groups, 1, units),
-        send_gz=dma((pieces, 2, hops)),
-        recv_gz=dma((pieces, 2, hops)),
-        send_gy=dma((pieces, 2, hops)),
-        recv_gy=dma((pieces, 2, hops)),
-        send_gc=dma((pieces, 2)),
-        recv_gc=dma((pieces, 2)),
-        weight_sem=dma((pieces, groups, 4)),
+        send_gz=dma((pieces,)),
+        recv_gz=dma((pieces, groups)),
+        send_gy=dma((pieces,)),
+        recv_gy=dma((pieces,)),
+        send_gc=dma((pieces,)),
+        recv_gc=dma((pieces,)),
+        weight_sem=dma((pieces,)),
         enter_sem=dma((2,)),
-        send_b=dma((3, groups)),
-        recv_b=dma((3, groups)),
+        send_b=dma((3,)),
+        recv_b=dma((3,)),
         send_x=dma((4,)),
         recv_x=dma((4,)),
         store_sem=dma((ring,)),
-        send_c=dma((slots, 2)),
-        recv_c=dma((slots, 2)),
+        send_c=dma((slots,)),
+        recv_c=dma((slots,)),
         send_y=dma((slots,)),
         recv_y=dma((slots,)),
-        send_z=dma((slots, 2, groups)),
-        recv_z=dma((slots, 2, groups)),
+        send_z=dma((slots,)),
+        recv_z=dma((slots, groups + 1)),
         send_f=dma((slots,)),
         recv_f=dma((slots,)),
-        own_sem=dma((4, 2)),
+        own_sem=dma((4,)),
         out_sem=dma((2, 2)),
-        send_a=dma((2, cuts, 2, hops)),
-        recv_a=dma((2, cuts, 2, hops)),
+        send_a=dma((2, 2)),
+        recv_a=dma((2, cuts, groups)),
         local_sem=dma((2, groups + 1)),
-        send_s=dma((2, peers)),
-        recv_s=dma((2, peers)),
+        send_s=dma((2,)),
+        recv_s=dma((2,)),
         free=pltpu.SemaphoreType.REGULAR((5,)),
         zero_sem=dma((4 + rows_max // TILE,)),
     )
@@ -1501,7 +1600,7 @@
     out = pl.pallas_call(
         partial(layer_kernel, settings, layout, plan),
         out_shape=(
-            line, line, shape((rows_max, TILE), wide), shape((16, padded), wide),
+            line, line, shape((rows_max, TILE)), shape((16, padded), wide),
         ) + tuple(shape((groups,) + w.shape) for w in weights)
         + (shape((groups, rows_max, padded)),),
         in_specs=[ANY] * 8 + [VMEM] * 8,
@@ -1518,40 +1617,45 @@
     if stride > 1:
         teams = [[q * stride + b for b in range(stride)] for q in range(4)]
         reduced = lax.psum_scatter(
-            reduced.astype(low), "dp", scatter_dimension=1, axis_index_groups=teams, tiled=True
-        ).astype(wide)
-    columns = padded // copies
-    part = inner // copies
-    vector_grads = lax.dynamic_slice_in_dim(small[:9], copy * columns, columns, 1)
-    up_bias_grad = lax.dynamic_slice_in_dim(
-        small[9:12].reshape(groups * units), (member * copies + copy) * (units // copies),
-        units // copies, 0)
-    pair_grads = lax.dynamic_slice_in_dim(
-        small[12:16], (member * copies + copy) * part, part, 1)
-
-    def turned(start):
-        return reduced[start : start + 3 * inner].reshape(3, inner, columns).transpose(2, 0, 1)
-
-    g_cross_in, g_attend_in = turned(layout.cross_in), turned(layout.attend_in)
-    g_cross_out = reduced[layout.cross_out : layout.cross_out + inner]
-    g_attend_out = reduced[layout.attend_out : layout.attend_out + inner]
-    g_up = reduced[layout.up : layout.up + units].T
-    g_down = reduced[layout.down : layout.down + units]
+            reduced, "dp", scatter_dimension=1, axis_index_groups=teams, tiled=True)
+
+    columns, part = padded // copies, inner // copies
+    shapes = (
+        line, line, shape((3, columns, inner), wide), shape((3, columns, inner), wide),
+        shape((inner, columns), wide), shape((inner, columns), wide),
+        shape((columns, units), wide), shape((units, columns), wide),
+        shape((2, part), wide), shape((2, part), wide), shape((1, units // copies), wide),
+    ) + (shape((3, 1, columns), wide),) * 3
+    (layer_out, hidden_grad, g_cross_in, g_attend_in, g_cross_out, g_attend_out, g_up, g_down,
+     g_cross_bias, g_attend_bias, g_up_bias, g_out_bias, g_gains, g_shifts) = pl.pallas_call(
+        partial(place_kernel, layout, groups, copies),
+        out_shape=shapes,
+        in_specs=[HBM] * 3 + [VMEM],
+        out_specs=(HBM,) * 8 + (VMEM,) * 6,
+        scratch_shapes=[
+            short(2, groups, tokens, padded), short(rows_max // inner, inner, columns),
+            real(columns, units), real(2 + units // inner, inner, columns),
+            real(6, columns, inner), dma((rows_max // inner + 2 * groups,)),
+            dma((9 + units // inner + 2 * groups,)),
+        ],
+        compiler_params=pltpu.CompilerParams(vmem_limit_bytes=VMEM_LIMIT),
+        name="place",
+    )(layer_out, hidden_grad, reduced, small)
     return (
         layer_out.reshape(1, groups * tokens, padded),
         hidden_grad.reshape(1, groups * tokens, padded),
-        g_cross_in[None],
-        pair_grads[None, 2:4],
+        g_cross_in.transpose(1, 0, 2)[None],
+        g_cross_bias[None],
         g_cross_out[None],
         g_up[None],
-        up_bias_grad[None],
+        g_up_bias,
         g_down[None],
-        g_attend_in[None],
-        pair_grads[None, 0:2],
+        g_attend_in.transpose(1, 0, 2)[None],
+        g_attend_bias[None],
         g_attend_out[None],
-        vector_grads[None, 0:3],
-        vector_grads[None, 3:6],
-        vector_grads[None, 6:9],
+        g_out_bias.transpose(1, 0, 2),
+        g_gains.transpose(1, 0, 2),
+        g_shifts.transpose(1, 0, 2),
     )
 
 

time: 304 us -> 281 us (0.924)
  local copies, waits for them, and re-layouts: 15.9 us -> 0.72 us
  Pallas kernels: 286 us -> 278 us
    pallas_call x1, Pallas kernels: 286 us -> 270 us  [shards(): pl.pallas_call(partial(layer_kernel, settings, layout, plan), out_shape=(...]
    pallas_call x0 -> x1, Pallas kernels: none -> 7.52 us  [shards(): pl.pallas_call(partial(place_kernel, layout, groups, copies), out_shape=s...]
    unnamed x12 -> x0, local copies, waits for them, and re-layouts: 6.56 us -> none
    slice x3 -> x0, local copies, waits for them, and re-layouts: 3.06 us -> none  [the longest x1 3.05 us: turned(): reduced[start:start + 3 * inner].reshape(3, inner, columns)]
where the time goes in v4:
time: 281 us; the launch traced here: 280 us
  Pallas kernels  278 us (99%)
    pallas_call x1, Pallas kernels, shards(): pl.pallas_call(partial(layer_kernel, settings, layout, plan), out_shape=(...  270 us
    pallas_call x1, Pallas kernels, shards(): pl.pallas_call(partial(place_kernel, layout, groups, copies), out_shape=s...  7.52 us

profile of v4, /device:TPU:0, one launch (start us, length us, event | category | flops | bytes accessed | tf_op | source)
XLA Modules:
  0.0 280.3 jit_solution(5182852311325903440)
XLA Ops:
  0.7 0.7 fusion.2
  1.4 0.8 fusion.1
  2.2 270.4 %layer.1 = (bf16[4,256,1024]{2,1,0:T(8,128)(2,1)}, bf16[4,256,1024]{2,1,0:T(8,128)(2,1)}, bf16[3584,256]{1,0:T(8,128)(2,1)}, f32[16,1024]{1,0:T(8,128)}, bf16[4,...) custom-call(bf16[3,1024,256]{2,1,0:T(8,128)(2,1)} %bitcast.49, ...), custom_call_target="tpu_custom_call" | custom-call | tf_op jit(solution)/shard_map/layer/pallas_call | solution.py:1600
  272.6 7.5 %place.1 = (bf16[4,256,1024]{2,1,0:T(8,128)(2,1)}, bf16[4,256,1024]{2,1,0:T(8,128)(2,1)}, f32[3,256,256]{2,1,0:T(8,128)}, f32[3,256,256]{2,1,0:T(8,128)}, f32[25...) custom-call(bf16[4,256,1024]{2,1,0:T(8,128)(2,1)} %get-tuple-element, ...), custom_call_target="tpu_custom_call" | custom-call | tf_op jit(solution)/shard_map/place/pallas_call | solution.py:1630

commit v5 on v4

--- a/solution.py
+++ b/solution.py
@@ -1185,9 +1185,6 @@
     weights.wait("attend_out")
     leave(r.context2, groups * inner, r.w_attend_out, lambda cols: scaled(r.n2, 1, cols), 2)
     norm(r.n3, r.r3, 2, r.layer_rows)
-    outputs.begin(0)
-    for item in outputs.local(0):
-        item.start()
 
     def store(row, g):
         return pltpu.make_async_copy(
@@ -1291,6 +1288,11 @@
         for item in outputs.local(1):
             item.start()
 
+    def layer_send(_):
+        outputs.begin(0)
+        for item in outputs.local(0):
+            item.start()
+
     def drain_gather(_):
         for p in range(len(gather.pieces)):
             gather.drained(p)
@@ -1307,12 +1309,13 @@
 
     r.small_in[...] = jnp.zeros_like(r.small_in)
     back_norm(r.grad_out, r.n3, r.r3, 2)
-    pl.loop(0, groups)(context_back(r.w_attend_out))
     weight_grads(of(r.context2), r.low_grad, layout.attend_out, inner)(0)
     nb = u // TILE
     take = plan.when[which]
     schedule = (
+        (0, 4, 4, False, context_back(r.w_attend_out)),
         (0, 4, 2, False, self_step),
+        (1, 1, 1, False, layer_send),
         (2, 3, 1, True, attend_grads),
         (2, 4, 2, False, enter_back(lambda g: [(d, g * inner) for d in (r.d.at[0], r.d.at[1], r.d.at[2])],
                                     r.w_in, 3)),
@@ -1349,6 +1352,7 @@
         for n in storing:
             flushes = jnp.logical_or(flushes, j == n + 1)
         pl.when(flushes)(flush)
+        reduce.iteration(j)
         for start, steps, per, _, step in schedule:
             @pl.when(jnp.logical_and(j >= start, j < start + steps // per))
             def _():
@@ -1356,8 +1360,7 @@
                     step(j - start)
                 else:
                     pl.loop(0, per)(lambda n: step((j - start) * per + n))
-        reduce.iteration(j)
-        outputs.step(0, j, True)
+        outputs.step(0, j - 1, True)
         outputs.step(1, j - hidden_at)
 
     reduce.drained()
@@ -1584,8 +1587,8 @@
     plan = Plan(
         groups=groups, copies=copies, inner=inner, length=length, rows=rows_dev,
         tokens=tokens, units=units, chunk=chunk, slots=slots, cuts=cuts,
-        ring=ring, lags=(3, 8, 2, 2),
-        when=(26, 24),
+        ring=ring, lags=(1, 8, 2, 2),
+        when=(25, 25),
         forward=((4, 5, 6, 10, 11, 12, 13, 14), (4, 5, 6, 8, 9, 10, 11, 12)),
     )
     weights = (

time: 281 us -> 275 us (0.979)
  Pallas kernels: 278 us -> 272 us
    pallas_call x1, Pallas kernels: 270 us -> 265 us  [shards(): pl.pallas_call(partial(layer_kernel, settings, layout, plan), out_shape=(...]
where the time goes in v5:
time: 275 us
  Pallas kernels  272 us (99%)
    pallas_call x1, Pallas kernels, shards(): pl.pallas_call(partial(layer_kernel, settings, layout, plan), out_shape=(...  265 us
    pallas_call x1, Pallas kernels, shards(): pl.pallas_call(partial(place_kernel, layout, groups, copies), out_shape=s...  7.52 us

profile of v5, /device:TPU:0, one launch (start us, length us, event | category | flops | bytes accessed | tf_op | source)
XLA Modules:
  0.0 274.8 jit_solution(14177793376438697944)
XLA Ops:
  0.7 0.7 fusion.2
  1.4 0.8 fusion.1
  2.2 264.8 %layer.1 = (bf16[4,256,1024]{2,1,0:T(8,128)(2,1)}, bf16[4,256,1024]{2,1,0:T(8,128)(2,1)}, bf16[3584,256]{1,0:T(8,128)(2,1)}, f32[16,1024]{1,0:T(8,128)}, bf16[4,...) custom-call(bf16[3,1024,256]{2,1,0:T(8,128)(2,1)} %bitcast.49, ...), custom_call_target="tpu_custom_call" | custom-call | tf_op jit(solution)/shard_map/layer/pallas_call | solution.py:1603
  267.1 7.5 %place.1 = (bf16[4,256,1024]{2,1,0:T(8,128)(2,1)}, bf16[4,256,1024]{2,1,0:T(8,128)(2,1)}, f32[3,256,256]{2,1,0:T(8,128)}, f32[3,256,256]{2,1,0:T(8,128)}, f32[25...) custom-call(bf16[4,256,1024]{2,1,0:T(8,128)(2,1)} %get-tuple-element, ...), custom_call_target="tpu_custom_call" | custom-call | tf_op jit(solution)/shard_map/place/pallas_call | solution.py:1633

commit v6 on v5

--- a/solution.py
+++ b/solution.py
@@ -402,8 +402,9 @@
         columns("up", j, r.up, r.f_up, r.w_up)
     for j in range(u // TILE):
         rows("down", j, u, r.down, r.f_down, r.w_down)
-    for b in range(3):
-        matrix("attend_in", b, r.attend_in, r.f_attend_in)
+    matrix("attend_q", 0, r.attend_in, r.f_attend_in)
+    matrix("attend_k", 1, r.attend_in, r.f_attend_in)
+    matrix("attend_v", 2, r.attend_in, r.f_attend_in)
     rows("attend_out", 0, inner, r.attend_out, r.f_attend_out, r.w_attend_out)
     return pieces, named
 
@@ -1134,7 +1135,7 @@
         gather.settled(weights, "q")
         weights.wait("q")
         project(0, r.x, r.q, r.a_cross_bias, 0)
-        weights.load_own("attend_in")
+        weights.load_own("attend_q", "attend_k", "attend_v")
 
     def do_cross_first():
         gather.settled(weights, "cross_out")
@@ -1161,21 +1162,27 @@
     def do_feed_second():
         feed_part(groups // 2, groups)
 
+    def do_second_norm():
+        weights.wait("down")
+        leave(r.active, groups * u, r.w_down, lambda cols: scaled(r.n1, 0, cols), 1)
+        norm(r.n2, r.r2, 1, r.h2)
+
     work = dict(zip(plan.forward[which], (
         do_key, do_value, do_query, do_cross_first, do_cross_second, do_first_norm,
-        do_feed_first, do_feed_second)))
+        do_feed_first, do_feed_second, do_second_norm)))
     for i in range(gather.waves() + 1):
         gather.wave(i, 2)
         if i in work:
             work[i]()
-    weights.wait("down")
-    leave(r.active, groups * u, r.w_down, lambda cols: scaled(r.n1, 0, cols), 1)
-    norm(r.n2, r.r2, 1, r.h2)
-    gather.settled(weights, "attend_in", "attend_out")
-    weights.wait("attend_in")
-    project(0, r.h2, r.q2, r.a_attend_bias, 0)
-    project(1, r.h2, r.k2, None, None)
-    project(2, r.h2, r.v2, r.a_attend_bias, 1)
+    if len(plan.forward[which]) < 9:
+        do_second_norm()
+    for name, part, target, bias_ref, line in (
+            ("attend_q", 0, r.q2, r.a_attend_bias, 0), ("attend_k", 1, r.k2, None, None),
+            ("attend_v", 2, r.v2, r.a_attend_bias, 1)):
+        gather.settled(weights, name)
+        weights.wait(name)
+        project(part, r.h2, target, bias_ref, line)
+    gather.settled(weights, "attend_out")
 
     @pl.loop(0, groups)
     def _(g):
@@ -1388,7 +1395,7 @@
              for z in range(groups)]
     carries = [pltpu.make_async_copy(source.at[z], held.at[n, z], load_sem.at[blocks + k])
                for k, ((source, _, n), z) in enumerate(large)]
-    for item in loads + carries:
+    for item in loads[:1] + carries + loads[1:]:
         item.start()
 
     def turn(n, slot):
@@ -1403,6 +1410,9 @@
         "attend_out", "attend_in", "down", "up", "cross_out", "cross_in")}
     keep(first["attend_out"], 0)
     store(flat_out.at[0], attend_out)
+    for item, ((_, target, n), z) in zip(carries, large):
+        item.wait()
+        store(held.at[n, z], target.at[z])
     for k in range(3):
         turn(first["attend_in"] + k, k)
         store(turned.at[k], attend_in.at[k])
@@ -1413,9 +1423,6 @@
         loads[first["up"] + j].wait()
         tall[:, j * inner : (j + 1) * inner] = rows[first["up"] + j].astype(wide).T
     store(tall, up)
-    for item, ((_, target, n), z) in zip(carries, large):
-        item.wait()
-        store(held.at[n, z], target.at[z])
     keep(first["cross_out"], 1)
     store(flat_out.at[1], cross_out)
     for k in range(3):
@@ -1589,7 +1596,7 @@
         tokens=tokens, units=units, chunk=chunk, slots=slots, cuts=cuts,
         ring=ring, lags=(1, 8, 2, 2),
         when=(25, 25),
-        forward=((4, 5, 6, 10, 11, 12, 13, 14), (4, 5, 6, 8, 9, 10, 11, 12)),
+        forward=((4, 5, 6, 10, 11, 12, 13, 14, 15), (4, 5, 6, 8, 9, 10, 11, 12)),
     )
     weights = (
         jnp.swapaxes(cross_in[0], 0, 1),

time: 275 us -> 275 us (level)
  no operation moved by 1% of the time
where the time goes in v6:
time: 275 us; the launch traced here: 274 us
  Pallas kernels  272 us (99%)
    pallas_call x1, Pallas kernels, shards(): pl.pallas_call(partial(layer_kernel, settings, layout, plan), out_shape=(...  265 us
    pallas_call x1, Pallas kernels, shards(): pl.pallas_call(partial(place_kernel, layout, groups, copies), out_shape=s...  7.22 us

profile of v6, /device:TPU:0, one launch (start us, length us, event | category | flops | bytes accessed | tf_op | source)
XLA Modules:
  0.0 274.4 jit_solution(15793837527026533839)
XLA Ops:
  0.7 0.7 fusion.2
  1.4 0.8 fusion.1
  2.2 264.8 %layer.1 = (bf16[4,256,1024]{2,1,0:T(8,128)(2,1)}, bf16[4,256,1024]{2,1,0:T(8,128)(2,1)}, bf16[3584,256]{1,0:T(8,128)(2,1)}, f32[16,1024]{1,0:T(8,128)}, bf16[4,...) custom-call(bf16[3,1024,256]{2,1,0:T(8,128)(2,1)} %bitcast.49, ...), custom_call_target="tpu_custom_call" | custom-call | tf_op jit(solution)/shard_map/layer/pallas_call | solution.py:1610
  267.0 7.2 %place.1 = (bf16[4,256,1024]{2,1,0:T(8,128)(2,1)}, bf16[4,256,1024]{2,1,0:T(8,128)(2,1)}, f32[3,256,256]{2,1,0:T(8,128)}, f32[3,256,256]{2,1,0:T(8,128)}, f32[25...) custom-call(bf16[4,256,1024]{2,1,0:T(8,128)(2,1)} %get-tuple-element, ...), custom_call_target="tpu_custom_call" | custom-call | tf_op jit(solution)/shard_map/place/pallas_call | solution.py:1640
